TPU v7x, 128 devices: a whole 4x4x4 slice. The times are simulated.
128 devices in a mesh: dp: 8 (over y, x_lo), mp: 16 (over x_hi, z, core).
Axes of the slice: x: 4 (x_hi: 2, x_lo: 2; x = x_hi * 2 + x_lo), y: 4, z: 4, core: 2. Of those that a mesh axis runs over, the one named last changes fastest.
Arguments:
- hidden_states: bfloat16 [4096, 4096], P('dp', 'mp'), may hold values from -6 to 6
- gate_online: bfloat16 [4096, 14336], P('dp', 'mp'), may hold values from -0.09375 to 0.09375
- up_online: bfloat16 [4096, 14336], P('dp', 'mp'), may hold values from -0.09375 to 0.09375
- down_online: bfloat16 [14336, 4096], P('mp', 'dp'), may hold values from -0.046875 to 0.046875
- gate_previous: bfloat16 [4096, 14336], P(None, 'mp'), may hold values from -0.09375 to 0.09375
- up_previous: bfloat16 [4096, 14336], P(None, 'mp'), may hold values from -0.09375 to 0.09375
- down_previous: bfloat16 [14336, 4096], P('mp'), may hold values from -0.046875 to 0.046875
Outputs:
- online_output: bfloat16 [4096, 4096], P('dp', 'mp')
- target_output: bfloat16 [4096, 4096], P('dp', 'mp')
All inputs are finite; a program needn't handle non-finite values.
Results may differ from a plain program's by a relative error of at most 0.0072.
Values may be sent and summed in bfloat16 or wider, within the bound.
A program may use at most 128 MiB of HBM per device.

v0:
```python
import jax
import jax.numpy as jnp
from jax import lax
from jax.sharding import PartitionSpec as P

POLYAK = 0.25


def blend(online, previous):
    return (
        POLYAK * online.astype(jnp.float32) + (1.0 - POLYAK) * previous.astype(jnp.float32)
    ).astype(jnp.bfloat16)


def add_pair(features_all, piece, previous):
    target_piece = blend(piece, previous)
    online_sum = jnp.dot(features_all, piece, preferred_element_type=jnp.float32)
    target_sum = jnp.dot(features_all, target_piece, preferred_element_type=jnp.float32)
    return (online_sum, target_sum)


def local(
    hidden_states, gate_online, up_online, down_online, gate_previous, up_previous, down_previous
):
    features_all = lax.all_gather(hidden_states, "mp", axis=1, tiled=True)
    gate_o, gate_t = add_pair(
        features_all, lax.all_gather(gate_online, "dp", axis=0, tiled=True), gate_previous
    )
    up_o, up_t = add_pair(
        features_all, lax.all_gather(up_online, "dp", axis=0, tiled=True), up_previous
    )
    inner_o = (jax.nn.silu(gate_o) * up_o).astype(jnp.bfloat16)
    inner_t = (jax.nn.silu(gate_t) * up_t).astype(jnp.bfloat16)
    piece = lax.all_gather(down_online, "dp", axis=1, tiled=True)
    target_piece = blend(piece, down_previous)
    online_part = jnp.dot(inner_o, piece, preferred_element_type=jnp.float32)
    target_part = jnp.dot(inner_t, target_piece, preferred_element_type=jnp.float32)
    terms = jnp.stack([online_part, target_part], axis=0)
    summed = lax.psum_scatter(terms, "mp", scatter_dimension=2, tiled=True)
    result = summed.astype(jnp.bfloat16)
    return (result[0], result[1])


def solution(mesh):
    in_specs = (
        P("dp", "mp"),
        P("dp", "mp"),
        P("dp", "mp"),
        P("mp", "dp"),
        P(None, "mp"),
        P(None, "mp"),
        P("mp", None),
    )
    out_specs = (P("dp", "mp"), P("dp", "mp"))
    return jax.shard_map(local, mesh=mesh, in_specs=in_specs, out_specs=out_specs, check_vma=False)
```

profile of v0, /device:TPU:1, one launch (start us, length us, event | category | flops | bytes accessed | tf_op | source)
XLA Modules:
  0.0 729.1 jit_solution(7389197562212726520)
XLA Ops:
  7.2 0.0 all-gather.5.cloned.1.call-start
  7.2 0.7 all-gather.5.cloned.1.call-update
  7.9 0.0 all-gather.7.cloned.1.call-start
  7.9 0.7 all-gather.7.cloned.1.call-update
  8.6 0.0 all-gather.9.cloned.1.call-start
  8.7 0.7 all-gather.9.cloned.1.call-update
  9.4 0.0 all-gather.11.cloned.1.call-start
  9.4 0.5 all-gather.11.cloned.1.call-update
  10.0 0.0 reduce-scatter.2.cloned.1.call-start
  10.0 60.8 %all-gather.5.cloned.1.call-done = bf16[512,4096]{1,0:T(8,128)(2,1)} async-done(((bf16[512,256]{1,0:T(8,128)(2,1)}), bf16[512,4096]{1,0:T(8,128)(2,1)}) %all-gather.5.cloned.1.call-update) | async-done | bytes 4194320 | tf_op jit(solution)/shard_map/all_gather | solution.py:25
  70.8 147.5 %all-gather.7.cloned.1.call-done = bf16[4096,896]{1,0:T(8,128)(2,1)} async-done(((bf16[512,896]{1,0:T(8,128)(2,1)}), bf16[4096,896]{1,0:T(8,128)(2,1)}) %all-gather.7.cloned.1.call-update) | async-done | bytes 7340048 | tf_op jit(solution)/shard_map/all_gather | solution.py:27
  218.3 0.0 copy-start
  218.3 0.0 copy-start.1
  218.3 10.2 %fusion.22 = f32[512,896]{1,0:T(8,128)} fusion(bf16[512,4096]{1,0:T(8,128)(2,1)} %all-gather.5.cloned.1.call-done, bf16[4096,896]{1,0:T(8,128)(2,1)} %all-gather.7.cloned.1.call-done), kind=kOutput, calls=%fused_computation.31 | convolution fusion | flops 3758096384 | bytes 13369344 | tf_op jit(solution)/shard_map/dot_general | solution.py:17
  228.5 0.0 copy-done
  228.5 0.0 copy-done.1
  228.5 7.9 %fusion = f32[896,512]{0,1:T(8,128)S(1)} fusion(bf16[512,4096]{1,0:T(8,128)(2,1)S(1)} %copy-done.1, bf16[4096,896]{1,0:T(8,128)(2,1)} %param.11, bf16[4096,896]{1,0:T(8,128)(2,1)S(1)} %copy-done), kind=kOutput, calls=%fused_computation.4 | convolution fusion | flops 3780116480 | bytes 20709376 | tf_op jit(solution)/shard_map/dot_general | solution.py:18
  236.5 133.2 %all-gather.9.cloned.1.call-done = bf16[4096,896]{1,0:T(8,128)(2,1)} async-done(((bf16[512,896]{1,0:T(8,128)(2,1)}), bf16[4096,896]{1,0:T(8,128)(2,1)}) %all-gather.9.cloned.1.call-update) | async-done | bytes 7340048 | tf_op jit(solution)/shard_map/all_gather | solution.py:30
  369.7 151.2 %all-gather.11.cloned.1.call-done = bf16[896,4096]{1,0:T(8,128)(2,1)} async-done(((bf16[896,512]{1,0:T(8,128)(2,1)}), bf16[896,4096]{1,0:T(8,128)(2,1)}) %all-gather.11.cloned.1.call-update) | async-done | bytes 7340048 | tf_op jit(solution)/shard_map/all_gather | solution.py:34
  520.9 17.2 %convolution_bitcast_fusion = f32[1,512,4096]{2,1,0:T(8,128)} fusion(bf16[896,4096]{1,0:T(8,128)(2,1)} %all-gather.11.cloned.1.call-done, f32[512,896]{1,0:T(8,128)} %fusion.22, bf16[512,4096]{1,0:T(8,128)(2,1)} %all-gather.5.cloned.1.call-done, bf16[4096,896]{1,0:T(8,128)(2,1)} %all-gather.9.cloned.1.call-done), kind=kOutput, calls=%fused_computation.14 | convolution fusion | flops 7518945280 | bytes 29097984 | tf_op jit(solution)/shard_map/dot_general | solution.py:36
  538.2 22.9 %fusion.9 = f32[1,512,4096]{2,1,0:T(8,128)} fusion(bf16[896,4096]{1,0:T(8,128)(2,1)} %param.13, bf16[896,4096]{1,0:T(8,128)(2,1)} %all-gather.11.cloned.1.call-done, f32[896,512]{0,1:T(8,128)S(1)} %fusion, bf16[512,4096]{1,0:T(8,128)(2,1)} %all-gather.5.cloned.1.call-done, bf16[4096,896]{1,0:T(8,128)(2,1)} %param.12, ...), kind=kOutput, calls=%fused_computation.13 | convolution fusion | flops 7562985472 | bytes 43778048 | tf_op jit(solution)/shard_map/dot_general | solution.py:37
  561.0 11.6 %pad_maximum_fusion = f32[2,512,4096]{2,1,0:T(8,128)} fusion(f32[1,512,4096]{2,1,0:T(8,128)} %fusion.9, f32[1,512,4096]{2,1,0:T(8,128)} %convolution_bitcast_fusion), kind=kLoop, calls=%fused_computation | loop fusion | flops 4194304 | bytes 33554432 | tf_op jit(solution)/shard_map/stack | solution.py:38
  572.6 0.0 reduce-scatter.2.cloned.1.call-update
  572.6 147.9 %reduce-scatter.2.cloned.1.call-done = f32[2,512,256]{2,1,0:T(8,128)} async-done(((f32[2,512,4096]{2,1,0:T(8,128)}), f32[2,512,256]{2,1,0:T(8,128)}) %reduce-scatter.2.cloned.1.call-update) | async-done | bytes 1048592 | tf_op jit(solution)/shard_map/reduce_scatter | solution.py:39
  720.5 1.3 convert_element_type.47
  721.8 0.8 slice_bitcast_fusion
Async XLA Ops:
  7.2 63.6 %all-gather.5.cloned.1.call-start = ((), (), s32[]{:S(2)}) async-start(), calls=%async_computation.1 | async-start | bytes 4456448 | tf_op jit(solution)/shard_map/all_gather | solution.py:25
  7.9 210.4 %all-gather.7.cloned.1.call-start = ((), (), s32[]{:S(2)}) async-start(), calls=%async_computation.2 | async-start | bytes 8257536 | tf_op jit(solution)/shard_map/all_gather | solution.py:27
  8.6 361.0 %all-gather.9.cloned.1.call-start = ((), (), s32[]{:S(2)}) async-start(), calls=%async_computation.3 | async-start | bytes 8257536 | tf_op jit(solution)/shard_map/all_gather | solution.py:30
  9.4 511.5 %all-gather.11.cloned.1.call-start = ((), (), s32[]{:S(2)}) async-start(), calls=%async_computation.4 | async-start | bytes 8257536 | tf_op jit(solution)/shard_map/all_gather | solution.py:34
  10.0 710.6 %reduce-scatter.2.cloned.1.call-start = ((), (), s32[]{:S(2)}) async-start(), calls=%async_computation.5 | async-start | bytes 17825792 | tf_op jit(solution)/shard_map/reduce_scatter | solution.py:39
  218.3 10.2 %copy-start = (bf16[4096,896]{1,0:T(8,128)(2,1)S(1)}, bf16[4096,896]{1,0:T(8,128)(2,1)}, u32[]{:S(2)}) copy-start(bf16[4096,896]{1,0:T(8,128)(2,1)} %all-gather.7.cloned.1.call-done) | copy-start | bytes 22020100
  218.3 10.2 %copy-start.1 = (bf16[512,4096]{1,0:T(8,128)(2,1)S(1)}, bf16[512,4096]{1,0:T(8,128)(2,1)}, u32[]{:S(2)}) copy-start(bf16[512,4096]{1,0:T(8,128)(2,1)} %all-gather.5.cloned.1.call-done) | copy-start | bytes 12582916
Sparse Core Ops, SparseCore 0:
  10.3 60.4 all-gather.4
  72.4 145.8 all-gather.6
  220.0 149.6 all-gather.8
  371.2 149.6 all-gather.10
  572.7 147.7 reduce-scatter.1
where the time goes:
time: 729 us
  waiting for transfers between devices  643 us (88%)
  matrix products  58.3 us (8%)
  between operations  13.8 us (2%)
  other arithmetic  12.8 us (2%)
    all_gather x1, waiting for transfers between devices, local(): piece = lax.all_gather(down_online, 'dp', axis=1, tiled=True)  151 us
    reduce_scatter x1, waiting for transfers between devices, local(): summed = lax.psum_scatter(terms, 'mp', scatter_dimension=2, tiled=True)  148 us
    all_gather x1, waiting for transfers between devices, local(): lax.all_gather(gate_online, 'dp', axis=0, tiled=True)  148 us
    all_gather x1, waiting for transfers between devices, local(): lax.all_gather(up_online, 'dp', axis=0, tiled=True)  133 us
    all_gather x1, waiting for transfers between devices, local(): features_all = lax.all_gather(hidden_states, 'mp', axis=1, tiled=True)  60.8 us
    dot_general x1, matrix products, local(): jnp.dot(inner_t, target_piece, preferred_element_type=jnp.float32)  22.9 us
    dot_general x1, matrix products, local(): online_part = jnp.dot(inner_o, piece, preferred_element_type=jnp.float32)  17.2 us
  transfers between devices with their start and end apart: 5, of which 5 were waited for; matrix products, arithmetic and copies ran while one was open for 2% of the time, Pallas kernels for 0%

commit v1 on v0

v1 whole, which is shorter than its diff:
```python
import functools

import jax
import jax.numpy as jnp
from jax import lax
from jax.experimental import pallas as pl
from jax.experimental.pallas import tpu as pltpu
from jax.sharding import PartitionSpec as P

POLYAK = 0.25
MESH = pl.DeviceIdType.MESH


def blend(online, previous):
    return (
        POLYAK * online.astype(jnp.float32) + (1.0 - POLYAK) * previous.astype(jnp.float32)
    ).astype(jnp.bfloat16)


def gather_kernel(ndp, nmp, h_ref, g_ref, u_ref, dn_ref, hf_ref, gf_ref, uf_ref, df_ref,
                  send_sem, recv_sem, local_sem):
    d = lax.axis_index("dp")
    m = lax.axis_index("mp")
    kr = g_ref.shape[0]
    dc = dn_ref.shape[1]
    hc = h_ref.shape[1]
    rows = pl.ds(pl.multiple_of(d * kr, kr), kr)
    cols = pl.ds(pl.multiple_of(d * dc, dc), dc)
    hcols = pl.ds(pl.multiple_of(m * hc, hc), hc)

    locals_ = [
        pltpu.make_async_copy(h_ref, hf_ref.at[:, hcols], local_sem.at[0]),
        pltpu.make_async_copy(g_ref, gf_ref.at[rows], local_sem.at[1]),
        pltpu.make_async_copy(u_ref, uf_ref.at[rows], local_sem.at[2]),
        pltpu.make_async_copy(dn_ref, df_ref.at[:, cols], local_sem.at[3]),
    ]
    for c in locals_:
        c.start()

    copies = []
    k = 0
    for s in range(1, ndp):
        peer = lax.rem(d + s, ndp)
        for src, dst in ((g_ref, gf_ref.at[rows]), (u_ref, uf_ref.at[rows]),
                         (dn_ref, df_ref.at[:, cols])):
            copies.append(pltpu.make_async_remote_copy(
                src_ref=src, dst_ref=dst, send_sem=send_sem.at[k], recv_sem=recv_sem.at[k],
                device_id=(peer, m), device_id_type=MESH))
            k += 1
    for s in range(1, nmp):
        peer = lax.rem(m + s, nmp)
        copies.append(pltpu.make_async_remote_copy(
            src_ref=h_ref, dst_ref=hf_ref.at[:, hcols], send_sem=send_sem.at[k],
            recv_sem=recv_sem.at[k], device_id=(d, peer), device_id_type=MESH))
        k += 1
    for c in copies:
        c.start()
    for c in locals_:
        c.wait()
    for c in copies:
        c.wait()


def gather_all(h, g, u, dn, ndp, nmp):
    n_copies = 3 * (ndp - 1) + (nmp - 1)
    any_spec = pl.BlockSpec(memory_space=pl.ANY)
    out_shape = (
        jax.ShapeDtypeStruct((h.shape[0], h.shape[1] * nmp), h.dtype),
        jax.ShapeDtypeStruct((g.shape[0] * ndp, g.shape[1]), g.dtype),
        jax.ShapeDtypeStruct((u.shape[0] * ndp, u.shape[1]), u.dtype),
        jax.ShapeDtypeStruct((dn.shape[0], dn.shape[1] * ndp), dn.dtype),
    )
    return pl.pallas_call(
        functools.partial(gather_kernel, ndp, nmp),
        out_shape=out_shape,
        in_specs=[any_spec] * 4,
        out_specs=[any_spec] * 4,
        scratch_shapes=[
            pltpu.SemaphoreType.DMA((n_copies,)),
            pltpu.SemaphoreType.DMA((n_copies,)),
            pltpu.SemaphoreType.DMA((4,)),
        ],
        compiler_params=pltpu.CompilerParams(has_side_effects=True),
    )(h, g, u, dn)


def local(ndp, nmp, hidden_states, gate_online, up_online, down_online, gate_previous,
          up_previous, down_previous):
    features_all, gate_full, up_full, down_full = gather_all(
        hidden_states, gate_online, up_online, down_online, ndp, nmp)

    def pair(piece, previous):
        target_piece = blend(piece, previous)
        o = jnp.dot(features_all, piece, preferred_element_type=jnp.float32)
        t = jnp.dot(features_all, target_piece, preferred_element_type=jnp.float32)
        return o, t

    gate_o, gate_t = pair(gate_full, gate_previous)
    up_o, up_t = pair(up_full, up_previous)
    inner_o = (jax.nn.silu(gate_o) * up_o).astype(jnp.bfloat16)
    inner_t = (jax.nn.silu(gate_t) * up_t).astype(jnp.bfloat16)
    target_down = blend(down_full, down_previous)
    online_part = jnp.dot(inner_o, down_full, preferred_element_type=jnp.float32)
    target_part = jnp.dot(inner_t, target_down, preferred_element_type=jnp.float32)
    terms = jnp.stack([online_part, target_part], axis=0)
    summed = lax.psum_scatter(terms, "mp", scatter_dimension=2, tiled=True)
    result = summed.astype(jnp.bfloat16)
    return (result[0], result[1])


def solution(mesh):
    ndp = mesh.shape["dp"]
    nmp = mesh.shape["mp"]
    in_specs = (
        P("dp", "mp"),
        P("dp", "mp"),
        P("dp", "mp"),
        P("mp", "dp"),
        P(None, "mp"),
        P(None, "mp"),
        P("mp", None),
    )
    out_specs = (P("dp", "mp"), P("dp", "mp"))
    return jax.shard_map(functools.partial(local, ndp, nmp), mesh=mesh, in_specs=in_specs,
                         out_specs=out_specs, check_vma=False)
```

time: 729 us -> 545 us (0.75)
  waiting for transfers between devices: 643 us -> 158 us
  Pallas kernels: 0 us -> 303 us
    all_gather x4 -> x0, waiting for transfers between devices: 493 us -> none  [the longest x1 151 us: local(): piece = lax.all_gather(down_online, 'dp', axis=1, tiled=True)]
    pallas_call x0 -> x1, Pallas kernels: none -> 303 us  [gather_all(): pl.pallas_call(functools.partial(gather_kernel, ndp, nmp), out_shape=out_...]
    reduce_scatter x1, waiting for transfers between devices: 148 us -> 158 us  [local(): summed = lax.psum_scatter(terms, 'mp', scatter_dimension=2, tiled=True)]
  transfers between devices with their start and end apart: 5 -> 1, of which waited for: 5 -> 1; matrix products, arithmetic and copies ran while one was open for 2% -> 0% of each run, Pallas kernels for 0% -> 0%
where the time goes in v1:
time: 545 us
  Pallas kernels  303 us (56%)
  waiting for transfers between devices  158 us (29%)
  matrix products  56.5 us (10%)
  between operations  14.1 us (3%)
  other arithmetic  12.8 us (2%)
    pallas_call x1, Pallas kernels, gather_all(): pl.pallas_call(functools.partial(gather_kernel, ndp, nmp), out_shape=out_...  303 us
    reduce_scatter x1, waiting for transfers between devices, local(): summed = lax.psum_scatter(terms, 'mp', scatter_dimension=2, tiled=True)  158 us
    dot_general x1, matrix products, local(): jnp.dot(inner_t, target_down, preferred_element_type=jnp.float32)  23.1 us
    dot_general x1, matrix products, local(): jnp.dot(inner_o, down_full, preferred_element_type=jnp.float32)  17.4 us
    another operation x1, other arithmetic, local(): terms = jnp.stack([online_part, target_part], axis=0)  11.6 us
  transfers between devices with their start and end apart: 1, of which 1 were waited for; matrix products, arithmetic and copies ran while one was open for 0% of the time, Pallas kernels for 0%

profile of v1, /device:TPU:1, one launch (start us, length us, event | category | flops | bytes accessed | tf_op | source)
XLA Modules:
  0.0 545.2 jit_solution(4709121395465431118)
XLA Ops:
  7.2 0.0 reduce-scatter.2.cloned.1.call-start
  7.2 0.0 slice-start
  7.2 303.3 %shard_map.86 = (bf16[512,4096]{1,0:T(8,128)(2,1)}, bf16[4096,896]{1,0:T(8,128)(2,1)}, bf16[4096,896]{1,0:T(8,128)(2,1)}, bf16[896,4096]{1,0:T(8,128)(2,1)}) custom-call(bf16[512,256]{1,0:T(8,128)(2,1)} %h_ref.1, bf16[512,896]{1,0:T(8,128)(2,1)} %g_ref.1, bf16[512,896]{1,0:T(8,128)(2,1)} %u_ref.1, bf16[896,512]{1,0:T(8,128)(2,1)} %dn_ref.1), custom_call_target="tpu_custom_call" | custom-call | tf_op jit(solution)/shard_map/pallas_call | solution.py:73
  310.5 0.0 slice-start.1
  310.5 0.0 copy-start
  310.6 0.0 copy-start.1
  310.6 10.2 %fusion.18 = f32[512,896]{1,0:T(8,128)} fusion(bf16[512,4096]{1,0:T(8,128)(2,1)} %get-tuple-element.6, bf16[4096,896]{1,0:T(8,128)(2,1)} %get-tuple-element.7), kind=kOutput, calls=%fused_computation.25 | convolution fusion | flops 3758096384 | bytes 13369344 | tf_op jit(solution)/shard_map/dot_general | solution.py:94
  320.8 0.0 slice-done
  320.8 0.0 slice-done.1
  320.8 0.0 copy-done
  320.8 0.0 copy-done.1
  320.8 5.8 %fusion.1 = f32[512,896]{1,0:T(8,128)} fusion(bf16[512,4096]{1,0:T(8,128)(2,1)S(1)} %copy-done.1, bf16[4096,896]{1,0:T(8,128)(2,1)S(1)} %bitcast.16, bf16[4096,896]{1,0:T(8,128)(2,1)S(1)} %copy-done), kind=kOutput, calls=%fused_computation.5 | convolution fusion | flops 3780116480 | bytes 20709376 | tf_op jit(solution)/shard_map/dot_general | solution.py:95
  326.6 0.0 copy-start.2
  326.6 17.4 %convolution_bitcast_fusion = f32[1,512,4096]{2,1,0:T(8,128)} fusion(bf16[896,4096]{1,0:T(8,128)(2,1)} %get-tuple-element.9, f32[512,896]{1,0:T(8,128)} %fusion.18, bf16[512,4096]{1,0:T(8,128)(2,1)} %get-tuple-element.6, bf16[4096,896]{1,0:T(8,128)(2,1)} %get-tuple-element.8), kind=kOutput, calls=%fused_computation.14 | convolution fusion | flops 7518945280 | bytes 29097984 | tf_op jit(solution)/shard_map/dot_general | solution.py:103
  344.0 0.0 copy-done.2
  344.0 23.1 %fusion.9 = f32[1,512,4096]{2,1,0:T(8,128)} fusion(bf16[896,4096]{1,0:T(8,128)(2,1)} %param.13, bf16[896,4096]{1,0:T(8,128)(2,1)} %get-tuple-element.9, f32[512,896]{1,0:T(8,128)S(1)} %copy-done.2, bf16[512,4096]{1,0:T(8,128)(2,1)} %get-tuple-element.6, bf16[4096,896]{1,0:T(8,128)(2,1)} %param.11, bf16[4096,896]{1,0:T(8,128)(2,1)} %get-tuple-element.7), kind=kOutput, calls=%fused_computation.13 | convolution fusion | flops 7562985472 | bytes 43778048 | tf_op jit(solution)/shard_map/dot_general | solution.py:104
  367.1 11.6 %pad_maximum_fusion = f32[2,512,4096]{2,1,0:T(8,128)} fusion(f32[1,512,4096]{2,1,0:T(8,128)} %fusion.9, f32[1,512,4096]{2,1,0:T(8,128)} %convolution_bitcast_fusion), kind=kLoop, calls=%fused_computation | loop fusion | flops 4194304 | bytes 33554432 | tf_op jit(solution)/shard_map/stack | solution.py:105
  378.6 0.0 reduce-scatter.2.cloned.1.call-update
  378.7 157.6 %reduce-scatter.2.cloned.1.call-done = f32[2,512,256]{2,1,0:T(8,128)} async-done(((f32[2,512,4096]{2,1,0:T(8,128)}), f32[2,512,256]{2,1,0:T(8,128)}) %reduce-scatter.2.cloned.1.call-update) | async-done | bytes 1048592 | tf_op jit(solution)/shard_map/reduce_scatter | solution.py:106
  536.3 1.3 convert_element_type.47
  537.6 0.8 slice_bitcast_fusion
  (1 shorter events, 0.0 us)
Async XLA Ops:
  7.2 529.1 %reduce-scatter.2.cloned.1.call-start = ((), (), s32[]{:S(2)}) async-start(), calls=%async_computation.1 | async-start | bytes 17825792 | tf_op jit(solution)/shard_map/reduce_scatter | solution.py:106
  7.2 313.6 %slice-start = ((s8[7340032]{0:T(1024)(128)(4,1)}), s8[3145728]{0:T(1024)(128)(4,1)S(1)}, s32[]{:S(2)}) async-start(s8[7340032]{0:T(1024)(128)(4,1)} %bitcast.15), calls=%async_computation.2 | async-start | bytes 6291456
  310.5 10.3 %slice-start.1 = ((s8[7340032]{0:T(1024)(128)(4,1)}), s8[4194304]{0:T(1024)(128)(4,1)S(1)}, s32[]{:S(2)}) async-start(s8[7340032]{0:T(1024)(128)(4,1)} %bitcast.15), calls=%async_computation.3 | async-start | bytes 8388608
  310.5 10.3 %copy-start = (bf16[4096,896]{1,0:T(8,128)(2,1)S(1)}, bf16[4096,896]{1,0:T(8,128)(2,1)}, u32[]{:S(2)}) copy-start(bf16[4096,896]{1,0:T(8,128)(2,1)} %get-tuple-element.8) | copy-start | bytes 22020100
  310.6 10.3 %copy-start.1 = (bf16[512,4096]{1,0:T(8,128)(2,1)S(1)}, bf16[512,4096]{1,0:T(8,128)(2,1)}, u32[]{:S(2)}) copy-start(bf16[512,4096]{1,0:T(8,128)(2,1)} %get-tuple-element.6) | copy-start | bytes 12582916
  326.6 17.4 %copy-start.2 = (f32[512,896]{1,0:T(8,128)S(1)}, f32[512,896]{1,0:T(8,128)}, u32[]{:S(2)}) copy-start(f32[512,896]{1,0:T(8,128)} %fusion.1) | copy-start | bytes 5505028
Sparse Core Ops, SparseCore 0:
  378.8 157.4 reduce-scatter.1

commit v2 on v1

--- a/solution.py
+++ b/solution.py
@@ -84,6 +84,58 @@
     )(h, g, u, dn)
 
 
+def reduce_kernel(nmp, t_ref, o_ref, buf, send_sem, recv_sem, local_sem):
+    d = lax.axis_index("dp")
+    m = lax.axis_index("mp")
+    w = o_ref.shape[2]
+    mine = pl.ds(pl.multiple_of(m * w, w), w)
+    local_copy = pltpu.make_async_copy(t_ref.at[:, :, mine], buf.at[0], local_sem.at[0])
+    local_copy.start()
+    copies = []
+    for s in range(1, nmp):
+        peer = lax.rem(m + s, nmp)
+        theirs = pl.ds(pl.multiple_of(peer * w, w), w)
+        copies.append(pltpu.make_async_remote_copy(
+            src_ref=t_ref.at[:, :, theirs], dst_ref=buf.at[s], send_sem=send_sem.at[s],
+            recv_sem=recv_sem.at[s], device_id=(d, peer), device_id_type=MESH))
+    for c in copies:
+        c.start()
+    local_copy.wait()
+    for c in copies:
+        c.wait()
+    rows = 32
+
+    def body(i, carry):
+        r = pl.ds(pl.multiple_of(i * rows, rows), rows)
+        for k in range(o_ref.shape[0]):
+            acc = buf[0, k, r, :].astype(jnp.float32)
+            for s in range(1, nmp):
+                acc = acc + buf[s, k, r, :].astype(jnp.float32)
+            o_ref[k, r, :] = acc.astype(o_ref.dtype)
+        return carry
+
+    lax.fori_loop(0, o_ref.shape[1] // rows, body, 0)
+
+
+def reduce_scatter(terms, nmp):
+    n, t, width = terms.shape
+    w = width // nmp
+    return pl.pallas_call(
+        functools.partial(reduce_kernel, nmp),
+        out_shape=jax.ShapeDtypeStruct((n, t, w), jnp.bfloat16),
+        in_specs=[pl.BlockSpec(memory_space=pl.ANY)],
+        out_specs=pl.BlockSpec(memory_space=pltpu.VMEM),
+        scratch_shapes=[
+            pltpu.VMEM((nmp, n, t, w), jnp.bfloat16),
+            pltpu.SemaphoreType.DMA((nmp,)),
+            pltpu.SemaphoreType.DMA((nmp,)),
+            pltpu.SemaphoreType.DMA((1,)),
+        ],
+        compiler_params=pltpu.CompilerParams(has_side_effects=True,
+                                             vmem_limit_bytes=48 * 1024 * 1024),
+    )(terms)
+
+
 def local(ndp, nmp, hidden_states, gate_online, up_online, down_online, gate_previous,
           up_previous, down_previous):
     features_all, gate_full, up_full, down_full = gather_all(
@@ -102,9 +154,8 @@
     target_down = blend(down_full, down_previous)
     online_part = jnp.dot(inner_o, down_full, preferred_element_type=jnp.float32)
     target_part = jnp.dot(inner_t, target_down, preferred_element_type=jnp.float32)
-    terms = jnp.stack([online_part, target_part], axis=0)
-    summed = lax.psum_scatter(terms, "mp", scatter_dimension=2, tiled=True)
-    result = summed.astype(jnp.bfloat16)
+    terms = jnp.stack([online_part, target_part], axis=0).astype(jnp.bfloat16)
+    result = reduce_scatter(terms, nmp)
     return (result[0], result[1])
 
 

time: 545 us -> 527 us (0.967)
  the two profiles are of different devices: /device:TPU:1 before, /device:TPU:97 now
where the time goes in v2:
time: 527 us; the launch traced here: 526 us
  Pallas kernels  456 us (87%)
  matrix products  61.3 us (12%)
  other arithmetic  7.44 us (1%)
    pallas_call x1, Pallas kernels, gather_all(): pl.pallas_call(functools.partial(gather_kernel, ndp, nmp), out_shape=out_...  314 us
    pallas_call x1, Pallas kernels, reduce_scatter(): pl.pallas_call(functools.partial(reduce_kernel, nmp), out_shape=jax.Shape...  142 us
    dot_general x1, matrix products, local(): jnp.dot(inner_t, target_down, preferred_element_type=jnp.float32)  24.2 us
    dot_general x1, matrix products, local(): jnp.dot(inner_o, down_full, preferred_element_type=jnp.float32)  16.3 us
    dot_general x1, matrix products, pair(): t = jnp.dot(features_all, target_piece, preferred_element_type=jnp.float32)  11 us

profile of v2, /device:TPU:97, one launch (start us, length us, event | category | flops | bytes accessed | tf_op | source)
XLA Modules:
  0.0 526.5 jit_solution(16946194563063668398)
XLA Ops:
  0.6 313.7 %shard_map.86 = (bf16[512,4096]{1,0:T(8,128)(2,1)}, bf16[4096,896]{1,0:T(8,128)(2,1)}, bf16[4096,896]{1,0:T(8,128)(2,1)}, bf16[896,4096]{1,0:T(8,128)(2,1)}) custom-call(bf16[512,256]{1,0:T(8,128)(2,1)} %h_ref.1, bf16[512,896]{1,0:T(8,128)(2,1)} %g_ref.1, bf16[512,896]{1,0:T(8,128)(2,1)} %u_ref.1, bf16[896,512]{1,0:T(8,128)(2,1)} %dn_ref.1), custom_call_target="tpu_custom_call" | custom-call | tf_op jit(solution)/shard_map/pallas_call | solution.py:73
  314.4 9.8 %fusion.20 = f32[512,896]{1,0:T(8,128)S(1)} fusion(bf16[512,4096]{1,0:T(8,128)(2,1)} %get-tuple-element.6, bf16[4096,896]{1,0:T(8,128)(2,1)} %get-tuple-element.7), kind=kOutput, calls=%fused_computation.27 | convolution fusion | flops 3758096384 | bytes 13369344 | tf_op jit(solution)/shard_map/dot_general | solution.py:146
  324.2 16.3 %fusion.10 = bf16[1,512,4096]{2,1,0:T(8,128)(2,1)} fusion(bf16[896,4096]{1,0:T(8,128)(2,1)} %get-tuple-element.9, f32[512,896]{1,0:T(8,128)S(1)} %fusion.20, bf16[512,4096]{1,0:T(8,128)(2,1)} %get-tuple-element.6, bf16[4096,896]{1,0:T(8,128)(2,1)} %get-tuple-element.8), kind=kOutput, calls=%fused_computation.15 | convolution fusion | flops 7521042432 | bytes 24903680 | tf_op jit(solution)/shard_map/dot_general | solution.py:155
  340.5 11.0 %fusion.1 = f32[512,896]{1,0:T(8,128)S(1)} fusion(bf16[512,4096]{1,0:T(8,128)(2,1)} %get-tuple-element.6, bf16[4096,896]{1,0:T(8,128)(2,1)} %param.12, bf16[4096,896]{1,0:T(8,128)(2,1)} %get-tuple-element.8), kind=kOutput, calls=%fused_computation.5 | convolution fusion | flops 3780116480 | bytes 20709376 | tf_op jit(solution)/shard_map/dot_general | solution.py:147
  351.6 24.2 %fusion.11 = bf16[1,512,4096]{2,1,0:T(8,128)(2,1)} fusion(bf16[896,4096]{1,0:T(8,128)(2,1)} %param.13, bf16[896,4096]{1,0:T(8,128)(2,1)} %get-tuple-element.9, f32[512,896]{1,0:T(8,128)S(1)} %fusion.1, bf16[512,4096]{1,0:T(8,128)(2,1)} %get-tuple-element.6, bf16[4096,896]{1,0:T(8,128)(2,1)} %param.11, bf16[4096,896]{1,0:T(8,128)(2,1)} %get-tuple-element.7), kind=kOutput, calls=%fused_computation.16 | convolution fusion | flops 7565082624 | bytes 39583744 | tf_op jit(solution)/shard_map/dot_general | solution.py:156
  375.7 7.4 %pad_maximum_fusion.t_ref = bf16[2,512,4096]{2,1,0:T(8,128)(2,1)} fusion(bf16[1,512,4096]{2,1,0:T(8,128)(2,1)} %fusion.11, bf16[1,512,4096]{2,1,0:T(8,128)(2,1)} %fusion.10), kind=kLoop, calls=%fused_computation.3 | loop fusion | flops 4194304 | bytes 16777216 | tf_op jit(solution)/shard_map/stack | solution.py:157
  383.2 142.5 %shard_map.87 = bf16[2,512,256]{2,1,0:T(8,128)(2,1)S(1)} custom-call(bf16[2,512,4096]{2,1,0:T(8,128)(2,1)} %pad_maximum_fusion.t_ref), custom_call_target="tpu_custom_call" | custom-call | tf_op jit(solution)/shard_map/pallas_call | solution.py:123
  525.7 0.8 slice_bitcast_fusion

commit v3 on v2

--- a/solution.py
+++ b/solution.py
@@ -17,22 +17,19 @@
     ).astype(jnp.bfloat16)
 
 
-def gather_kernel(ndp, nmp, h_ref, g_ref, u_ref, dn_ref, hf_ref, gf_ref, uf_ref, df_ref,
-                  send_sem, recv_sem, local_sem):
+def gather_kernel(ndp, g_ref, u_ref, dn_ref, gf_ref, uf_ref, df_ref, send_sem, recv_sem,
+                  local_sem):
     d = lax.axis_index("dp")
     m = lax.axis_index("mp")
     kr = g_ref.shape[0]
     dc = dn_ref.shape[1]
-    hc = h_ref.shape[1]
     rows = pl.ds(pl.multiple_of(d * kr, kr), kr)
     cols = pl.ds(pl.multiple_of(d * dc, dc), dc)
-    hcols = pl.ds(pl.multiple_of(m * hc, hc), hc)
 
     locals_ = [
-        pltpu.make_async_copy(h_ref, hf_ref.at[:, hcols], local_sem.at[0]),
-        pltpu.make_async_copy(g_ref, gf_ref.at[rows], local_sem.at[1]),
-        pltpu.make_async_copy(u_ref, uf_ref.at[rows], local_sem.at[2]),
-        pltpu.make_async_copy(dn_ref, df_ref.at[:, cols], local_sem.at[3]),
+        pltpu.make_async_copy(g_ref, gf_ref.at[rows], local_sem.at[0]),
+        pltpu.make_async_copy(u_ref, uf_ref.at[rows], local_sem.at[1]),
+        pltpu.make_async_copy(dn_ref, df_ref.at[:, cols], local_sem.at[2]),
     ]
     for c in locals_:
         c.start()
@@ -47,12 +44,6 @@
                 src_ref=src, dst_ref=dst, send_sem=send_sem.at[k], recv_sem=recv_sem.at[k],
                 device_id=(peer, m), device_id_type=MESH))
             k += 1
-    for s in range(1, nmp):
-        peer = lax.rem(m + s, nmp)
-        copies.append(pltpu.make_async_remote_copy(
-            src_ref=h_ref, dst_ref=hf_ref.at[:, hcols], send_sem=send_sem.at[k],
-            recv_sem=recv_sem.at[k], device_id=(d, peer), device_id_type=MESH))
-        k += 1
     for c in copies:
         c.start()
     for c in locals_:
@@ -61,27 +52,26 @@
         c.wait()
 
 
-def gather_all(h, g, u, dn, ndp, nmp):
-    n_copies = 3 * (ndp - 1) + (nmp - 1)
+def gather_weights(g, u, dn, ndp):
+    n_copies = 3 * (ndp - 1)
     any_spec = pl.BlockSpec(memory_space=pl.ANY)
     out_shape = (
-        jax.ShapeDtypeStruct((h.shape[0], h.shape[1] * nmp), h.dtype),
         jax.ShapeDtypeStruct((g.shape[0] * ndp, g.shape[1]), g.dtype),
         jax.ShapeDtypeStruct((u.shape[0] * ndp, u.shape[1]), u.dtype),
         jax.ShapeDtypeStruct((dn.shape[0], dn.shape[1] * ndp), dn.dtype),
     )
     return pl.pallas_call(
-        functools.partial(gather_kernel, ndp, nmp),
+        functools.partial(gather_kernel, ndp),
         out_shape=out_shape,
-        in_specs=[any_spec] * 4,
-        out_specs=[any_spec] * 4,
+        in_specs=[any_spec] * 3,
+        out_specs=[any_spec] * 3,
         scratch_shapes=[
             pltpu.SemaphoreType.DMA((n_copies,)),
             pltpu.SemaphoreType.DMA((n_copies,)),
-            pltpu.SemaphoreType.DMA((4,)),
+            pltpu.SemaphoreType.DMA((3,)),
         ],
         compiler_params=pltpu.CompilerParams(has_side_effects=True),
-    )(h, g, u, dn)
+    )(g, u, dn)
 
 
 def reduce_kernel(nmp, t_ref, o_ref, buf, send_sem, recv_sem, local_sem):
@@ -138,8 +128,8 @@
 
 def local(ndp, nmp, hidden_states, gate_online, up_online, down_online, gate_previous,
           up_previous, down_previous):
-    features_all, gate_full, up_full, down_full = gather_all(
-        hidden_states, gate_online, up_online, down_online, ndp, nmp)
+    features_all = lax.all_gather(hidden_states, "mp", axis=1, tiled=True)
+    gate_full, up_full, down_full = gather_weights(gate_online, up_online, down_online, ndp)
 
     def pair(piece, previous):
         target_piece = blend(piece, previous)
@@ -154,9 +144,9 @@
     target_down = blend(down_full, down_previous)
     online_part = jnp.dot(inner_o, down_full, preferred_element_type=jnp.float32)
     target_part = jnp.dot(inner_t, target_down, preferred_element_type=jnp.float32)
-    terms = jnp.stack([online_part, target_part], axis=0).astype(jnp.bfloat16)
-    result = reduce_scatter(terms, nmp)
-    return (result[0], result[1])
+    online_out = lax.psum_scatter(online_part, "mp", scatter_dimension=1, tiled=True)
+    target_out = reduce_scatter(target_part.astype(jnp.bfloat16)[None], nmp)
+    return (online_out.astype(jnp.bfloat16), target_out[0])
 
 
 def solution(mesh):

time: 527 us -> 456 us (0.87)
  the two profiles are of different devices: /device:TPU:97 before, /device:TPU:1 now
where the time goes in v3:
time: 456 us
  Pallas kernels  335 us (73%)
  matrix products  68.1 us (15%)
  waiting for transfers between devices  33.8 us (7%)
  between operations  14.1 us (3%)
    pallas_call x1, Pallas kernels, gather_weights(): pl.pallas_call(functools.partial(gather_kernel, ndp), out_shape=out_shape...  265 us
    pallas_call x1, Pallas kernels, reduce_scatter(): pl.pallas_call(functools.partial(reduce_kernel, nmp), out_shape=jax.Shape...  70.6 us
    reduce_scatter x1, waiting for transfers between devices, local(): lax.psum_scatter(online_part, 'mp', scatter_dimension=1, tiled=True)  33 us
    dot_general x1, matrix products, local(): jnp.dot(inner_t, target_down, preferred_element_type=jnp.float32)  30.9 us
    dot_general x1, matrix products, local(): jnp.dot(inner_o, down_full, preferred_element_type=jnp.float32)  18.3 us
    dot_general x1, matrix products, pair(): t = jnp.dot(features_all, target_piece, preferred_element_type=jnp.float32)  10.6 us
  transfers between devices with their start and end apart: 2, of which 1 were waited for; matrix products, arithmetic and copies ran while one was open for 9% of the time, Pallas kernels for 74%

profile of v3, /device:TPU:1, one launch (start us, length us, event | category | flops | bytes accessed | tf_op | source)
XLA Modules:
  0.0 455.9 jit_solution(2293221479667231600)
XLA Ops:
  7.2 0.0 all-gather.2.cloned.1.call-start
  7.2 0.7 all-gather.2.cloned.1.call-update
  7.9 0.0 reduce-scatter.2.cloned.1.call-start
  7.9 264.6 %shard_map.86 = (bf16[4096,896]{1,0:T(8,128)(2,1)}, bf16[4096,896]{1,0:T(8,128)(2,1)}, bf16[896,4096]{1,0:T(8,128)(2,1)}) custom-call(bf16[512,896]{1,0:T(8,128)(2,1)} %g_ref.1, bf16[512,896]{1,0:T(8,128)(2,1)} %u_ref.1, bf16[896,512]{1,0:T(8,128)(2,1)} %dn_ref.1), custom_call_target="tpu_custom_call" | custom-call | tf_op jit(solution)/shard_map/pallas_call | solution.py:63
  272.6 0.0 all-gather.2.cloned.1.call-done
  272.6 8.3 %fusion.28 = f32[896,512]{1,0:T(8,128)S(1)} fusion(bf16[4096,896]{1,0:T(8,128)(2,1)} %get-tuple-element.5, bf16[512,4096]{1,0:T(8,128)(2,1)} %all-gather.2.cloned.1.call-done), kind=kOutput, calls=%fused_computation.37 | convolution fusion | flops 3758096384 | bytes 13369344 | tf_op jit(solution)/shard_map/dot_general | solution.py:136
  280.9 18.3 %fusion.19 = f32[512,4096]{1,0:T(8,128)} fusion(bf16[896,4096]{1,0:T(8,128)(2,1)} %get-tuple-element.7, f32[896,512]{1,0:T(8,128)S(1)} %fusion.28, bf16[4096,896]{1,0:T(8,128)(2,1)} %get-tuple-element.6, bf16[512,4096]{1,0:T(8,128)(2,1)} %all-gather.2.cloned.1.call-done), kind=kOutput, calls=%fused_computation.28 | convolution fusion | flops 7518945280 | bytes 29097984 | tf_op jit(solution)/shard_map/dot_general | solution.py:145
  299.2 0.0 reduce-scatter.2.cloned.1.call-update
  299.2 10.6 %fusion = f32[896,512]{1,0:T(8,128)S(1)} fusion(bf16[512,4096]{1,0:T(8,128)(2,1)} %all-gather.2.cloned.1.call-done, bf16[4096,896]{1,0:T(8,128)(2,1)} %param.11, bf16[4096,896]{1,0:T(8,128)(2,1)} %get-tuple-element.5), kind=kOutput, calls=%fused_computation.3 | convolution fusion | flops 3780116480 | bytes 20709376 | tf_op jit(solution)/shard_map/dot_general | solution.py:137
  309.8 30.9 %fusion.10.t_ref = bf16[1,512,4096]{2,1,0:T(8,128)(2,1)} fusion(bf16[896,4096]{1,0:T(8,128)(2,1)} %param.13, bf16[896,4096]{1,0:T(8,128)(2,1)} %get-tuple-element.7, f32[896,512]{1,0:T(8,128)S(1)} %fusion, bf16[512,4096]{1,0:T(8,128)(2,1)} %all-gather.2.cloned.1.call-done, bf16[4096,896]{1,0:T(8,128)(2,1)} %param.12, bf16[4096,896]{1,0:T(8,128)(2,1)} %get-tuple-element.6), kind=kOutput, calls=%fused_computation.13 | convolution fusion | flops 7565082624 | bytes 39583744 | tf_op jit(solution)/shard_map/dot_general | solution.py:146
  340.7 0.0 copy-start
  340.7 2.2 copy-done
  342.9 70.6 %shard_map.87 = bf16[1,512,256]{2,1,0:T(8,128)(2,1)S(1)} custom-call(bf16[1,512,4096]{2,1,0:T(8,128)(2,1)S(1)} %copy-done), custom_call_target="tpu_custom_call" | custom-call | tf_op jit(solution)/shard_map/pallas_call | solution.py:113
  413.5 33.0 %reduce-scatter.2.cloned.1.call-done = f32[512,256]{1,0:T(8,128)} async-done(((f32[512,4096]{1,0:T(8,128)}), f32[512,256]{1,0:T(8,128)}) %reduce-scatter.2.cloned.1.call-update) | async-done | bytes 524304 | tf_op jit(solution)/shard_map/reduce_scatter | solution.py:147
  446.6 1.8 convert_element_type.40
  448.4 0.7 copy.10
Async XLA Ops:
  7.2 265.4 %all-gather.2.cloned.1.call-start = ((), (), s32[]{:S(2)}) async-start(), calls=%async_computation.1 | async-start | bytes 4456448 | tf_op jit(solution)/shard_map/all_gather | solution.py:131
  7.9 438.7 %reduce-scatter.2.cloned.1.call-start = ((), (), s32[]{:S(2)}) async-start(), calls=%async_computation.2 | async-start | bytes 8912896 | tf_op jit(solution)/shard_map/reduce_scatter | solution.py:147
  340.7 2.2 copy-start
Sparse Core Ops, SparseCore 0:
  10.3 75.1 all-gather.1
  299.3 147.2 reduce-scatter.1

commit v4 on v3

--- a/solution.py
+++ b/solution.py
@@ -17,19 +17,15 @@
     ).astype(jnp.bfloat16)
 
 
-def gather_kernel(ndp, g_ref, u_ref, dn_ref, gf_ref, uf_ref, df_ref, send_sem, recv_sem,
-                  local_sem):
+def gather_kernel(ndp, g_ref, u_ref, gf_ref, uf_ref, send_sem, recv_sem, local_sem):
     d = lax.axis_index("dp")
     m = lax.axis_index("mp")
     kr = g_ref.shape[0]
-    dc = dn_ref.shape[1]
     rows = pl.ds(pl.multiple_of(d * kr, kr), kr)
-    cols = pl.ds(pl.multiple_of(d * dc, dc), dc)
 
     locals_ = [
         pltpu.make_async_copy(g_ref, gf_ref.at[rows], local_sem.at[0]),
         pltpu.make_async_copy(u_ref, uf_ref.at[rows], local_sem.at[1]),
-        pltpu.make_async_copy(dn_ref, df_ref.at[:, cols], local_sem.at[2]),
     ]
     for c in locals_:
         c.start()
@@ -38,8 +34,7 @@
     k = 0
     for s in range(1, ndp):
         peer = lax.rem(d + s, ndp)
-        for src, dst in ((g_ref, gf_ref.at[rows]), (u_ref, uf_ref.at[rows]),
-                         (dn_ref, df_ref.at[:, cols])):
+        for src, dst in ((g_ref, gf_ref.at[rows]), (u_ref, uf_ref.at[rows])):
             copies.append(pltpu.make_async_remote_copy(
                 src_ref=src, dst_ref=dst, send_sem=send_sem.at[k], recv_sem=recv_sem.at[k],
                 device_id=(peer, m), device_id_type=MESH))
@@ -52,26 +47,25 @@
         c.wait()
 
 
-def gather_weights(g, u, dn, ndp):
-    n_copies = 3 * (ndp - 1)
+def gather_weights(g, u, ndp):
+    n_copies = 2 * (ndp - 1)
     any_spec = pl.BlockSpec(memory_space=pl.ANY)
     out_shape = (
         jax.ShapeDtypeStruct((g.shape[0] * ndp, g.shape[1]), g.dtype),
         jax.ShapeDtypeStruct((u.shape[0] * ndp, u.shape[1]), u.dtype),
-        jax.ShapeDtypeStruct((dn.shape[0], dn.shape[1] * ndp), dn.dtype),
     )
     return pl.pallas_call(
         functools.partial(gather_kernel, ndp),
         out_shape=out_shape,
-        in_specs=[any_spec] * 3,
-        out_specs=[any_spec] * 3,
+        in_specs=[any_spec] * 2,
+        out_specs=[any_spec] * 2,
         scratch_shapes=[
             pltpu.SemaphoreType.DMA((n_copies,)),
             pltpu.SemaphoreType.DMA((n_copies,)),
-            pltpu.SemaphoreType.DMA((3,)),
+            pltpu.SemaphoreType.DMA((2,)),
         ],
         compiler_params=pltpu.CompilerParams(has_side_effects=True),
-    )(g, u, dn)
+    )(g, u)
 
 
 def reduce_kernel(nmp, t_ref, o_ref, buf, send_sem, recv_sem, local_sem):
@@ -129,7 +123,8 @@
 def local(ndp, nmp, hidden_states, gate_online, up_online, down_online, gate_previous,
           up_previous, down_previous):
     features_all = lax.all_gather(hidden_states, "mp", axis=1, tiled=True)
-    gate_full, up_full, down_full = gather_weights(gate_online, up_online, down_online, ndp)
+    down_full = lax.all_gather(down_online, "dp", axis=1, tiled=True)
+    gate_full, up_full = gather_weights(gate_online, up_online, ndp)
 
     def pair(piece, previous):
         target_piece = blend(piece, previous)

time: 456 us -> 507 us (1.11)
  waiting for transfers between devices: 33.8 us -> 66.6 us
  Pallas kernels: 335 us -> 353 us
    all_gather x0 -> x1, waiting for transfers between devices: none -> 31.9 us  [local(): down_full = lax.all_gather(down_online, 'dp', axis=1, tiled=True)]
    pallas_call x1, Pallas kernels: 265 us -> 283 us  [gather_weights(): pl.pallas_call(functools.partial(gather_kernel, ndp), out_shape=out_shape...]
  transfers between devices with their start and end apart: 2 -> 3, of which waited for: 1 -> 2; matrix products, arithmetic and copies ran while one was open for 9% -> 10% of each run, Pallas kernels for 74% -> 70%
where the time goes in v4:
time: 507 us
  Pallas kernels  353 us (70%)
  matrix products  68.1 us (13%)
  waiting for transfers between devices  66.6 us (13%)
  between operations  13.8 us (3%)
    pallas_call x1, Pallas kernels, gather_weights(): pl.pallas_call(functools.partial(gather_kernel, ndp), out_shape=out_shape...  283 us
    pallas_call x1, Pallas kernels, reduce_scatter(): pl.pallas_call(functools.partial(reduce_kernel, nmp), out_shape=jax.Shape...  70.6 us
    reduce_scatter x1, waiting for transfers between devices, local(): lax.psum_scatter(online_part, 'mp', scatter_dimension=1, tiled=True)  33.2 us
    all_gather x1, waiting for transfers between devices, local(): down_full = lax.all_gather(down_online, 'dp', axis=1, tiled=True)  31.9 us
    dot_general x1, matrix products, local(): jnp.dot(inner_t, target_down, preferred_element_type=jnp.float32)  30.9 us
    dot_general x1, matrix products, local(): jnp.dot(inner_o, down_full, preferred_element_type=jnp.float32)  18.3 us
    dot_general x1, matrix products, pair(): t = jnp.dot(features_all, target_piece, preferred_element_type=jnp.float32)  10.6 us
  transfers between devices with their start and end apart: 3, of which 2 were waited for; matrix products, arithmetic and copies ran while one was open for 10% of the time, Pallas kernels for 70%

profile of v4, /device:TPU:1, one launch (start us, length us, event | category | flops | bytes accessed | tf_op | source)
XLA Modules:
  0.0 506.6 jit_solution(14739452347955813664)
XLA Ops:
  7.2 0.0 all-gather.3.cloned.1.call-start
  7.2 0.7 all-gather.3.cloned.1.call-update
  7.9 0.0 all-gather.5.cloned.1.call-start
  7.9 0.7 all-gather.5.cloned.1.call-update
  8.6 0.0 reduce-scatter.2.cloned.1.call-start
  8.7 282.7 %shard_map.86 = (bf16[4096,896]{1,0:T(8,128)(2,1)}, bf16[4096,896]{1,0:T(8,128)(2,1)}) custom-call(bf16[512,896]{1,0:T(8,128)(2,1)} %g_ref.1, bf16[512,896]{1,0:T(8,128)(2,1)} %u_ref.1), custom_call_target="tpu_custom_call" | custom-call | tf_op jit(solution)/shard_map/pallas_call | solution.py:57
  291.4 0.0 all-gather.3.cloned.1.call-done
  291.5 8.4 %fusion.28 = f32[896,512]{1,0:T(8,128)S(1)} fusion(bf16[4096,896]{1,0:T(8,128)(2,1)} %get-tuple-element.4, bf16[512,4096]{1,0:T(8,128)(2,1)} %all-gather.3.cloned.1.call-done), kind=kOutput, calls=%fused_computation.37 | convolution fusion | flops 3758096384 | bytes 13369344 | tf_op jit(solution)/shard_map/dot_general | solution.py:131
  299.8 31.9 %all-gather.5.cloned.1.call-done = bf16[896,4096]{1,0:T(8,128)(2,1)} async-done(((bf16[896,512]{1,0:T(8,128)(2,1)}), bf16[896,4096]{1,0:T(8,128)(2,1)}) %all-gather.5.cloned.1.call-update) | async-done | bytes 7340048 | tf_op jit(solution)/shard_map/all_gather | solution.py:126
  331.8 18.3 %fusion.19 = f32[512,4096]{1,0:T(8,128)} fusion(bf16[896,4096]{1,0:T(8,128)(2,1)} %all-gather.5.cloned.1.call-done, f32[896,512]{1,0:T(8,128)S(1)} %fusion.28, bf16[4096,896]{1,0:T(8,128)(2,1)} %get-tuple-element.5, bf16[512,4096]{1,0:T(8,128)(2,1)} %all-gather.3.cloned.1.call-done), kind=kOutput, calls=%fused_computation.28 | convolution fusion | flops 7518945280 | bytes 29097984 | tf_op jit(solution)/shard_map/dot_general | solution.py:140
  350.0 0.0 reduce-scatter.2.cloned.1.call-update
  350.0 10.6 %fusion = f32[896,512]{1,0:T(8,128)S(1)} fusion(bf16[512,4096]{1,0:T(8,128)(2,1)} %all-gather.3.cloned.1.call-done, bf16[4096,896]{1,0:T(8,128)(2,1)} %param.11, bf16[4096,896]{1,0:T(8,128)(2,1)} %get-tuple-element.4), kind=kOutput, calls=%fused_computation.3 | convolution fusion | flops 3780116480 | bytes 20709376 | tf_op jit(solution)/shard_map/dot_general | solution.py:132
  360.7 30.9 %fusion.10.t_ref = bf16[1,512,4096]{2,1,0:T(8,128)(2,1)} fusion(bf16[896,4096]{1,0:T(8,128)(2,1)} %param.13, bf16[896,4096]{1,0:T(8,128)(2,1)} %all-gather.5.cloned.1.call-done, f32[896,512]{1,0:T(8,128)S(1)} %fusion, bf16[512,4096]{1,0:T(8,128)(2,1)} %all-gather.3.cloned.1.call-done, bf16[4096,896]{1,0:T(8,128)(2,1)} %param.12, ...), kind=kOutput, calls=%fused_computation.13 | convolution fusion | flops 7565082624 | bytes 39583744 | tf_op jit(solution)/shard_map/dot_general | solution.py:141
  391.5 0.0 copy-start
  391.5 2.2 copy-done
  393.7 70.6 %shard_map.87 = bf16[1,512,256]{2,1,0:T(8,128)(2,1)S(1)} custom-call(bf16[1,512,4096]{2,1,0:T(8,128)(2,1)S(1)} %copy-done), custom_call_target="tpu_custom_call" | custom-call | tf_op jit(solution)/shard_map/pallas_call | solution.py:107
  464.4 33.2 %reduce-scatter.2.cloned.1.call-done = f32[512,256]{1,0:T(8,128)} async-done(((f32[512,4096]{1,0:T(8,128)}), f32[512,256]{1,0:T(8,128)}) %reduce-scatter.2.cloned.1.call-update) | async-done | bytes 524304 | tf_op jit(solution)/shard_map/reduce_scatter | solution.py:142
  497.6 1.8 convert_element_type.40
  499.4 0.7 copy.10
Async XLA Ops:
  7.2 284.3 %all-gather.3.cloned.1.call-start = ((), (), s32[]{:S(2)}) async-start(), calls=%async_computation.1 | async-start | bytes 4456448 | tf_op jit(solution)/shard_map/all_gather | solution.py:125
  7.9 323.9 %all-gather.5.cloned.1.call-start = ((), (), s32[]{:S(2)}) async-start(), calls=%async_computation.2 | async-start | bytes 8257536 | tf_op jit(solution)/shard_map/all_gather | solution.py:126
  8.6 488.9 %reduce-scatter.2.cloned.1.call-start = ((), (), s32[]{:S(2)}) async-start(), calls=%async_computation.3 | async-start | bytes 8912896 | tf_op jit(solution)/shard_map/reduce_scatter | solution.py:142
  391.5 2.2 copy-start
Sparse Core Ops, SparseCore 0:
  10.3 75.1 all-gather.2
  87.1 244.5 all-gather.4
  350.2 147.3 reduce-scatter.1

commit v5 on v3

--- a/solution.py
+++ b/solution.py
@@ -52,7 +52,7 @@
         c.wait()
 
 
-def gather_weights(g, u, dn, ndp):
+def gather_weights_direct(g, u, dn, ndp):
     n_copies = 3 * (ndp - 1)
     any_spec = pl.BlockSpec(memory_space=pl.ANY)
     out_shape = (
@@ -74,6 +74,98 @@
     )(g, u, dn)
 
 
+def relay_gather_kernel(g_ref, u_ref, dn_ref, gf_ref, uf_ref, df_ref, send_sem, recv_sem,
+                        local_sem):
+    ndp = 8
+    d = lax.axis_index("dp")
+    m = lax.axis_index("mp")
+    lo = d % 2
+    partner = d - lo + (1 - lo)
+    nxt = (d + 2) % ndp
+    prv = (d + ndp - 2) % ndp
+    far = (d + 4) % ndp
+    owns = (g_ref, u_ref, dn_ref)
+    fulls = (gf_ref, uf_ref, df_ref)
+
+    def slot(w, idx, half=None):
+        if w < 2:
+            kr = owns[w].shape[0]
+            if half is None:
+                return fulls[w].at[pl.ds(pl.multiple_of(idx * kr, kr), kr)]
+            hk = kr // 2
+            return fulls[w].at[pl.ds(pl.multiple_of(idx * kr + half * hk, hk), hk)]
+        rr, dc = owns[w].shape
+        cols = pl.ds(pl.multiple_of(idx * dc, dc), dc)
+        if half is None:
+            return fulls[w].at[:, cols]
+        hr = rr // 2
+        return fulls[w].at[pl.ds(half * hr, hr), cols]
+
+    def rc(w, k, src, dst, target):
+        i = w * 8 + k
+        return pltpu.make_async_remote_copy(
+            src_ref=src, dst_ref=dst, send_sem=send_sem.at[i], recv_sem=recv_sem.at[i],
+            device_id=(target, m), device_id_type=MESH)
+
+    locals_ = [pltpu.make_async_copy(owns[w], slot(w, d), local_sem.at[w]) for w in range(3)]
+    c = {}
+    for w in range(3):
+        c[w, 0] = rc(w, 0, owns[w], slot(w, d), partner)
+        c[w, 1] = rc(w, 1, owns[w], slot(w, d), nxt)
+        c[w, 2] = rc(w, 2, owns[w], slot(w, d), prv)
+        c[w, 3] = rc(w, 3, slot(w, partner), slot(w, partner), nxt)
+        c[w, 4] = rc(w, 4, slot(w, partner), slot(w, partner), prv)
+        c[w, 5] = rc(w, 5, slot(w, prv, 0), slot(w, prv, 0), nxt)
+        c[w, 6] = rc(w, 6, slot(w, nxt, 1), slot(w, nxt, 1), prv)
+        c[w, 7] = rc(w, 7, slot(w, far), slot(w, far), partner)
+    for w in range(3):
+        locals_[w].start()
+        for k in range(3):
+            c[w, k].start()
+    for w in range(3):
+        c[w, 0].wait_recv()
+        c[w, 3].start()
+        c[w, 4].start()
+        c[w, 1].wait_recv()
+        c[w, 5].start()
+        c[w, 2].wait_recv()
+        c[w, 6].start()
+    for w in range(3):
+        c[w, 5].wait_recv()
+        c[w, 6].wait_recv()
+        c[w, 7].start()
+    for w in range(3):
+        for k in (3, 4, 7):
+            c[w, k].wait_recv()
+    for w in range(3):
+        for k in range(8):
+            c[w, k].wait_send()
+        locals_[w].wait()
+
+
+def gather_weights(g, u, dn, ndp):
+    if ndp != 8:
+        return gather_weights_direct(g, u, dn, ndp)
+    any_spec = pl.BlockSpec(memory_space=pl.ANY)
+    out_shape = (
+        jax.ShapeDtypeStruct((g.shape[0] * ndp, g.shape[1]), g.dtype),
+        jax.ShapeDtypeStruct((u.shape[0] * ndp, u.shape[1]), u.dtype),
+        jax.ShapeDtypeStruct((dn.shape[0], dn.shape[1] * ndp), dn.dtype),
+    )
+    return pl.pallas_call(
+        relay_gather_kernel,
+        out_shape=out_shape,
+        in_specs=[any_spec] * 3,
+        out_specs=[any_spec] * 3,
+        scratch_shapes=[
+            pltpu.SemaphoreType.DMA((24,)),
+            pltpu.SemaphoreType.DMA((24,)),
+            pltpu.SemaphoreType.DMA((3,)),
+        ],
+        compiler_params=pltpu.CompilerParams(has_side_effects=True),
+    )(g, u, dn)
+
+
 def reduce_kernel(nmp, t_ref, o_ref, buf, send_sem, recv_sem, local_sem):
     d = lax.axis_index("dp")
     m = lax.axis_index("mp")

time: 456 us -> 375 us (0.82)
  Pallas kernels: 335 us -> 254 us
    pallas_call x1, Pallas kernels: 265 us -> 184 us  [gather_weights(): pl.pallas_call(relay_gather_kernel, out_shape=out_shape, in_specs=[any_sp...]
  transfers between devices with their start and end apart: 2 -> 2, of which waited for: 1 -> 1; matrix products, arithmetic and copies ran while one was open for 9% -> 11% of each run, Pallas kernels for 74% -> 68%
where the time goes in v5:
time: 375 us; the launch traced here: 374 us
  Pallas kernels  254 us (68%)
  matrix products  68.1 us (18%)
  waiting for transfers between devices  33.7 us (9%)
  between operations  14.1 us (4%)
    pallas_call x1, Pallas kernels, gather_weights(): pl.pallas_call(relay_gather_kernel, out_shape=out_shape, in_specs=[any_sp...  184 us
    pallas_call x1, Pallas kernels, reduce_scatter(): pl.pallas_call(functools.partial(reduce_kernel, nmp), out_shape=jax.Shape...  70.1 us
    reduce_scatter x1, waiting for transfers between devices, local(): lax.psum_scatter(online_part, 'mp', scatter_dimension=1, tiled=True)  32.9 us
    dot_general x1, matrix products, local(): jnp.dot(inner_t, target_down, preferred_element_type=jnp.float32)  30.9 us
    dot_general x1, matrix products, local(): jnp.dot(inner_o, down_full, preferred_element_type=jnp.float32)  18.3 us
    dot_general x1, matrix products, pair(): t = jnp.dot(features_all, target_piece, preferred_element_type=jnp.float32)  10.6 us
    dot_general x1, matrix products, pair(): o = jnp.dot(features_all, piece, preferred_element_type=jnp.float32)  8.32 us
  transfers between devices with their start and end apart: 2, of which 1 were waited for; matrix products, arithmetic and copies ran while one was open for 11% of the time, Pallas kernels for 68%

profile of v5, /device:TPU:1, one launch (start us, length us, event | category | flops | bytes accessed | tf_op | source)
XLA Modules:
  0.0 374.4 jit_solution(9800972700017665597)
XLA Ops:
  7.2 0.0 all-gather.2.cloned.1.call-start
  7.2 0.7 all-gather.2.cloned.1.call-update
  7.9 0.0 reduce-scatter.2.cloned.1.call-start
  7.9 183.8 %shard_map.86 = (bf16[4096,896]{1,0:T(8,128)(2,1)}, bf16[4096,896]{1,0:T(8,128)(2,1)}, bf16[896,4096]{1,0:T(8,128)(2,1)}) custom-call(bf16[512,896]{1,0:T(8,128)(2,1)} %g_ref.1, bf16[512,896]{1,0:T(8,128)(2,1)} %u_ref.1, bf16[896,512]{1,0:T(8,128)(2,1)} %dn_ref.1), custom_call_target="tpu_custom_call" | custom-call | tf_op jit(solution)/shard_map/pallas_call | solution.py:155
  191.8 0.0 all-gather.2.cloned.1.call-done
  191.8 8.3 %fusion.28 = f32[896,512]{1,0:T(8,128)S(1)} fusion(bf16[4096,896]{1,0:T(8,128)(2,1)} %get-tuple-element.5, bf16[512,4096]{1,0:T(8,128)(2,1)} %all-gather.2.cloned.1.call-done), kind=kOutput, calls=%fused_computation.37 | convolution fusion | flops 3758096384 | bytes 13369344 | tf_op jit(solution)/shard_map/dot_general | solution.py:228
  200.1 18.3 %fusion.19 = f32[512,4096]{1,0:T(8,128)} fusion(bf16[896,4096]{1,0:T(8,128)(2,1)} %get-tuple-element.7, f32[896,512]{1,0:T(8,128)S(1)} %fusion.28, bf16[4096,896]{1,0:T(8,128)(2,1)} %get-tuple-element.6, bf16[512,4096]{1,0:T(8,128)(2,1)} %all-gather.2.cloned.1.call-done), kind=kOutput, calls=%fused_computation.28 | convolution fusion | flops 7518945280 | bytes 29097984 | tf_op jit(solution)/shard_map/dot_general | solution.py:237
  218.4 0.0 reduce-scatter.2.cloned.1.call-update
  218.4 10.6 %fusion = f32[896,512]{1,0:T(8,128)S(1)} fusion(bf16[512,4096]{1,0:T(8,128)(2,1)} %all-gather.2.cloned.1.call-done, bf16[4096,896]{1,0:T(8,128)(2,1)} %param.11, bf16[4096,896]{1,0:T(8,128)(2,1)} %get-tuple-element.5), kind=kOutput, calls=%fused_computation.3 | convolution fusion | flops 3780116480 | bytes 20709376 | tf_op jit(solution)/shard_map/dot_general | solution.py:229
  229.0 30.9 %fusion.10.t_ref = bf16[1,512,4096]{2,1,0:T(8,128)(2,1)} fusion(bf16[896,4096]{1,0:T(8,128)(2,1)} %param.13, bf16[896,4096]{1,0:T(8,128)(2,1)} %get-tuple-element.7, f32[896,512]{1,0:T(8,128)S(1)} %fusion, bf16[512,4096]{1,0:T(8,128)(2,1)} %all-gather.2.cloned.1.call-done, bf16[4096,896]{1,0:T(8,128)(2,1)} %param.12, bf16[4096,896]{1,0:T(8,128)(2,1)} %get-tuple-element.6), kind=kOutput, calls=%fused_computation.13 | convolution fusion | flops 7565082624 | bytes 39583744 | tf_op jit(solution)/shard_map/dot_general | solution.py:238
  259.9 0.0 copy-start
  259.9 2.2 copy-done
  262.1 70.1 %shard_map.87 = bf16[1,512,256]{2,1,0:T(8,128)(2,1)S(1)} custom-call(bf16[1,512,4096]{2,1,0:T(8,128)(2,1)S(1)} %copy-done), custom_call_target="tpu_custom_call" | custom-call | tf_op jit(solution)/shard_map/pallas_call | solution.py:205
  332.2 32.9 %reduce-scatter.2.cloned.1.call-done = f32[512,256]{1,0:T(8,128)} async-done(((f32[512,4096]{1,0:T(8,128)}), f32[512,256]{1,0:T(8,128)}) %reduce-scatter.2.cloned.1.call-update) | async-done | bytes 524304 | tf_op jit(solution)/shard_map/reduce_scatter | solution.py:239
  365.1 1.8 convert_element_type.40
  366.9 0.7 copy.10
Async XLA Ops:
  7.2 184.6 %all-gather.2.cloned.1.call-start = ((), (), s32[]{:S(2)}) async-start(), calls=%async_computation.1 | async-start | bytes 4456448 | tf_op jit(solution)/shard_map/all_gather | solution.py:223
  7.9 357.2 %reduce-scatter.2.cloned.1.call-start = ((), (), s32[]{:S(2)}) async-start(), calls=%async_computation.2 | async-start | bytes 8912896 | tf_op jit(solution)/shard_map/reduce_scatter | solution.py:239
  259.9 2.2 copy-start
Sparse Core Ops, SparseCore 0:
  10.3 75.1 all-gather.1
  218.5 146.5 reduce-scatter.1

commit v6 on v5

--- a/solution.py
+++ b/solution.py
@@ -218,6 +218,105 @@
     )(terms)
 
 
+def hier_reduce_kernel(t_ref, o_ref, own, r1, sb2, r2, s2, sb3, r3,
+                       ls, ss1, rs1, ss2, rs2, ss3, rs3):
+    d = lax.axis_index("dp")
+    m = lax.axis_index("mp")
+    c = m % 2
+    z = (m // 2) % 4
+    xh = m // 8
+    w = o_ref.shape[2]
+    rows = 32
+    nchunk = o_ref.shape[1] // rows
+
+    def blk(b):
+        return t_ref.at[:, :, pl.ds(pl.multiple_of(b * w, w), w)]
+
+    def dev(mm):
+        return (d, mm)
+
+    locs = []
+    st1 = []
+    for j in range(8):
+        bx, bz = j // 4, j % 4
+        locs.append(pltpu.make_async_copy(blk(bx * 8 + bz * 2 + c), own.at[j], ls.at[j]))
+        st1.append(pltpu.make_async_remote_copy(
+            src_ref=blk(bx * 8 + bz * 2 + (1 - c)), dst_ref=r1.at[j], send_sem=ss1.at[j],
+            recv_sem=rs1.at[j], device_id=dev(m + 1 - 2 * c), device_id_type=MESH))
+    for j in range(8):
+        st1[j].start()
+        locs[j].start()
+    for j in range(8):
+        locs[j].wait()
+        st1[j].wait()
+
+    st2 = []
+    for s in range(1, 4):
+        zt = (z + s) % 4
+
+        def fill(i, carry, s=s, zt=zt):
+            r = pl.ds(pl.multiple_of(i * rows, rows), rows)
+            for bx in range(2):
+                idx = bx * 4 + zt
+                sb2[s - 1, bx, :, r, :] = (own[idx, :, r, :].astype(jnp.float32)
+                                           + r1[idx, :, r, :].astype(jnp.float32)
+                                           ).astype(sb2.dtype)
+            return carry
+
+        lax.fori_loop(0, nchunk, fill, 0)
+        cp = pltpu.make_async_remote_copy(
+            src_ref=sb2.at[s - 1], dst_ref=r2.at[s - 1], send_sem=ss2.at[s - 1],
+            recv_sem=rs2.at[s - 1], device_id=dev(xh * 8 + zt * 2 + c), device_id_type=MESH)
+        cp.start()
+        st2.append(cp)
+    for cp in st2:
+        cp.wait()
+
+    def sum2(i, carry):
+        r = pl.ds(pl.multiple_of(i * rows, rows), rows)
+        for bx in range(2):
+            idx = bx * 4 + z
+            acc = own[idx, :, r, :].astype(jnp.float32) + r1[idx, :, r, :].astype(jnp.float32)
+            for k in range(3):
+                acc = acc + r2[k, bx, :, r, :].astype(jnp.float32)
+            s2[bx, :, r, :] = acc
+        return carry
+
+    lax.fori_loop(0, nchunk, sum2, 0)
+    sb3[...] = s2[1 - xh].astype(sb3.dtype)
+    cp3 = pltpu.make_async_remote_copy(
+        src_ref=sb3, dst_ref=r3, send_sem=ss3.at[0], recv_sem=rs3.at[0],
+        device_id=dev(m + 8 - 16 * xh), device_id_type=MESH)
+    cp3.start()
+    cp3.wait()
+    o_ref[...] = (s2[xh] + r3[...].astype(jnp.float32)).astype(o_ref.dtype)
+
+
+def hier_reduce_scatter(terms):
+    n, t, width = terms.shape
+    w = width // 16
+    bf = jnp.bfloat16
+    dma = pltpu.SemaphoreType.DMA
+    return pl.pallas_call(
+        hier_reduce_kernel,
+        out_shape=jax.ShapeDtypeStruct((n, t, w), bf),
+        in_specs=[pl.BlockSpec(memory_space=pl.ANY)],
+        out_specs=pl.BlockSpec(memory_space=pltpu.VMEM),
+        scratch_shapes=[
+            pltpu.VMEM((8, n, t, w), bf),
+            pltpu.VMEM((8, n, t, w), bf),
+            pltpu.VMEM((3, 2, n, t, w), bf),
+            pltpu.VMEM((3, 2, n, t, w), bf),
+            pltpu.VMEM((2, n, t, w), jnp.float32),
+            pltpu.VMEM((n, t, w), bf),
+            pltpu.VMEM((n, t, w), bf),
+            dma((8,)), dma((8,)), dma((8,)), dma((3,)), dma((3,)), dma((1,)), dma((1,)),
+        ],
+        compiler_params=pltpu.CompilerParams(has_side_effects=True,
+                                             vmem_limit_bytes=56 * 1024 * 1024),
+    )(terms)
+
+
 def local(ndp, nmp, hidden_states, gate_online, up_online, down_online, gate_previous,
           up_previous, down_previous):
     features_all = lax.all_gather(hidden_states, "mp", axis=1, tiled=True)
@@ -236,9 +335,12 @@
     target_down = blend(down_full, down_previous)
     online_part = jnp.dot(inner_o, down_full, preferred_element_type=jnp.float32)
     target_part = jnp.dot(inner_t, target_down, preferred_element_type=jnp.float32)
-    online_out = lax.psum_scatter(online_part, "mp", scatter_dimension=1, tiled=True)
-    target_out = reduce_scatter(target_part.astype(jnp.bfloat16)[None], nmp)
-    return (online_out.astype(jnp.bfloat16), target_out[0])
+    terms = jnp.stack([online_part, target_part], axis=0).astype(jnp.bfloat16)
+    if nmp == 16:
+        result = hier_reduce_scatter(terms)
+    else:
+        result = reduce_scatter(terms, nmp)
+    return (result[0], result[1])
 
 
 def solution(mesh):

time: 375 us -> 350 us (0.933)
  waiting for transfers between devices: 33.7 us -> 0.7 us
  Pallas kernels: 254 us -> 265 us
  matrix products: 68.1 us -> 60.8 us
  other arithmetic: 1.77 us -> 7.45 us
    reduce_scatter x1 -> x0, waiting for transfers between devices: 32.9 us -> none  [local(): lax.psum_scatter(online_part, 'mp', scatter_dimension=1, tiled=True)]
    pallas_call x1, Pallas kernels: 70.1 us -> 81 us  [hier_reduce_scatter(): pl.pallas_call(hier_reduce_kernel, out_shape=jax.ShapeDtypeStruct((n, t,...]
    another operation x0 -> x1, other arithmetic: none -> 7.45 us  [local(): terms = jnp.stack([online_part, target_part], axis=0).astype(jnp.bfloat16)]
    dot_general x1, matrix products: 10.6 us -> 5.39 us  [pair(): t = jnp.dot(features_all, target_piece, preferred_element_type=jnp.float32)]
  transfers between devices with their start and end apart: 2 -> 1, of which waited for: 1 -> 0; matrix products, arithmetic and copies ran while one was open for 11% -> 0% of each run, Pallas kernels for 68% -> 53%
where the time goes in v6:
time: 350 us
  Pallas kernels  265 us (76%)
  matrix products  60.8 us (17%)
  between operations  14.1 us (4%)
  other arithmetic  7.45 us (2%)
    pallas_call x1, Pallas kernels, gather_weights(): pl.pallas_call(relay_gather_kernel, out_shape=out_shape, in_specs=[any_sp...  184 us
    pallas_call x1, Pallas kernels, hier_reduce_scatter(): pl.pallas_call(hier_reduce_kernel, out_shape=jax.ShapeDtypeStruct((n, t,...  81 us
    dot_general x1, matrix products, local(): jnp.dot(inner_t, target_down, preferred_element_type=jnp.float32)  27.8 us
    dot_general x1, matrix products, local(): jnp.dot(inner_o, down_full, preferred_element_type=jnp.float32)  17.9 us
    dot_general x1, matrix products, pair(): o = jnp.dot(features_all, piece, preferred_element_type=jnp.float32)  9.66 us
    another operation x1, other arithmetic, local(): terms = jnp.stack([online_part, target_part], axis=0).astype(jnp.bfloat16)  7.45 us
  transfers between devices with their start and end apart: 1, of which 0 were waited for; matrix products, arithmetic and copies ran while one was open for 0% of the time, Pallas kernels for 53%

profile of v6, /device:TPU:1, one launch (start us, length us, event | category | flops | bytes accessed | tf_op | source)
XLA Modules:
  0.0 349.7 jit_solution(15666514141820884343)
XLA Ops:
  7.2 0.0 all-gather.2.cloned.1.call-start
  7.2 0.7 all-gather.2.cloned.1.call-update
  7.9 0.0 slice-start
  7.9 183.8 %shard_map.86 = (bf16[4096,896]{1,0:T(8,128)(2,1)}, bf16[4096,896]{1,0:T(8,128)(2,1)}, bf16[896,4096]{1,0:T(8,128)(2,1)}) custom-call(bf16[512,896]{1,0:T(8,128)(2,1)} %g_ref.1, bf16[512,896]{1,0:T(8,128)(2,1)} %u_ref.1, bf16[896,512]{1,0:T(8,128)(2,1)} %dn_ref.1), custom_call_target="tpu_custom_call" | custom-call | tf_op jit(solution)/shard_map/pallas_call | solution.py:155
  191.7 0.0 all-gather.2.cloned.1.call-done
  191.7 0.0 slice-start.1
  191.8 0.0 copy-start
  191.8 0.0 copy-start.1
  191.8 9.7 %fusion.28 = f32[896,512]{1,0:T(8,128)} fusion(bf16[4096,896]{1,0:T(8,128)(2,1)} %get-tuple-element.5, bf16[512,4096]{1,0:T(8,128)(2,1)} %all-gather.2.cloned.1.call-done), kind=kOutput, calls=%fused_computation.41 | convolution fusion | flops 3758096384 | bytes 13369344 | tf_op jit(solution)/shard_map/dot_general | solution.py:327
  201.4 0.0 slice-done
  201.4 0.0 slice-done.1
  201.4 0.0 copy-done
  201.4 0.0 copy-done.1
  201.5 5.4 %fusion = f32[896,512]{1,0:T(8,128)} fusion(bf16[512,4096]{1,0:T(8,128)(2,1)S(1)} %copy-done.1, bf16[4096,896]{1,0:T(8,128)(2,1)S(1)} %bitcast.67, bf16[4096,896]{1,0:T(8,128)(2,1)S(1)} %copy-done), kind=kOutput, calls=%fused_computation.4 | convolution fusion | flops 3780116480 | bytes 20709376 | tf_op jit(solution)/shard_map/dot_general | solution.py:328
  206.9 0.0 copy-start.2
  206.9 17.9 %fusion.10 = bf16[1,512,4096]{2,1,0:T(8,128)(2,1)} fusion(bf16[896,4096]{1,0:T(8,128)(2,1)} %get-tuple-element.7, f32[896,512]{1,0:T(8,128)} %fusion.28, bf16[4096,896]{1,0:T(8,128)(2,1)} %get-tuple-element.6, bf16[512,4096]{1,0:T(8,128)(2,1)} %all-gather.2.cloned.1.call-done), kind=kOutput, calls=%fused_computation.15 | convolution fusion | flops 7521042432 | bytes 24903680 | tf_op jit(solution)/shard_map/dot_general | solution.py:336
  224.8 0.0 copy-done.2
  224.8 27.8 %fusion.11 = bf16[1,512,4096]{2,1,0:T(8,128)(2,1)} fusion(bf16[896,4096]{1,0:T(8,128)(2,1)} %param.13, bf16[896,4096]{1,0:T(8,128)(2,1)} %get-tuple-element.7, f32[896,512]{1,0:T(8,128)S(1)} %copy-done.2, bf16[512,4096]{1,0:T(8,128)(2,1)} %all-gather.2.cloned.1.call-done, bf16[4096,896]{1,0:T(8,128)(2,1)} %param.12, bf16[4096,896]{1,0:T(8,128)(2,1)} %get-tuple-element.6), kind=kOutput, calls=%fused_computation.16 | convolution fusion | flops 7565082624 | bytes 39583744 | tf_op jit(solution)/shard_map/dot_general | solution.py:337
  252.6 7.4 %pad_maximum_fusion.t_ref = bf16[2,512,4096]{2,1,0:T(8,128)(2,1)} fusion(bf16[1,512,4096]{2,1,0:T(8,128)(2,1)} %fusion.11, bf16[1,512,4096]{2,1,0:T(8,128)(2,1)} %fusion.10), kind=kLoop, calls=%fused_computation.3 | loop fusion | flops 4194304 | bytes 16777216 | tf_op jit(solution)/shard_map/stack | solution.py:338
  260.1 81.0 %shard_map.87 = bf16[2,512,256]{2,1,0:T(8,128)(2,1)} custom-call(bf16[2,512,4096]{2,1,0:T(8,128)(2,1)} %pad_maximum_fusion.t_ref), custom_call_target="tpu_custom_call" | custom-call | tf_op jit(solution)/shard_map/pallas_call | solution.py:300
  341.0 1.9 slice_bitcast_fusion
  (1 shorter events, 0.0 us)
Async XLA Ops:
  7.2 184.6 %all-gather.2.cloned.1.call-start = ((), (), s32[]{:S(2)}) async-start(), calls=%async_computation | async-start | bytes 4456448 | tf_op jit(solution)/shard_map/all_gather | solution.py:322
  7.9 193.5 %slice-start = ((s8[7340032]{0:T(1024)(128)(4,1)}), s8[3145728]{0:T(1024)(128)(4,1)S(1)}, s32[]{:S(2)}) async-start(s8[7340032]{0:T(1024)(128)(4,1)} %bitcast.66), calls=%async_computation.1 | async-start | bytes 6291456
  191.7 9.7 %slice-start.1 = ((s8[7340032]{0:T(1024)(128)(4,1)}), s8[4194304]{0:T(1024)(128)(4,1)S(1)}, s32[]{:S(2)}) async-start(s8[7340032]{0:T(1024)(128)(4,1)} %bitcast.66), calls=%async_computation.2 | async-start | bytes 8388608
  191.8 9.7 %copy-start = (bf16[4096,896]{1,0:T(8,128)(2,1)S(1)}, bf16[4096,896]{1,0:T(8,128)(2,1)}, u32[]{:S(2)}) copy-start(bf16[4096,896]{1,0:T(8,128)(2,1)} %get-tuple-element.5) | copy-start | bytes 22020100
  191.8 9.7 %copy-start.1 = (bf16[512,4096]{1,0:T(8,128)(2,1)S(1)}, bf16[512,4096]{1,0:T(8,128)(2,1)}, u32[]{:S(2)}) copy-start(bf16[512,4096]{1,0:T(8,128)(2,1)} %all-gather.2.cloned.1.call-done) | copy-start | bytes 12582916
  206.9 17.9 %copy-start.2 = (f32[896,512]{1,0:T(8,128)S(1)}, f32[896,512]{1,0:T(8,128)}, u32[]{:S(2)}) copy-start(f32[896,512]{1,0:T(8,128)} %fusion) | copy-start | bytes 5505028
Sparse Core Ops, SparseCore 0:
  10.3 75.1 all-gather.1

commit v7 on v6

--- a/solution.py
+++ b/solution.py
@@ -218,7 +218,7 @@
     )(terms)
 
 
-def hier_reduce_kernel(t_ref, o_ref, own, r1, sb2, r2, s2, sb3, r3,
+def hier_reduce_kernel(ta_ref, tb_ref, o_ref, own, r1, sb2, r2, s2, sb3, r3,
                        ls, ss1, rs1, ss2, rs2, ss3, rs3):
     d = lax.axis_index("dp")
     m = lax.axis_index("mp")
@@ -229,24 +229,26 @@
     rows = 32
     nchunk = o_ref.shape[1] // rows
 
-    def blk(b):
-        return t_ref.at[:, :, pl.ds(pl.multiple_of(b * w, w), w)]
+    def blk(b, k):
+        return (ta_ref, tb_ref)[k].at[:, pl.ds(pl.multiple_of(b * w, w), w)]
 
     def dev(mm):
         return (d, mm)
 
     locs = []
     st1 = []
-    for j in range(8):
-        bx, bz = j // 4, j % 4
-        locs.append(pltpu.make_async_copy(blk(bx * 8 + bz * 2 + c), own.at[j], ls.at[j]))
+    for j in range(16):
+        bx, bz, k = j // 8, (j // 2) % 4, j % 2
+        jj = bx * 4 + bz
+        locs.append(pltpu.make_async_copy(blk(bx * 8 + bz * 2 + c, k), own.at[jj, k],
+                                          ls.at[j]))
         st1.append(pltpu.make_async_remote_copy(
-            src_ref=blk(bx * 8 + bz * 2 + (1 - c)), dst_ref=r1.at[j], send_sem=ss1.at[j],
+            src_ref=blk(bx * 8 + bz * 2 + (1 - c), k), dst_ref=r1.at[jj, k], send_sem=ss1.at[j],
             recv_sem=rs1.at[j], device_id=dev(m + 1 - 2 * c), device_id_type=MESH))
-    for j in range(8):
+    for j in range(16):
         st1[j].start()
         locs[j].start()
-    for j in range(8):
+    for j in range(16):
         locs[j].wait()
         st1[j].wait()
 
@@ -292,15 +294,16 @@
     o_ref[...] = (s2[xh] + r3[...].astype(jnp.float32)).astype(o_ref.dtype)
 
 
-def hier_reduce_scatter(terms):
-    n, t, width = terms.shape
+def hier_reduce_scatter(ta, tb):
+    n = 2
+    t, width = ta.shape
     w = width // 16
     bf = jnp.bfloat16
     dma = pltpu.SemaphoreType.DMA
     return pl.pallas_call(
         hier_reduce_kernel,
         out_shape=jax.ShapeDtypeStruct((n, t, w), bf),
-        in_specs=[pl.BlockSpec(memory_space=pl.ANY)],
+        in_specs=[pl.BlockSpec(memory_space=pl.ANY)] * 2,
         out_specs=pl.BlockSpec(memory_space=pltpu.VMEM),
         scratch_shapes=[
             pltpu.VMEM((8, n, t, w), bf),
@@ -310,11 +313,11 @@
             pltpu.VMEM((2, n, t, w), jnp.float32),
             pltpu.VMEM((n, t, w), bf),
             pltpu.VMEM((n, t, w), bf),
-            dma((8,)), dma((8,)), dma((8,)), dma((3,)), dma((3,)), dma((1,)), dma((1,)),
+            dma((16,)), dma((16,)), dma((16,)), dma((3,)), dma((3,)), dma((1,)), dma((1,)),
         ],
         compiler_params=pltpu.CompilerParams(has_side_effects=True,
                                              vmem_limit_bytes=56 * 1024 * 1024),
-    )(terms)
+    )(ta, tb)
 
 
 def local(ndp, nmp, hidden_states, gate_online, up_online, down_online, gate_previous,
@@ -335,10 +338,11 @@
     target_down = blend(down_full, down_previous)
     online_part = jnp.dot(inner_o, down_full, preferred_element_type=jnp.float32)
     target_part = jnp.dot(inner_t, target_down, preferred_element_type=jnp.float32)
-    terms = jnp.stack([online_part, target_part], axis=0).astype(jnp.bfloat16)
     if nmp == 16:
-        result = hier_reduce_scatter(terms)
+        result = hier_reduce_scatter(online_part.astype(jnp.bfloat16),
+                                     target_part.astype(jnp.bfloat16))
     else:
+        terms = jnp.stack([online_part, target_part], axis=0).astype(jnp.bfloat16)
         result = reduce_scatter(terms, nmp)
     return (result[0], result[1])
 

time: 350 us -> 343 us (0.980)
  other arithmetic: 7.45 us -> 0.01 us
    another operation x1 -> x0, other arithmetic: 7.45 us -> none  [local(): terms = jnp.stack([online_part, target_part], axis=0).astype(jnp.bfloat16)]
  transfers between devices with their start and end apart: 1 -> 1, of which waited for: 0 -> 0; matrix products, arithmetic and copies ran while one was open for 0% -> 0% of each run, Pallas kernels for 53% -> 54%
where the time goes in v7:
time: 343 us; the launch traced here: 342 us
  Pallas kernels  265 us (77%)
  matrix products  60.8 us (18%)
  between operations  14.1 us (4%)
    pallas_call x1, Pallas kernels, gather_weights(): pl.pallas_call(relay_gather_kernel, out_shape=out_shape, in_specs=[any_sp...  184 us
    pallas_call x1, Pallas kernels, hier_reduce_scatter(): pl.pallas_call(hier_reduce_kernel, out_shape=jax.ShapeDtypeStruct((n, t,...  81.1 us
    dot_general x1, matrix products, local(): jnp.dot(inner_t, target_down, preferred_element_type=jnp.float32)  27.8 us
    dot_general x1, matrix products, local(): jnp.dot(inner_o, down_full, preferred_element_type=jnp.float32)  17.9 us
    dot_general x1, matrix products, pair(): o = jnp.dot(features_all, piece, preferred_element_type=jnp.float32)  9.66 us
  transfers between devices with their start and end apart: 1, of which 0 were waited for; matrix products, arithmetic and copies ran while one was open for 0% of the time, Pallas kernels for 54%

profile of v7, /device:TPU:1, one launch (start us, length us, event | category | flops | bytes accessed | tf_op | source)
XLA Modules:
  0.0 342.5 jit_solution(9975496391446744351)
XLA Ops:
  7.2 0.0 all-gather.2.cloned.1.call-start
  7.2 0.7 all-gather.2.cloned.1.call-update
  7.9 0.0 slice-start
  7.9 183.8 %shard_map.86 = (bf16[4096,896]{1,0:T(8,128)(2,1)}, bf16[4096,896]{1,0:T(8,128)(2,1)}, bf16[896,4096]{1,0:T(8,128)(2,1)}) custom-call(bf16[512,896]{1,0:T(8,128)(2,1)} %g_ref.1, bf16[512,896]{1,0:T(8,128)(2,1)} %u_ref.1, bf16[896,512]{1,0:T(8,128)(2,1)} %dn_ref.1), custom_call_target="tpu_custom_call" | custom-call | tf_op jit(solution)/shard_map/pallas_call | solution.py:155
  191.7 0.0 all-gather.2.cloned.1.call-done
  191.7 0.0 slice-start.1
  191.8 0.0 copy-start
  191.8 0.0 copy-start.1
  191.8 9.7 %fusion.27 = f32[896,512]{1,0:T(8,128)} fusion(bf16[4096,896]{1,0:T(8,128)(2,1)} %get-tuple-element.5, bf16[512,4096]{1,0:T(8,128)(2,1)} %all-gather.2.cloned.1.call-done), kind=kOutput, calls=%fused_computation.37 | convolution fusion | flops 3758096384 | bytes 13369344 | tf_op jit(solution)/shard_map/dot_general | solution.py:330
  201.4 0.0 slice-done
  201.4 0.0 slice-done.1
  201.4 0.0 copy-done
  201.4 0.0 copy-done.1
  201.5 5.4 %fusion = f32[896,512]{1,0:T(8,128)} fusion(bf16[512,4096]{1,0:T(8,128)(2,1)S(1)} %copy-done.1, bf16[4096,896]{1,0:T(8,128)(2,1)S(1)} %bitcast.54, bf16[4096,896]{1,0:T(8,128)(2,1)S(1)} %copy-done), kind=kOutput, calls=%fused_computation.3 | convolution fusion | flops 3780116480 | bytes 20709376 | tf_op jit(solution)/shard_map/dot_general | solution.py:331
  206.9 0.0 copy-start.2
  206.9 17.9 %convolution_convert_fusion.ta_ref = bf16[512,4096]{1,0:T(8,128)(2,1)} fusion(bf16[896,4096]{1,0:T(8,128)(2,1)} %get-tuple-element.7, f32[896,512]{1,0:T(8,128)} %fusion.27, bf16[4096,896]{1,0:T(8,128)(2,1)} %get-tuple-element.6, bf16[512,4096]{1,0:T(8,128)(2,1)} %all-gather.2.cloned.1.call-done), kind=kOutput, calls=%fused_computation.13 | convolution fusion | flops 7521042432 | bytes 24903680 | tf_op jit(solution)/shard_map/dot_general | solution.py:339
  224.8 0.0 copy-done.2
  224.8 27.8 %fusion.9.tb_ref = bf16[512,4096]{1,0:T(8,128)(2,1)} fusion(bf16[896,4096]{1,0:T(8,128)(2,1)} %param.13, bf16[896,4096]{1,0:T(8,128)(2,1)} %get-tuple-element.7, f32[896,512]{1,0:T(8,128)S(1)} %copy-done.2, bf16[512,4096]{1,0:T(8,128)(2,1)} %all-gather.2.cloned.1.call-done, bf16[4096,896]{1,0:T(8,128)(2,1)} %param.12, bf16[4096,896]{1,0:T(8,128)(2,1)} %get-tuple-element.6), kind=kOutput, calls=%fused_computation.12 | convolution fusion | flops 7565082624 | bytes 39583744 | tf_op jit(solution)/shard_map/dot_general | solution.py:340
  252.6 81.1 %shard_map.87 = bf16[2,512,256]{2,1,0:T(8,128)(2,1)} custom-call(bf16[512,4096]{1,0:T(8,128)(2,1)} %convolution_convert_fusion.ta_ref, bf16[512,4096]{1,0:T(8,128)(2,1)} %fusion.9.tb_ref), custom_call_target="tpu_custom_call" | custom-call | tf_op jit(solution)/shard_map/pallas_call | solution.py:303
  333.8 1.9 slice_bitcast_fusion
  (1 shorter events, 0.0 us)
Async XLA Ops:
  7.2 184.6 %all-gather.2.cloned.1.call-start = ((), (), s32[]{:S(2)}) async-start(), calls=%async_computation | async-start | bytes 4456448 | tf_op jit(solution)/shard_map/all_gather | solution.py:325
  7.9 193.5 %slice-start = ((s8[7340032]{0:T(1024)(128)(4,1)}), s8[3145728]{0:T(1024)(128)(4,1)S(1)}, s32[]{:S(2)}) async-start(s8[7340032]{0:T(1024)(128)(4,1)} %bitcast.53), calls=%async_computation.1 | async-start | bytes 6291456
  191.7 9.7 %slice-start.1 = ((s8[7340032]{0:T(1024)(128)(4,1)}), s8[4194304]{0:T(1024)(128)(4,1)S(1)}, s32[]{:S(2)}) async-start(s8[7340032]{0:T(1024)(128)(4,1)} %bitcast.53), calls=%async_computation.2 | async-start | bytes 8388608
  191.8 9.7 %copy-start = (bf16[4096,896]{1,0:T(8,128)(2,1)S(1)}, bf16[4096,896]{1,0:T(8,128)(2,1)}, u32[]{:S(2)}) copy-start(bf16[4096,896]{1,0:T(8,128)(2,1)} %get-tuple-element.5) | copy-start | bytes 22020100
  191.8 9.7 %copy-start.1 = (bf16[512,4096]{1,0:T(8,128)(2,1)S(1)}, bf16[512,4096]{1,0:T(8,128)(2,1)}, u32[]{:S(2)}) copy-start(bf16[512,4096]{1,0:T(8,128)(2,1)} %all-gather.2.cloned.1.call-done) | copy-start | bytes 12582916
  206.9 17.9 %copy-start.2 = (f32[896,512]{1,0:T(8,128)S(1)}, f32[896,512]{1,0:T(8,128)}, u32[]{:S(2)}) copy-start(f32[896,512]{1,0:T(8,128)} %fusion) | copy-start | bytes 5505028
Sparse Core Ops, SparseCore 0:
  10.3 75.1 all-gather.1

commit v8 on v7

--- a/solution.py
+++ b/solution.py
@@ -320,21 +320,203 @@
     )(ta, tb)
 
 
+def fused_gather_kernel(h_ref, g_ref, u_ref, dn_ref, gp_ref, upv_ref,
+                        gf_ref, uf_ref, df_ref, io_ref, it_ref,
+                        hfull, acc, wbuf, tbuf, send_sem, recv_sem, local_sem,
+                        hsend, hrecv, wsem):
+    ndp = 8
+    nmp = 16
+    d = lax.axis_index("dp")
+    m = lax.axis_index("mp")
+    lo = d % 2
+    partner = d - lo + (1 - lo)
+    nxt = (d + 2) % ndp
+    prv = (d + ndp - 2) % ndp
+    far = (d + 4) % ndp
+    owns = (g_ref, u_ref, dn_ref)
+    fulls = (gf_ref, uf_ref, df_ref)
+    kr = g_ref.shape[0]
+    hc = h_ref.shape[1]
+    tokens = h_ref.shape[0]
+
+    def slot(w, idx, half=None):
+        if w < 2:
+            if half is None:
+                return fulls[w].at[pl.ds(pl.multiple_of(idx * kr, kr), kr)]
+            hk = kr // 2
+            return fulls[w].at[pl.ds(pl.multiple_of(idx * kr + half * hk, hk), hk)]
+        rr, dc = owns[w].shape
+        cols = pl.ds(pl.multiple_of(idx * dc, dc), dc)
+        if half is None:
+            return fulls[w].at[:, cols]
+        hr = rr // 2
+        return fulls[w].at[pl.ds(half * hr, hr), cols]
+
+    def rc(w, k, src, dst, target):
+        i = w * 8 + k
+        return pltpu.make_async_remote_copy(
+            src_ref=src, dst_ref=dst, send_sem=send_sem.at[i], recv_sem=recv_sem.at[i],
+            device_id=(target, m), device_id_type=MESH)
+
+    hmine = hfull.at[:, pl.ds(pl.multiple_of(m * hc, hc), hc)]
+    hlocal = pltpu.make_async_copy(h_ref, hmine, local_sem.at[3])
+    hcopies = []
+    for s in range(1, nmp):
+        hcopies.append(pltpu.make_async_remote_copy(
+            src_ref=h_ref, dst_ref=hmine, send_sem=hsend.at[s - 1], recv_sem=hrecv.at[s - 1],
+            device_id=(d, lax.rem(m + s, nmp)), device_id_type=MESH))
+    locals_ = [pltpu.make_async_copy(owns[w], slot(w, d), local_sem.at[w]) for w in range(3)]
+    c = {}
+    for w in range(3):
+        c[w, 0] = rc(w, 0, owns[w], slot(w, d), partner)
+        c[w, 1] = rc(w, 1, owns[w], slot(w, d), nxt)
+        c[w, 2] = rc(w, 2, owns[w], slot(w, d), prv)
+        c[w, 3] = rc(w, 3, slot(w, partner), slot(w, partner), nxt)
+        c[w, 4] = rc(w, 4, slot(w, partner), slot(w, partner), prv)
+        c[w, 5] = rc(w, 5, slot(w, prv, 0), slot(w, prv, 0), nxt)
+        c[w, 6] = rc(w, 6, slot(w, nxt, 1), slot(w, nxt, 1), prv)
+        c[w, 7] = rc(w, 7, slot(w, far), slot(w, far), partner)
+    for w in range(3):
+        locals_[w].start()
+        for k in range(3):
+            c[w, k].start()
+    hlocal.start()
+    for cp in hcopies:
+        cp.start()
+
+    acc[...] = jnp.zeros_like(acc)
+    tile = 128
+    chunk = 64
+
+    def compute_slot(idx):
+        rows = pl.ds(pl.multiple_of(idx * kr, kr), kr)
+        loads = [
+            pltpu.make_async_copy(gf_ref.at[rows], wbuf.at[0], wsem.at[0]),
+            pltpu.make_async_copy(gp_ref.at[rows], wbuf.at[1], wsem.at[1]),
+            pltpu.make_async_copy(uf_ref.at[rows], wbuf.at[2], wsem.at[2]),
+            pltpu.make_async_copy(upv_ref.at[rows], wbuf.at[3], wsem.at[3]),
+        ]
+        for ld in loads:
+            ld.start()
+        for ld in loads:
+            ld.wait()
+
+        def mix(i, carry):
+            r = pl.ds(pl.multiple_of(i * chunk, chunk), chunk)
+            for j in range(2):
+                on = wbuf[2 * j, r, :].astype(jnp.float32)
+                pv = wbuf[2 * j + 1, r, :].astype(jnp.float32)
+                tbuf[j, r, :] = (POLYAK * on + (1.0 - POLYAK) * pv).astype(tbuf.dtype)
+            return carry
+
+        lax.fori_loop(0, kr // chunk, mix, 0)
+        hcols = pl.ds(pl.multiple_of(idx * kr, kr), kr)
+
+        def mm(i, carry):
+            r = pl.ds(pl.multiple_of(i * tile, tile), tile)
+            hs = hfull[r, hcols]
+            f32 = jnp.float32
+            acc[0, r, :] += jnp.dot(hs, wbuf[0], preferred_element_type=f32)
+            acc[1, r, :] += jnp.dot(hs, tbuf[0], preferred_element_type=f32)
+            acc[2, r, :] += jnp.dot(hs, wbuf[2], preferred_element_type=f32)
+            acc[3, r, :] += jnp.dot(hs, tbuf[1], preferred_element_type=f32)
+            return carry
+
+        lax.fori_loop(0, tokens // tile, mm, 0)
+
+    hlocal.wait()
+    for cp in hcopies:
+        cp.wait_recv()
+    for w in range(3):
+        locals_[w].wait()
+    compute_slot(d)
+    for w in range(3):
+        c[w, 0].wait_recv()
+        c[w, 3].start()
+        c[w, 4].start()
+        c[w, 1].wait_recv()
+        c[w, 5].start()
+        c[w, 2].wait_recv()
+        c[w, 6].start()
+    compute_slot(partner)
+    compute_slot(prv)
+    compute_slot(nxt)
+    for w in range(3):
+        c[w, 5].wait_recv()
+        c[w, 6].wait_recv()
+        c[w, 7].start()
+    compute_slot(far)
+    for w in range(3):
+        for k in (3, 4, 7):
+            c[w, k].wait_recv()
+    compute_slot((partner + 2) % ndp)
+    compute_slot((partner + ndp - 2) % ndp)
+    compute_slot((partner + 4) % ndp)
+    for w in range(3):
+        for k in range(8):
+            c[w, k].wait_send()
+    for cp in hcopies:
+        cp.wait_send()
+
+    def finish(i, carry):
+        r = pl.ds(pl.multiple_of(i * chunk, chunk), chunk)
+        io_ref[r, :] = (jax.nn.silu(acc[0, r, :]) * acc[2, r, :]).astype(io_ref.dtype)
+        it_ref[r, :] = (jax.nn.silu(acc[1, r, :]) * acc[3, r, :]).astype(it_ref.dtype)
+        return carry
+
+    lax.fori_loop(0, tokens // chunk, finish, 0)
+
+
+def fused_gather(h, g, u, dn, gp, upv):
+    ndp, nmp = 8, 16
+    any_spec = pl.BlockSpec(memory_space=pl.ANY)
+    tokens, ff = h.shape[0], g.shape[1]
+    bf = jnp.bfloat16
+    dma = pltpu.SemaphoreType.DMA
+    out_shape = (
+        jax.ShapeDtypeStruct((g.shape[0] * ndp, ff), g.dtype),
+        jax.ShapeDtypeStruct((u.shape[0] * ndp, ff), u.dtype),
+        jax.ShapeDtypeStruct((dn.shape[0], dn.shape[1] * ndp), dn.dtype),
+        jax.ShapeDtypeStruct((tokens, ff), bf),
+        jax.ShapeDtypeStruct((tokens, ff), bf),
+    )
+    vspec = pl.BlockSpec(memory_space=pltpu.VMEM)
+    return pl.pallas_call(
+        fused_gather_kernel,
+        out_shape=out_shape,
+        in_specs=[any_spec] * 6,
+        out_specs=[any_spec] * 3 + [vspec] * 2,
+        scratch_shapes=[
+            pltpu.VMEM((tokens, h.shape[1] * nmp), bf),
+            pltpu.VMEM((4, tokens, ff), jnp.float32),
+            pltpu.VMEM((4, g.shape[0], ff), bf),
+            pltpu.VMEM((2, g.shape[0], ff), bf),
+            dma((24,)), dma((24,)), dma((4,)), dma((nmp - 1,)), dma((nmp - 1,)), dma((4,)),
+        ],
+        compiler_params=pltpu.CompilerParams(has_side_effects=True,
+                                             vmem_limit_bytes=56 * 1024 * 1024),
+    )(h, g, u, dn, gp, upv)
+
+
 def local(ndp, nmp, hidden_states, gate_online, up_online, down_online, gate_previous,
           up_previous, down_previous):
-    features_all = lax.all_gather(hidden_states, "mp", axis=1, tiled=True)
-    gate_full, up_full, down_full = gather_weights(gate_online, up_online, down_online, ndp)
-
-    def pair(piece, previous):
-        target_piece = blend(piece, previous)
-        o = jnp.dot(features_all, piece, preferred_element_type=jnp.float32)
-        t = jnp.dot(features_all, target_piece, preferred_element_type=jnp.float32)
-        return o, t
-
-    gate_o, gate_t = pair(gate_full, gate_previous)
-    up_o, up_t = pair(up_full, up_previous)
-    inner_o = (jax.nn.silu(gate_o) * up_o).astype(jnp.bfloat16)
-    inner_t = (jax.nn.silu(gate_t) * up_t).astype(jnp.bfloat16)
+    if ndp == 8 and nmp == 16:
+        _, _, down_full, inner_o, inner_t = fused_gather(
+            hidden_states, gate_online, up_online, down_online, gate_previous, up_previous)
+    else:
+        features_all = lax.all_gather(hidden_states, "mp", axis=1, tiled=True)
+        gate_full, up_full, down_full = gather_weights(gate_online, up_online, down_online, ndp)
+
+        def pair(piece, previous):
+            target_piece = blend(piece, previous)
+            o = jnp.dot(features_all, piece, preferred_element_type=jnp.float32)
+            t = jnp.dot(features_all, target_piece, preferred_element_type=jnp.float32)
+            return o, t
+
+        gate_o, gate_t = pair(gate_full, gate_previous)
+        up_o, up_t = pair(up_full, up_previous)
+        inner_o = (jax.nn.silu(gate_o) * up_o).astype(jnp.bfloat16)
+        inner_t = (jax.nn.silu(gate_t) * up_t).astype(jnp.bfloat16)
     target_down = blend(down_full, down_previous)
     online_part = jnp.dot(inner_o, down_full, preferred_element_type=jnp.float32)
     target_part = jnp.dot(inner_t, target_down, preferred_element_type=jnp.float32)

time: 343 us -> 365 us (1.064)
  Pallas kernels: 265 us -> 346 us
  matrix products: 60.8 us -> 16.4 us
  between operations: 14.1 us -> 0.7 us
    pallas_call x1, Pallas kernels: 184 us -> 234 us  [fused_gather(): pl.pallas_call(fused_gather_kernel, out_shape=out_shape, in_specs=[any_sp...]
    pallas_call x1, Pallas kernels: 81.1 us -> 112 us  [hier_reduce_scatter(): pl.pallas_call(hier_reduce_kernel, out_shape=jax.ShapeDtypeStruct((n, t,...]
    dot_general x1, matrix products: 27.8 us -> 6.28 us  [local(): jnp.dot(inner_t, target_down, preferred_element_type=jnp.float32)]
    dot_general x2 -> x0, matrix products: 15 us -> none  [the longest x1 9.66 us: pair(): o = jnp.dot(features_all, piece, preferred_element_type=jnp.float32)]
    dot_general x1, matrix products: 17.9 us -> 10.1 us  [local(): jnp.dot(inner_o, down_full, preferred_element_type=jnp.float32)]
  transfers between devices with their start and end apart: 1 -> 0, of which waited for: 0 -> 0; matrix products, arithmetic and copies ran while one was open for 0% -> 0% of each run, Pallas kernels for 54% -> 0%
where the time goes in v8:
time: 365 us
  Pallas kernels  346 us (95%)
  matrix products  16.4 us (4%)
    pallas_call x1, Pallas kernels, fused_gather(): pl.pallas_call(fused_gather_kernel, out_shape=out_shape, in_specs=[any_sp...  234 us
    pallas_call x1, Pallas kernels, hier_reduce_scatter(): pl.pallas_call(hier_reduce_kernel, out_shape=jax.ShapeDtypeStruct((n, t,...  112 us
    dot_general x1, matrix products, local(): jnp.dot(inner_o, down_full, preferred_element_type=jnp.float32)  10.1 us

profile of v8, /device:TPU:1, one launch (start us, length us, event | category | flops | bytes accessed | tf_op | source)
XLA Modules:
  0.0 365.1 jit_solution(1420340353156954980)
XLA Ops:
  0.6 0.0 slice-start
  0.6 234.2 %shard_map.86 = (bf16[4096,896]{1,0:T(8,128)(2,1)}, bf16[4096,896]{1,0:T(8,128)(2,1)}, bf16[896,4096]{1,0:T(8,128)(2,1)}, bf16[512,896]{1,0:T(8,128)(2,1)}, bf16[512,896]{1,0:T(8,128)(2,1)}) custom-call(bf16[512,256]{1,0:T(8,128)(2,1)} %h_ref.1, bf16[512,896]{1,0:T(8,128)(2,1)} %g_ref.1, bf16[512,896]{1,0:T(8,128)(2,1)} %u_ref.1, bf16[896,512]{1,0:T(8,128)(2,1)} %dn_ref.1, ...), custom_call_target="tpu_custom_call" | custom-call | tf_op jit(solution)/shard_map/pallas_call | solution.py:484
  234.9 0.0 slice-start.1
  234.9 0.0 copy-start
  234.9 0.0 copy-start.1
  234.9 10.1 %convolution_convert_fusion.ta_ref = bf16[512,4096]{1,0:T(8,128)(2,1)} fusion(bf16[512,896]{1,0:T(8,128)(2,1)} %get-tuple-element.5, bf16[896,4096]{1,0:T(8,128)(2,1)} %get-tuple-element.6), kind=kOutput, calls=%fused_computation.5 | convolution fusion | flops 3760193536 | bytes 12451840 | tf_op jit(solution)/shard_map/dot_general | solution.py:521
  245.0 0.0 slice-done
  245.0 0.0 slice-done.1
  245.0 0.0 copy-done
  245.0 0.0 copy-done.1
  245.0 6.3 %fusion.3.tb_ref = bf16[512,4096]{1,0:T(8,128)(2,1)} fusion(bf16[512,896]{1,0:T(8,128)(2,1)S(1)} %copy-done.1, bf16[896,4096]{1,0:T(8,128)(2,1)S(1)} %bitcast.8, bf16[896,4096]{1,0:T(8,128)(2,1)S(1)} %copy-done), kind=kOutput, calls=%fused_computation.4 | convolution fusion | flops 3782213632 | bytes 19791872 | tf_op jit(solution)/shard_map/dot_general | solution.py:522
  251.3 111.9 %shard_map.87 = bf16[2,512,256]{2,1,0:T(8,128)(2,1)} custom-call(bf16[512,4096]{1,0:T(8,128)(2,1)} %convolution_convert_fusion.ta_ref, bf16[512,4096]{1,0:T(8,128)(2,1)} %fusion.3.tb_ref), custom_call_target="tpu_custom_call" | custom-call | tf_op jit(solution)/shard_map/pallas_call | solution.py:303
  363.3 1.9 slice_bitcast_fusion
  (1 shorter events, 0.0 us)
Async XLA Ops:
  0.6 244.4 %slice-start = ((s8[7340032]{0:T(1024)(128)(4,1)}), s8[3145728]{0:T(1024)(128)(4,1)S(1)}, s32[]{:S(2)}) async-start(s8[7340032]{0:T(1024)(128)(4,1)} %bitcast.7), calls=%async_computation | async-start | bytes 6291456
  234.9 10.1 %slice-start.1 = ((s8[7340032]{0:T(1024)(128)(4,1)}), s8[4194304]{0:T(1024)(128)(4,1)S(1)}, s32[]{:S(2)}) async-start(s8[7340032]{0:T(1024)(128)(4,1)} %bitcast.7), calls=%async_computation.1 | async-start | bytes 8388608
  234.9 10.1 %copy-start = (bf16[896,4096]{1,0:T(8,128)(2,1)S(1)}, bf16[896,4096]{1,0:T(8,128)(2,1)}, u32[]{:S(2)}) copy-start(bf16[896,4096]{1,0:T(8,128)(2,1)} %get-tuple-element.6) | copy-start | bytes 22020100
  234.9 10.1 %copy-start.1 = (bf16[512,896]{1,0:T(8,128)(2,1)S(1)}, bf16[512,896]{1,0:T(8,128)(2,1)}, u32[]{:S(2)}) copy-start(bf16[512,896]{1,0:T(8,128)(2,1)} %get-tuple-element.7) | copy-start | bytes 2752516

commit v9 on v7

--- a/solution.py
+++ b/solution.py
@@ -335,6 +335,7 @@
     up_o, up_t = pair(up_full, up_previous)
     inner_o = (jax.nn.silu(gate_o) * up_o).astype(jnp.bfloat16)
     inner_t = (jax.nn.silu(gate_t) * up_t).astype(jnp.bfloat16)
+    inner_o, inner_t = lax.optimization_barrier((inner_o, inner_t))
     target_down = blend(down_full, down_previous)
     online_part = jnp.dot(inner_o, down_full, preferred_element_type=jnp.float32)
     target_part = jnp.dot(inner_t, target_down, preferred_element_type=jnp.float32)

time: 343 us -> 340 us (level)
    dot_general x1, matrix products: 27.8 us -> 12.2 us  [local(): jnp.dot(inner_t, target_down, preferred_element_type=jnp.float32)]
    dot_general x1 -> x2, matrix products: 5.39 us -> 19.6 us  [pair(): t = jnp.dot(features_all, target_piece, preferred_element_type=jnp.float32)]
    dot_general x1, matrix products: 17.9 us -> 9.27 us  [local(): jnp.dot(inner_o, down_full, preferred_element_type=jnp.float32)]
    dot_general x1 -> x2, matrix products: 9.66 us -> 17.1 us  [pair(): o = jnp.dot(features_all, piece, preferred_element_type=jnp.float32)]
where the time goes in v9:
time: 340 us
  Pallas kernels  265 us (78%)
  matrix products  58.1 us (17%)
  between operations  14.2 us (4%)
    pallas_call x1, Pallas kernels, gather_weights(): pl.pallas_call(relay_gather_kernel, out_shape=out_shape, in_specs=[any_sp...  184 us
    pallas_call x1, Pallas kernels, hier_reduce_scatter(): pl.pallas_call(hier_reduce_kernel, out_shape=jax.ShapeDtypeStruct((n, t,...  81.2 us
    dot_general x2, matrix products, pair(): t = jnp.dot(features_all, target_piece, preferred_element_type=jnp.float32)  19.6 us
    dot_general x2, matrix products, pair(): o = jnp.dot(features_all, piece, preferred_element_type=jnp.float32)  17.1 us
    dot_general x1, matrix products, local(): jnp.dot(inner_t, target_down, preferred_element_type=jnp.float32)  12.2 us
    dot_general x1, matrix products, local(): jnp.dot(inner_o, down_full, preferred_element_type=jnp.float32)  9.27 us
  transfers between devices with their start and end apart: 1, of which 0 were waited for; matrix products, arithmetic and copies ran while one was open for 0% of the time, Pallas kernels for 54%

profile of v9, /device:TPU:1, one launch (start us, length us, event | category | flops | bytes accessed | tf_op | source)
XLA Modules:
  0.0 339.9 jit_solution(15672388087444537813)
XLA Ops:
  7.2 0.0 all-gather.2.cloned.1.call-start
  7.2 0.7 all-gather.2.cloned.1.call-update
  7.9 0.0 slice-start
  7.9 183.8 %shard_map.86 = (bf16[4096,896]{1,0:T(8,128)(2,1)}, bf16[4096,896]{1,0:T(8,128)(2,1)}, bf16[896,4096]{1,0:T(8,128)(2,1)}) custom-call(bf16[512,896]{1,0:T(8,128)(2,1)} %g_ref.1, bf16[512,896]{1,0:T(8,128)(2,1)} %u_ref.1, bf16[896,512]{1,0:T(8,128)(2,1)} %dn_ref.1), custom_call_target="tpu_custom_call" | custom-call | tf_op jit(solution)/shard_map/pallas_call | solution.py:155
  191.7 0.0 all-gather.2.cloned.1.call-done
  191.7 0.0 slice-start.1
  191.8 0.0 slice-start.2
  191.8 8.5 %fusion.24 = f32[896,512]{1,0:T(8,128)S(1)} fusion(bf16[4096,896]{1,0:T(8,128)(2,1)} %get-tuple-element.7, bf16[512,4096]{1,0:T(8,128)(2,1)} %all-gather.2.cloned.1.call-done), kind=kOutput, calls=%fused_computation.36 | convolution fusion | flops 3758096384 | bytes 13369344 | tf_op jit(solution)/shard_map/dot_general | solution.py:330
  200.2 0.0 slice-done
  200.2 0.0 slice-done.1
  200.3 0.0 slice-start.3
  200.3 9.7 %fusion = f32[896,512]{1,0:T(8,128)} fusion(bf16[512,4096]{1,0:T(8,128)(2,1)} %all-gather.2.cloned.1.call-done, bf16[4096,896]{1,0:T(8,128)(2,1)S(1)} %bitcast.48, bf16[4096,896]{1,0:T(8,128)(2,1)} %get-tuple-element.7), kind=kOutput, calls=%fused_computation.3 | convolution fusion | flops 3780116480 | bytes 20709376 | tf_op jit(solution)/shard_map/dot_general | solution.py:331
  209.9 0.0 copy-start
  209.9 0.0 slice-start.4
  210.0 8.6 %fusion.14 = bf16[512,896]{0,1:T(8,128)(2,1)S(1)} fusion(f32[896,512]{1,0:T(8,128)S(1)} %fusion.24, bf16[4096,896]{1,0:T(8,128)(2,1)} %get-tuple-element.8, bf16[512,4096]{1,0:T(8,128)(2,1)} %all-gather.2.cloned.1.call-done), kind=kOutput, calls=%fused_computation.22 | convolution fusion | flops 3760848896 | bytes 14286848 | tf_op jit(solution)/shard_map/dot_general | solution.py:330
  218.6 0.0 slice-done.2
  218.6 0.0 slice-done.3
  218.6 0.0 copy-done
  218.6 0.0 slice-start.5
  218.7 9.9 %fusion.10 = bf16[512,896]{0,1:T(8,128)(2,1)} fusion(f32[896,512]{1,0:T(8,128)S(1)} %copy-done, bf16[512,4096]{1,0:T(8,128)(2,1)} %all-gather.2.cloned.1.call-done, bf16[4096,896]{1,0:T(8,128)(2,1)S(1)} %bitcast.50, bf16[4096,896]{1,0:T(8,128)(2,1)} %get-tuple-element.8), kind=kOutput, calls=%fused_computation.15 | convolution fusion | flops 3782868992 | bytes 21626880 | tf_op jit(solution)/shard_map/dot_general | solution.py:331
  228.6 0.0 copy-start.1
  228.6 9.3 %convolution_convert_fusion.ta_ref = bf16[512,4096]{1,0:T(8,128)(2,1)} fusion(bf16[512,896]{0,1:T(8,128)(2,1)S(1)} %fusion.14, bf16[896,4096]{1,0:T(8,128)(2,1)} %get-tuple-element.10), kind=kOutput, calls=%fused_computation.13 | convolution fusion | flops 3760193536 | bytes 12451840 | tf_op jit(solution)/shard_map/dot_general | solution.py:340
  237.9 0.0 slice-done.4
  237.9 0.0 slice-done.5
  237.9 0.0 copy-done.1
  237.9 12.2 %fusion.9.tb_ref = bf16[512,4096]{1,0:T(8,128)(2,1)} fusion(bf16[512,896]{0,1:T(8,128)(2,1)S(1)} %copy-done.1, bf16[896,4096]{1,0:T(8,128)(2,1)S(1)} %bitcast.52, bf16[896,4096]{1,0:T(8,128)(2,1)} %get-tuple-element.10), kind=kOutput, calls=%fused_computation.12 | convolution fusion | flops 3782213632 | bytes 19791872 | tf_op jit(solution)/shard_map/dot_general | solution.py:341
  250.0 81.2 %shard_map.87 = bf16[2,512,256]{2,1,0:T(8,128)(2,1)} custom-call(bf16[512,4096]{1,0:T(8,128)(2,1)} %convolution_convert_fusion.ta_ref, bf16[512,4096]{1,0:T(8,128)(2,1)} %fusion.9.tb_ref), custom_call_target="tpu_custom_call" | custom-call | tf_op jit(solution)/shard_map/pallas_call | solution.py:303
  331.2 1.9 slice_bitcast_fusion
  (3 shorter events, 0.0 us)
Async XLA Ops:
  7.2 184.6 %all-gather.2.cloned.1.call-start = ((), (), s32[]{:S(2)}) async-start(), calls=%async_computation | async-start | bytes 4456448 | tf_op jit(solution)/shard_map/all_gather | solution.py:325
  7.9 192.3 %slice-start = ((s8[7340032]{0:T(1024)(128)(4,1)}), s8[3145728]{0:T(1024)(128)(4,1)S(1)}, s32[]{:S(2)}) async-start(s8[7340032]{0:T(1024)(128)(4,1)} %bitcast.47), calls=%async_computation.1 | async-start | bytes 6291456
  191.7 8.5 %slice-start.1 = ((s8[7340032]{0:T(1024)(128)(4,1)}), s8[4194304]{0:T(1024)(128)(4,1)S(1)}, s32[]{:S(2)}) async-start(s8[7340032]{0:T(1024)(128)(4,1)} %bitcast.47), calls=%async_computation.2 | async-start | bytes 8388608
  191.8 26.8 %slice-start.2 = ((s8[7340032]{0:T(1024)(128)(4,1)}), s8[4194304]{0:T(1024)(128)(4,1)S(1)}, s32[]{:S(2)}) async-start(s8[7340032]{0:T(1024)(128)(4,1)} %bitcast.49), calls=%async_computation.3 | async-start | bytes 8388608
  200.3 18.4 %slice-start.3 = ((s8[7340032]{0:T(1024)(128)(4,1)}), s8[3145728]{0:T(1024)(128)(4,1)S(1)}, s32[]{:S(2)}) async-start(s8[7340032]{0:T(1024)(128)(4,1)} %bitcast.49), calls=%async_computation.4 | async-start | bytes 6291456
  209.9 8.7 %copy-start = (f32[896,512]{1,0:T(8,128)S(1)}, f32[896,512]{1,0:T(8,128)}, u32[]{:S(2)}) copy-start(f32[896,512]{1,0:T(8,128)} %fusion) | copy-start | bytes 5505028
  209.9 27.9 %slice-start.4 = ((s8[7340032]{0:T(1024)(128)(4,1)}), s8[4194304]{0:T(1024)(128)(4,1)S(1)}, s32[]{:S(2)}) async-start(s8[7340032]{0:T(1024)(128)(4,1)} %bitcast.51), calls=%async_computation.5 | async-start | bytes 8388608
  218.6 19.2 %slice-start.5 = ((s8[7340032]{0:T(1024)(128)(4,1)}), s8[3145728]{0:T(1024)(128)(4,1)S(1)}, s32[]{:S(2)}) async-start(s8[7340032]{0:T(1024)(128)(4,1)} %bitcast.51), calls=%async_computation.6 | async-start | bytes 6291456
  228.6 9.3 %copy-start.1 = (bf16[512,896]{0,1:T(8,128)(2,1)S(1)}, bf16[512,896]{0,1:T(8,128)(2,1)}, u32[]{:S(2)}) copy-start(bf16[512,896]{0,1:T(8,128)(2,1)} %fusion.10) | copy-start | bytes 2752516
Sparse Core Ops, SparseCore 0:
  10.3 75.1 all-gather.1

commit v10 on v9

--- a/solution.py
+++ b/solution.py
@@ -74,8 +74,8 @@
     )(g, u, dn)
 
 
-def relay_gather_kernel(g_ref, u_ref, dn_ref, gf_ref, uf_ref, df_ref, send_sem, recv_sem,
-                        local_sem):
+def relay_gather_kernel(h_ref, g_ref, u_ref, dn_ref, hf_ref, gf_ref, uf_ref, df_ref, send_sem,
+                        recv_sem, local_sem, hsend, hrecv):
     ndp = 8
     d = lax.axis_index("dp")
     m = lax.axis_index("mp")
@@ -118,10 +118,22 @@
         c[w, 5] = rc(w, 5, slot(w, prv, 0), slot(w, prv, 0), nxt)
         c[w, 6] = rc(w, 6, slot(w, nxt, 1), slot(w, nxt, 1), prv)
         c[w, 7] = rc(w, 7, slot(w, far), slot(w, far), partner)
+    nmp = 16
+    hc = h_ref.shape[1]
+    hmine = hf_ref.at[:, pl.ds(pl.multiple_of(m * hc, hc), hc)]
+    hlocal = pltpu.make_async_copy(h_ref, hmine, local_sem.at[3])
+    hcopies = []
+    for s in range(1, nmp):
+        hcopies.append(pltpu.make_async_remote_copy(
+            src_ref=h_ref, dst_ref=hmine, send_sem=hsend.at[s - 1], recv_sem=hrecv.at[s - 1],
+            device_id=(d, lax.rem(m + s, nmp)), device_id_type=MESH))
     for w in range(3):
         locals_[w].start()
         for k in range(3):
             c[w, k].start()
+    hlocal.start()
+    for cp in hcopies:
+        cp.start()
     for w in range(3):
         c[w, 0].wait_recv()
         c[w, 3].start()
@@ -141,11 +153,12 @@
         for k in range(8):
             c[w, k].wait_send()
         locals_[w].wait()
-
-
-def gather_weights(g, u, dn, ndp):
-    if ndp != 8:
-        return gather_weights_direct(g, u, dn, ndp)
+    hlocal.wait()
+    for cp in hcopies:
+        cp.wait()
+
+
+def gather_relay(h, g, u, dn, ndp):
     any_spec = pl.BlockSpec(memory_space=pl.ANY)
     out_shape = (
         jax.ShapeDtypeStruct((g.shape[0] * ndp, g.shape[1]), g.dtype),
@@ -154,16 +167,18 @@
     )
     return pl.pallas_call(
         relay_gather_kernel,
-        out_shape=out_shape,
-        in_specs=[any_spec] * 3,
-        out_specs=[any_spec] * 3,
+        out_shape=(jax.ShapeDtypeStruct((h.shape[0], h.shape[1] * 16), h.dtype),) + out_shape,
+        in_specs=[any_spec] * 4,
+        out_specs=[any_spec] * 4,
         scratch_shapes=[
             pltpu.SemaphoreType.DMA((24,)),
             pltpu.SemaphoreType.DMA((24,)),
-            pltpu.SemaphoreType.DMA((3,)),
+            pltpu.SemaphoreType.DMA((4,)),
+            pltpu.SemaphoreType.DMA((15,)),
+            pltpu.SemaphoreType.DMA((15,)),
         ],
         compiler_params=pltpu.CompilerParams(has_side_effects=True),
-    )(g, u, dn)
+    )(h, g, u, dn)
 
 
 def reduce_kernel(nmp, t_ref, o_ref, buf, send_sem, recv_sem, local_sem):
@@ -322,8 +337,13 @@
 
 def local(ndp, nmp, hidden_states, gate_online, up_online, down_online, gate_previous,
           up_previous, down_previous):
-    features_all = lax.all_gather(hidden_states, "mp", axis=1, tiled=True)
-    gate_full, up_full, down_full = gather_weights(gate_online, up_online, down_online, ndp)
+    if ndp == 8 and nmp == 16:
+        features_all, gate_full, up_full, down_full = gather_relay(
+            hidden_states, gate_online, up_online, down_online, ndp)
+    else:
+        features_all = lax.all_gather(hidden_states, "mp", axis=1, tiled=True)
+        gate_full, up_full, down_full = gather_weights_direct(gate_online, up_online,
+                                                              down_online, ndp)
 
     def pair(piece, previous):
         target_piece = blend(piece, previous)

time: 340 us -> 335 us (0.985)
  between operations: 14.2 us -> 0.78 us
  Pallas kernels: 265 us -> 276 us
    pallas_call x1, Pallas kernels: 184 us -> 190 us  [gather_relay(): pl.pallas_call(relay_gather_kernel, out_shape=(jax.ShapeDtypeStruct((h.sh...]
    pallas_call x1, Pallas kernels: 81.2 us -> 86.2 us  [hier_reduce_scatter(): pl.pallas_call(hier_reduce_kernel, out_shape=jax.ShapeDtypeStruct((n, t,...]
  transfers between devices with their start and end apart: 1 -> 0, of which waited for: 0 -> 0; matrix products, arithmetic and copies ran while one was open for 0% -> 0% of each run, Pallas kernels for 54% -> 0%
where the time goes in v10:
time: 335 us
  Pallas kernels  276 us (82%)
  matrix products  55.7 us (17%)
    pallas_call x1, Pallas kernels, gather_relay(): pl.pallas_call(relay_gather_kernel, out_shape=(jax.ShapeDtypeStruct((h.sh...  190 us
    pallas_call x1, Pallas kernels, hier_reduce_scatter(): pl.pallas_call(hier_reduce_kernel, out_shape=jax.ShapeDtypeStruct((n, t,...  86.2 us
    dot_general x2, matrix products, pair(): t = jnp.dot(features_all, target_piece, preferred_element_type=jnp.float32)  20.1 us
    dot_general x2, matrix products, pair(): o = jnp.dot(features_all, piece, preferred_element_type=jnp.float32)  14.7 us
    dot_general x1, matrix products, local(): jnp.dot(inner_t, target_down, preferred_element_type=jnp.float32)  11.4 us
    dot_general x1, matrix products, local(): jnp.dot(inner_o, down_full, preferred_element_type=jnp.float32)  9.5 us

profile of v10, /device:TPU:1, one launch (start us, length us, event | category | flops | bytes accessed | tf_op | source)
XLA Modules:
  0.0 334.8 jit_solution(2115735773035855117)
XLA Ops:
  0.6 0.0 slice-start
  0.6 190.2 %shard_map.86 = (bf16[512,4096]{1,0:T(8,128)(2,1)}, bf16[4096,896]{1,0:T(8,128)(2,1)}, bf16[4096,896]{1,0:T(8,128)(2,1)}, bf16[896,4096]{1,0:T(8,128)(2,1)}) custom-call(bf16[512,256]{1,0:T(8,128)(2,1)} %h_ref.1, bf16[512,896]{1,0:T(8,128)(2,1)} %g_ref.1, bf16[512,896]{1,0:T(8,128)(2,1)} %u_ref.1, bf16[896,512]{1,0:T(8,128)(2,1)} %dn_ref.1), custom_call_target="tpu_custom_call" | custom-call | tf_op jit(solution)/shard_map/pallas_call | solution.py:168
  190.9 0.0 copy-start
  190.9 0.0 copy-start.1
  190.9 0.0 slice-start.1
  190.9 0.0 slice-start.2
  190.9 10.1 %fusion.16 = f32[512,896]{1,0:T(8,128)S(1)} fusion(bf16[512,4096]{1,0:T(8,128)(2,1)} %get-tuple-element.8, bf16[4096,896]{1,0:T(8,128)(2,1)} %get-tuple-element.9), kind=kOutput, calls=%fused_computation.24 | convolution fusion | flops 3758096384 | bytes 13369344 | tf_op jit(solution)/shard_map/dot_general | solution.py:350
  201.1 0.0 copy-done
  201.1 0.0 copy-done.1
  201.1 0.0 slice-start.3
  201.1 4.6 %multiply_convert_fusion.1 = bf16[512,896]{1,0:T(8,128)(2,1)S(1)} fusion(f32[512,896]{1,0:T(8,128)S(1)} %fusion.16, bf16[512,4096]{1,0:T(8,128)(2,1)S(1)} %copy-done.1, bf16[4096,896]{1,0:T(8,128)(2,1)S(1)} %copy-done), kind=kOutput, calls=%fused_computation.15 | convolution fusion | flops 3760848896 | bytes 14286848 | tf_op jit(solution)/shard_map/dot_general | solution.py:350
  205.7 0.0 slice-done
  205.7 0.0 slice-done.1
  205.7 0.0 slice-start.4
  205.7 10.3 %fusion.1 = f32[512,896]{1,0:T(8,128)} fusion(bf16[512,4096]{1,0:T(8,128)(2,1)} %get-tuple-element.8, bf16[4096,896]{1,0:T(8,128)(2,1)S(1)} %bitcast.14, bf16[4096,896]{1,0:T(8,128)(2,1)} %get-tuple-element.10), kind=kOutput, calls=%fused_computation.4 | convolution fusion | flops 3780116480 | bytes 20709376 | tf_op jit(solution)/shard_map/dot_general | solution.py:351
  216.0 0.0 slice-done.2
  216.0 0.0 slice-done.3
  216.0 0.0 slice-start.5
  216.0 9.9 %multiply_convert_fusion = bf16[512,896]{1,0:T(8,128)(2,1)S(1)} fusion(f32[512,896]{1,0:T(8,128)} %fusion.1, bf16[512,4096]{1,0:T(8,128)(2,1)} %get-tuple-element.8, bf16[4096,896]{1,0:T(8,128)(2,1)S(1)} %bitcast.16, bf16[4096,896]{1,0:T(8,128)(2,1)} %get-tuple-element.9), kind=kOutput, calls=%fused_computation.14 | convolution fusion | flops 3782868992 | bytes 21626880 | tf_op jit(solution)/shard_map/dot_general | solution.py:351
  225.9 9.5 %convolution_convert_fusion.ta_ref = bf16[512,4096]{1,0:T(8,128)(2,1)} fusion(bf16[512,896]{1,0:T(8,128)(2,1)S(1)} %multiply_convert_fusion.1, bf16[896,4096]{1,0:T(8,128)(2,1)} %get-tuple-element.12), kind=kOutput, calls=%fused_computation.13 | convolution fusion | flops 3760193536 | bytes 12451840 | tf_op jit(solution)/shard_map/dot_general | solution.py:360
  235.4 0.0 slice-done.4
  235.4 0.0 slice-done.5
  235.4 11.4 %fusion.9.tb_ref = bf16[512,4096]{1,0:T(8,128)(2,1)} fusion(bf16[512,896]{1,0:T(8,128)(2,1)S(1)} %multiply_convert_fusion, bf16[896,4096]{1,0:T(8,128)(2,1)S(1)} %bitcast.18, bf16[896,4096]{1,0:T(8,128)(2,1)} %get-tuple-element.12), kind=kOutput, calls=%fused_computation.12 | convolution fusion | flops 3782213632 | bytes 19791872 | tf_op jit(solution)/shard_map/dot_general | solution.py:361
  246.8 86.2 %shard_map.87 = bf16[2,512,256]{2,1,0:T(8,128)(2,1)} custom-call(bf16[512,4096]{1,0:T(8,128)(2,1)} %convolution_convert_fusion.ta_ref, bf16[512,4096]{1,0:T(8,128)(2,1)} %fusion.9.tb_ref), custom_call_target="tpu_custom_call" | custom-call | tf_op jit(solution)/shard_map/pallas_call | solution.py:318
  333.0 1.9 slice_bitcast_fusion
  (3 shorter events, 0.0 us)
Async XLA Ops:
  0.6 205.1 %slice-start = ((s8[7340032]{0:T(1024)(128)(4,1)}), s8[3145728]{0:T(1024)(128)(4,1)S(1)}, s32[]{:S(2)}) async-start(s8[7340032]{0:T(1024)(128)(4,1)} %bitcast.13), calls=%async_computation | async-start | bytes 6291456
  190.9 10.2 %copy-start = (bf16[4096,896]{1,0:T(8,128)(2,1)S(1)}, bf16[4096,896]{1,0:T(8,128)(2,1)}, u32[]{:S(2)}) copy-start(bf16[4096,896]{1,0:T(8,128)(2,1)} %get-tuple-element.10) | copy-start | bytes 22020100
  190.9 10.2 %copy-start.1 = (bf16[512,4096]{1,0:T(8,128)(2,1)S(1)}, bf16[512,4096]{1,0:T(8,128)(2,1)}, u32[]{:S(2)}) copy-start(bf16[512,4096]{1,0:T(8,128)(2,1)} %get-tuple-element.8) | copy-start | bytes 12582916
  190.9 14.8 %slice-start.1 = ((s8[7340032]{0:T(1024)(128)(4,1)}), s8[4194304]{0:T(1024)(128)(4,1)S(1)}, s32[]{:S(2)}) async-start(s8[7340032]{0:T(1024)(128)(4,1)} %bitcast.13), calls=%async_computation.1 | async-start | bytes 8388608
  190.9 25.1 %slice-start.2 = ((s8[7340032]{0:T(1024)(128)(4,1)}), s8[4194304]{0:T(1024)(128)(4,1)S(1)}, s32[]{:S(2)}) async-start(s8[7340032]{0:T(1024)(128)(4,1)} %bitcast.15), calls=%async_computation.2 | async-start | bytes 8388608
  201.1 14.9 %slice-start.3 = ((s8[7340032]{0:T(1024)(128)(4,1)}), s8[3145728]{0:T(1024)(128)(4,1)S(1)}, s32[]{:S(2)}) async-start(s8[7340032]{0:T(1024)(128)(4,1)} %bitcast.15), calls=%async_computation.3 | async-start | bytes 6291456
  205.7 29.7 %slice-start.4 = ((s8[7340032]{0:T(1024)(128)(4,1)}), s8[4194304]{0:T(1024)(128)(4,1)S(1)}, s32[]{:S(2)}) async-start(s8[7340032]{0:T(1024)(128)(4,1)} %bitcast.17), calls=%async_computation.4 | async-start | bytes 8388608
  216.0 19.4 %slice-start.5 = ((s8[7340032]{0:T(1024)(128)(4,1)}), s8[3145728]{0:T(1024)(128)(4,1)S(1)}, s32[]{:S(2)}) async-start(s8[7340032]{0:T(1024)(128)(4,1)} %bitcast.17), calls=%async_computation.5 | async-start | bytes 6291456

commit v11 on v10

--- a/solution.py
+++ b/solution.py
@@ -135,9 +135,6 @@
     for cp in hcopies:
         cp.start()
     for w in range(3):
-        c[w, 0].wait_recv()
-        c[w, 3].start()
-        c[w, 4].start()
         c[w, 1].wait_recv()
         c[w, 5].start()
         c[w, 2].wait_recv()
@@ -146,6 +143,10 @@
         c[w, 5].wait_recv()
         c[w, 6].wait_recv()
         c[w, 7].start()
+    for w in range(3):
+        c[w, 0].wait_recv()
+        c[w, 3].start()
+        c[w, 4].start()
     for w in range(3):
         for k in (3, 4, 7):
             c[w, k].wait_recv()

time: 335 us -> 335 us (level)
  no operation moved by 1% of the time
where the time goes in v11:
time: 335 us
  Pallas kernels  276 us (82%)
  matrix products  55.7 us (17%)
    pallas_call x1, Pallas kernels, gather_relay(): pl.pallas_call(relay_gather_kernel, out_shape=(jax.ShapeDtypeStruct((h.sh...  190 us
    pallas_call x1, Pallas kernels, hier_reduce_scatter(): pl.pallas_call(hier_reduce_kernel, out_shape=jax.ShapeDtypeStruct((n, t,...  86.2 us
    dot_general x2, matrix products, pair(): t = jnp.dot(features_all, target_piece, preferred_element_type=jnp.float32)  20.1 us
    dot_general x2, matrix products, pair(): o = jnp.dot(features_all, piece, preferred_element_type=jnp.float32)  14.7 us
    dot_general x1, matrix products, local(): jnp.dot(inner_t, target_down, preferred_element_type=jnp.float32)  11.4 us
    dot_general x1, matrix products, local(): jnp.dot(inner_o, down_full, preferred_element_type=jnp.float32)  9.5 us

profile of v11, /device:TPU:1, one launch (start us, length us, event | category | flops | bytes accessed | tf_op | source)
XLA Modules:
  0.0 334.8 jit_solution(1045708465549504428)
XLA Ops:
  0.6 0.0 slice-start
  0.6 190.2 %shard_map.86 = (bf16[512,4096]{1,0:T(8,128)(2,1)}, bf16[4096,896]{1,0:T(8,128)(2,1)}, bf16[4096,896]{1,0:T(8,128)(2,1)}, bf16[896,4096]{1,0:T(8,128)(2,1)}) custom-call(bf16[512,256]{1,0:T(8,128)(2,1)} %h_ref.1, bf16[512,896]{1,0:T(8,128)(2,1)} %g_ref.1, bf16[512,896]{1,0:T(8,128)(2,1)} %u_ref.1, bf16[896,512]{1,0:T(8,128)(2,1)} %dn_ref.1), custom_call_target="tpu_custom_call" | custom-call | tf_op jit(solution)/shard_map/pallas_call | solution.py:169
  190.9 0.0 copy-start
  190.9 0.0 copy-start.1
  190.9 0.0 slice-start.1
  190.9 0.0 slice-start.2
  190.9 10.1 %fusion.16 = f32[512,896]{1,0:T(8,128)S(1)} fusion(bf16[512,4096]{1,0:T(8,128)(2,1)} %get-tuple-element.8, bf16[4096,896]{1,0:T(8,128)(2,1)} %get-tuple-element.9), kind=kOutput, calls=%fused_computation.24 | convolution fusion | flops 3758096384 | bytes 13369344 | tf_op jit(solution)/shard_map/dot_general | solution.py:351
  201.1 0.0 copy-done
  201.1 0.0 copy-done.1
  201.1 0.0 slice-start.3
  201.1 4.6 %multiply_convert_fusion.1 = bf16[512,896]{1,0:T(8,128)(2,1)S(1)} fusion(f32[512,896]{1,0:T(8,128)S(1)} %fusion.16, bf16[512,4096]{1,0:T(8,128)(2,1)S(1)} %copy-done.1, bf16[4096,896]{1,0:T(8,128)(2,1)S(1)} %copy-done), kind=kOutput, calls=%fused_computation.15 | convolution fusion | flops 3760848896 | bytes 14286848 | tf_op jit(solution)/shard_map/dot_general | solution.py:351
  205.7 0.0 slice-done
  205.7 0.0 slice-done.1
  205.7 0.0 slice-start.4
  205.7 10.3 %fusion.1 = f32[512,896]{1,0:T(8,128)} fusion(bf16[512,4096]{1,0:T(8,128)(2,1)} %get-tuple-element.8, bf16[4096,896]{1,0:T(8,128)(2,1)S(1)} %bitcast.14, bf16[4096,896]{1,0:T(8,128)(2,1)} %get-tuple-element.10), kind=kOutput, calls=%fused_computation.4 | convolution fusion | flops 3780116480 | bytes 20709376 | tf_op jit(solution)/shard_map/dot_general | solution.py:352
  216.0 0.0 slice-done.2
  216.0 0.0 slice-done.3
  216.0 0.0 slice-start.5
  216.0 9.9 %multiply_convert_fusion = bf16[512,896]{1,0:T(8,128)(2,1)S(1)} fusion(f32[512,896]{1,0:T(8,128)} %fusion.1, bf16[512,4096]{1,0:T(8,128)(2,1)} %get-tuple-element.8, bf16[4096,896]{1,0:T(8,128)(2,1)S(1)} %bitcast.16, bf16[4096,896]{1,0:T(8,128)(2,1)} %get-tuple-element.9), kind=kOutput, calls=%fused_computation.14 | convolution fusion | flops 3782868992 | bytes 21626880 | tf_op jit(solution)/shard_map/dot_general | solution.py:352
  225.9 9.5 %convolution_convert_fusion.ta_ref = bf16[512,4096]{1,0:T(8,128)(2,1)} fusion(bf16[512,896]{1,0:T(8,128)(2,1)S(1)} %multiply_convert_fusion.1, bf16[896,4096]{1,0:T(8,128)(2,1)} %get-tuple-element.12), kind=kOutput, calls=%fused_computation.13 | convolution fusion | flops 3760193536 | bytes 12451840 | tf_op jit(solution)/shard_map/dot_general | solution.py:361
  235.4 0.0 slice-done.4
  235.4 0.0 slice-done.5
  235.4 11.4 %fusion.9.tb_ref = bf16[512,4096]{1,0:T(8,128)(2,1)} fusion(bf16[512,896]{1,0:T(8,128)(2,1)S(1)} %multiply_convert_fusion, bf16[896,4096]{1,0:T(8,128)(2,1)S(1)} %bitcast.18, bf16[896,4096]{1,0:T(8,128)(2,1)} %get-tuple-element.12), kind=kOutput, calls=%fused_computation.12 | convolution fusion | flops 3782213632 | bytes 19791872 | tf_op jit(solution)/shard_map/dot_general | solution.py:362
  246.8 86.2 %shard_map.87 = bf16[2,512,256]{2,1,0:T(8,128)(2,1)} custom-call(bf16[512,4096]{1,0:T(8,128)(2,1)} %convolution_convert_fusion.ta_ref, bf16[512,4096]{1,0:T(8,128)(2,1)} %fusion.9.tb_ref), custom_call_target="tpu_custom_call" | custom-call | tf_op jit(solution)/shard_map/pallas_call | solution.py:319
  333.0 1.9 slice_bitcast_fusion
  (3 shorter events, 0.0 us)
Async XLA Ops:
  0.6 205.1 %slice-start = ((s8[7340032]{0:T(1024)(128)(4,1)}), s8[3145728]{0:T(1024)(128)(4,1)S(1)}, s32[]{:S(2)}) async-start(s8[7340032]{0:T(1024)(128)(4,1)} %bitcast.13), calls=%async_computation | async-start | bytes 6291456
  190.9 10.2 %copy-start = (bf16[4096,896]{1,0:T(8,128)(2,1)S(1)}, bf16[4096,896]{1,0:T(8,128)(2,1)}, u32[]{:S(2)}) copy-start(bf16[4096,896]{1,0:T(8,128)(2,1)} %get-tuple-element.10) | copy-start | bytes 22020100
  190.9 10.2 %copy-start.1 = (bf16[512,4096]{1,0:T(8,128)(2,1)S(1)}, bf16[512,4096]{1,0:T(8,128)(2,1)}, u32[]{:S(2)}) copy-start(bf16[512,4096]{1,0:T(8,128)(2,1)} %get-tuple-element.8) | copy-start | bytes 12582916
  190.9 14.8 %slice-start.1 = ((s8[7340032]{0:T(1024)(128)(4,1)}), s8[4194304]{0:T(1024)(128)(4,1)S(1)}, s32[]{:S(2)}) async-start(s8[7340032]{0:T(1024)(128)(4,1)} %bitcast.13), calls=%async_computation.1 | async-start | bytes 8388608
  190.9 25.1 %slice-start.2 = ((s8[7340032]{0:T(1024)(128)(4,1)}), s8[4194304]{0:T(1024)(128)(4,1)S(1)}, s32[]{:S(2)}) async-start(s8[7340032]{0:T(1024)(128)(4,1)} %bitcast.15), calls=%async_computation.2 | async-start | bytes 8388608
  201.1 14.9 %slice-start.3 = ((s8[7340032]{0:T(1024)(128)(4,1)}), s8[3145728]{0:T(1024)(128)(4,1)S(1)}, s32[]{:S(2)}) async-start(s8[7340032]{0:T(1024)(128)(4,1)} %bitcast.15), calls=%async_computation.3 | async-start | bytes 6291456
  205.7 29.7 %slice-start.4 = ((s8[7340032]{0:T(1024)(128)(4,1)}), s8[4194304]{0:T(1024)(128)(4,1)S(1)}, s32[]{:S(2)}) async-start(s8[7340032]{0:T(1024)(128)(4,1)} %bitcast.17), calls=%async_computation.4 | async-start | bytes 8388608
  216.0 19.4 %slice-start.5 = ((s8[7340032]{0:T(1024)(128)(4,1)}), s8[3145728]{0:T(1024)(128)(4,1)S(1)}, s32[]{:S(2)}) async-start(s8[7340032]{0:T(1024)(128)(4,1)} %bitcast.17), calls=%async_computation.5 | async-start | bytes 6291456

commit v12 on v11

--- a/solution.py
+++ b/solution.py
@@ -336,6 +336,155 @@
     )(ta, tb)
 
 
+def split_reduce_kernel(ta_ref, tb_ref, o_ref, own, r1, sa2, ra2, fa2, sa3, ra3,
+                        sb2, rb2, fb2, sb3, rb3, ls, ss1, rs1, ssa2, rsa2, ssa3, rsa3,
+                        ssb2, rsb2, ssb3, rsb3):
+    d = lax.axis_index("dp")
+    m = lax.axis_index("mp")
+    c = m % 2
+    z = (m // 2) % 4
+    xh = m // 8
+    w = o_ref.shape[2]
+    half = o_ref.shape[1] // 2
+    ra = pl.ds(0, half)
+    rb = pl.ds(half, half)
+    rows = 32
+    nchunk = half // rows
+    f32 = jnp.float32
+    xpeer = m + 8 - 16 * xh
+
+    def blk(b, k):
+        return (ta_ref, tb_ref)[k].at[:, pl.ds(pl.multiple_of(b * w, w), w)]
+
+    def rcopy(src, dst, ss, rs, mm):
+        return pltpu.make_async_remote_copy(src_ref=src, dst_ref=dst, send_sem=ss, recv_sem=rs,
+                                            device_id=(d, mm), device_id_type=MESH)
+
+    locs = []
+    st1 = []
+    for j in range(16):
+        bx, bz, k = j // 8, (j // 2) % 4, j % 2
+        jj = bx * 4 + bz
+        locs.append(pltpu.make_async_copy(blk(bx * 8 + bz * 2 + c, k), own.at[jj, k],
+                                          ls.at[j]))
+        st1.append(rcopy(blk(bx * 8 + bz * 2 + (1 - c), k), r1.at[jj, k], ss1.at[j], rs1.at[j],
+                         m + 1 - 2 * c))
+    for j in range(16):
+        st1[j].start()
+        locs[j].start()
+    for j in range(16):
+        locs[j].wait()
+        st1[j].wait()
+
+    def pair_sum(idx, r):
+        return own[idx, :, r, :].astype(f32) + r1[idx, :, r, :].astype(f32)
+
+    def fill_b2(i, carry):
+        r = pl.ds(pl.multiple_of(half + i * rows, rows), rows)
+        q = pl.ds(pl.multiple_of(i * rows, rows), rows)
+        for bz in range(4):
+            sb2[bz, :, q, :] = pair_sum((1 - xh) * 4 + bz, r).astype(sb2.dtype)
+        return carry
+
+    lax.fori_loop(0, nchunk, fill_b2, 0)
+    cb2 = rcopy(sb2, rb2, ssb2.at[0], rsb2.at[0], xpeer)
+    cb2.start()
+    ca2 = []
+    for s in range(1, 4):
+        zt = (z + s) % 4
+
+        def fill_a2(i, carry, s=s, zt=zt):
+            q = pl.ds(pl.multiple_of(i * rows, rows), rows)
+            for bx in range(2):
+                sa2[s - 1, bx, :, q, :] = pair_sum(bx * 4 + zt, q).astype(sa2.dtype)
+            return carry
+
+        lax.fori_loop(0, nchunk, fill_a2, 0)
+        cp = rcopy(sa2.at[s - 1], ra2.at[s - 1], ssa2.at[s - 1], rsa2.at[s - 1],
+                   xh * 8 + zt * 2 + c)
+        cp.start()
+        ca2.append(cp)
+
+    cb2.wait()
+
+    def sum_b2(i, carry):
+        r = pl.ds(pl.multiple_of(half + i * rows, rows), rows)
+        q = pl.ds(pl.multiple_of(i * rows, rows), rows)
+        for bz in range(4):
+            fb2[bz, :, q, :] = pair_sum(xh * 4 + bz, r) + rb2[bz, :, q, :].astype(f32)
+        return carry
+
+    lax.fori_loop(0, nchunk, sum_b2, 0)
+    cb3 = []
+    for s in range(1, 4):
+        zt = (z + s) % 4
+        sb3[s - 1] = fb2[zt].astype(sb3.dtype)
+        cp = rcopy(sb3.at[s - 1], rb3.at[s - 1], ssb3.at[s - 1], rsb3.at[s - 1],
+                   xh * 8 + zt * 2 + c)
+        cp.start()
+        cb3.append(cp)
+
+    for cp in ca2:
+        cp.wait()
+
+    def sum_a2(i, carry):
+        q = pl.ds(pl.multiple_of(i * rows, rows), rows)
+        for bx in range(2):
+            acc = pair_sum(bx * 4 + z, q)
+            for k in range(3):
+                acc = acc + ra2[k, bx, :, q, :].astype(f32)
+            fa2[bx, :, q, :] = acc
+        return carry
+
+    lax.fori_loop(0, nchunk, sum_a2, 0)
+    sa3[...] = fa2[1 - xh].astype(sa3.dtype)
+    ca3 = rcopy(sa3, ra3, ssa3.at[0], rsa3.at[0], xpeer)
+    ca3.start()
+    for cp in cb3:
+        cp.wait()
+    acc = fb2[z]
+    for k in range(3):
+        acc = acc + rb3[k].astype(f32)
+    o_ref[:, rb, :] = acc.astype(o_ref.dtype)
+    ca3.wait()
+    o_ref[:, ra, :] = (fa2[xh] + ra3[...].astype(f32)).astype(o_ref.dtype)
+
+
+def split_reduce_scatter(ta, tb):
+    n = 2
+    t, width = ta.shape
+    w = width // 16
+    h = t // 2
+    bf = jnp.bfloat16
+    f32 = jnp.float32
+    dma = pltpu.SemaphoreType.DMA
+    return pl.pallas_call(
+        split_reduce_kernel,
+        out_shape=jax.ShapeDtypeStruct((n, t, w), bf),
+        in_specs=[pl.BlockSpec(memory_space=pl.ANY)] * 2,
+        out_specs=pl.BlockSpec(memory_space=pltpu.VMEM),
+        scratch_shapes=[
+            pltpu.VMEM((8, n, t, w), bf),
+            pltpu.VMEM((8, n, t, w), bf),
+            pltpu.VMEM((3, 2, n, h, w), bf),
+            pltpu.VMEM((3, 2, n, h, w), bf),
+            pltpu.VMEM((2, n, h, w), f32),
+            pltpu.VMEM((n, h, w), bf),
+            pltpu.VMEM((n, h, w), bf),
+            pltpu.VMEM((4, n, h, w), bf),
+            pltpu.VMEM((4, n, h, w), bf),
+            pltpu.VMEM((4, n, h, w), f32),
+            pltpu.VMEM((3, n, h, w), bf),
+            pltpu.VMEM((3, n, h, w), bf),
+            dma((16,)), dma((16,)), dma((16,)),
+            dma((3,)), dma((3,)), dma((1,)), dma((1,)),
+            dma((1,)), dma((1,)), dma((3,)), dma((3,)),
+        ],
+        compiler_params=pltpu.CompilerParams(has_side_effects=True,
+                                             vmem_limit_bytes=56 * 1024 * 1024),
+    )(ta, tb)
+
+
 def local(ndp, nmp, hidden_states, gate_online, up_online, down_online, gate_previous,
           up_previous, down_previous):
     if ndp == 8 and nmp == 16:
@@ -361,8 +510,8 @@
     online_part = jnp.dot(inner_o, down_full, preferred_element_type=jnp.float32)
     target_part = jnp.dot(inner_t, target_down, preferred_element_type=jnp.float32)
     if nmp == 16:
-        result = hier_reduce_scatter(online_part.astype(jnp.bfloat16),
-                                     target_part.astype(jnp.bfloat16))
+        result = split_reduce_scatter(online_part.astype(jnp.bfloat16),
+                                      target_part.astype(jnp.bfloat16))
     else:
         terms = jnp.stack([online_part, target_part], axis=0).astype(jnp.bfloat16)
         result = reduce_scatter(terms, nmp)

time: 335 us -> 312 us (0.931)
  Pallas kernels: 276 us -> 254 us
    pallas_call x1, Pallas kernels: 86.2 us -> 63.5 us  [split_reduce_scatter(): pl.pallas_call(split_reduce_kernel, out_shape=jax.ShapeDtypeStruct((n, t,...]
where the time goes in v12:
time: 312 us
  Pallas kernels  254 us (81%)
  matrix products  55.7 us (18%)
    pallas_call x1, Pallas kernels, gather_relay(): pl.pallas_call(relay_gather_kernel, out_shape=(jax.ShapeDtypeStruct((h.sh...  190 us
    pallas_call x1, Pallas kernels, split_reduce_scatter(): pl.pallas_call(split_reduce_kernel, out_shape=jax.ShapeDtypeStruct((n, t,...  63.5 us
    dot_general x2, matrix products, pair(): t = jnp.dot(features_all, target_piece, preferred_element_type=jnp.float32)  20.1 us
    dot_general x2, matrix products, pair(): o = jnp.dot(features_all, piece, preferred_element_type=jnp.float32)  14.7 us
    dot_general x1, matrix products, local(): jnp.dot(inner_t, target_down, preferred_element_type=jnp.float32)  11.4 us
    dot_general x1, matrix products, local(): jnp.dot(inner_o, down_full, preferred_element_type=jnp.float32)  9.5 us

profile of v12, /device:TPU:1, one launch (start us, length us, event | category | flops | bytes accessed | tf_op | source)
XLA Modules:
  0.0 312.1 jit_solution(5348574565353739745)
XLA Ops:
  0.6 0.0 slice-start
  0.6 190.2 %shard_map.86 = (bf16[512,4096]{1,0:T(8,128)(2,1)}, bf16[4096,896]{1,0:T(8,128)(2,1)}, bf16[4096,896]{1,0:T(8,128)(2,1)}, bf16[896,4096]{1,0:T(8,128)(2,1)}) custom-call(bf16[512,256]{1,0:T(8,128)(2,1)} %h_ref.1, bf16[512,896]{1,0:T(8,128)(2,1)} %g_ref.1, bf16[512,896]{1,0:T(8,128)(2,1)} %u_ref.1, bf16[896,512]{1,0:T(8,128)(2,1)} %dn_ref.1), custom_call_target="tpu_custom_call" | custom-call | tf_op jit(solution)/shard_map/pallas_call | solution.py:169
  190.9 0.0 copy-start
  190.9 0.0 copy-start.1
  190.9 0.0 slice-start.1
  190.9 0.0 slice-start.2
  190.9 10.1 %fusion.16 = f32[512,896]{1,0:T(8,128)S(1)} fusion(bf16[512,4096]{1,0:T(8,128)(2,1)} %get-tuple-element.8, bf16[4096,896]{1,0:T(8,128)(2,1)} %get-tuple-element.9), kind=kOutput, calls=%fused_computation.24 | convolution fusion | flops 3758096384 | bytes 13369344 | tf_op jit(solution)/shard_map/dot_general | solution.py:500
  201.1 0.0 copy-done
  201.1 0.0 copy-done.1
  201.1 0.0 slice-start.3
  201.1 4.6 %multiply_convert_fusion.1 = bf16[512,896]{1,0:T(8,128)(2,1)S(1)} fusion(f32[512,896]{1,0:T(8,128)S(1)} %fusion.16, bf16[512,4096]{1,0:T(8,128)(2,1)S(1)} %copy-done.1, bf16[4096,896]{1,0:T(8,128)(2,1)S(1)} %copy-done), kind=kOutput, calls=%fused_computation.15 | convolution fusion | flops 3760848896 | bytes 14286848 | tf_op jit(solution)/shard_map/dot_general | solution.py:500
  205.7 0.0 slice-done
  205.7 0.0 slice-done.1
  205.7 0.0 slice-start.4
  205.7 10.3 %fusion.1 = f32[512,896]{1,0:T(8,128)} fusion(bf16[512,4096]{1,0:T(8,128)(2,1)} %get-tuple-element.8, bf16[4096,896]{1,0:T(8,128)(2,1)S(1)} %bitcast.14, bf16[4096,896]{1,0:T(8,128)(2,1)} %get-tuple-element.10), kind=kOutput, calls=%fused_computation.4 | convolution fusion | flops 3780116480 | bytes 20709376 | tf_op jit(solution)/shard_map/dot_general | solution.py:501
  216.0 0.0 slice-done.2
  216.0 0.0 slice-done.3
  216.0 0.0 slice-start.5
  216.0 9.9 %multiply_convert_fusion = bf16[512,896]{1,0:T(8,128)(2,1)S(1)} fusion(f32[512,896]{1,0:T(8,128)} %fusion.1, bf16[512,4096]{1,0:T(8,128)(2,1)} %get-tuple-element.8, bf16[4096,896]{1,0:T(8,128)(2,1)S(1)} %bitcast.16, bf16[4096,896]{1,0:T(8,128)(2,1)} %get-tuple-element.9), kind=kOutput, calls=%fused_computation.14 | convolution fusion | flops 3782868992 | bytes 21626880 | tf_op jit(solution)/shard_map/dot_general | solution.py:501
  225.9 9.5 %convolution_convert_fusion.ta_ref = bf16[512,4096]{1,0:T(8,128)(2,1)} fusion(bf16[512,896]{1,0:T(8,128)(2,1)S(1)} %multiply_convert_fusion.1, bf16[896,4096]{1,0:T(8,128)(2,1)} %get-tuple-element.12), kind=kOutput, calls=%fused_computation.13 | convolution fusion | flops 3760193536 | bytes 12451840 | tf_op jit(solution)/shard_map/dot_general | solution.py:510
  235.4 0.0 slice-done.4
  235.4 0.0 slice-done.5
  235.4 11.4 %fusion.9.tb_ref = bf16[512,4096]{1,0:T(8,128)(2,1)} fusion(bf16[512,896]{1,0:T(8,128)(2,1)S(1)} %multiply_convert_fusion, bf16[896,4096]{1,0:T(8,128)(2,1)S(1)} %bitcast.18, bf16[896,4096]{1,0:T(8,128)(2,1)} %get-tuple-element.12), kind=kOutput, calls=%fused_computation.12 | convolution fusion | flops 3782213632 | bytes 19791872 | tf_op jit(solution)/shard_map/dot_general | solution.py:511
  246.8 63.5 %shard_map.87 = bf16[2,512,256]{2,1,0:T(8,128)(2,1)} custom-call(bf16[512,4096]{1,0:T(8,128)(2,1)} %convolution_convert_fusion.ta_ref, bf16[512,4096]{1,0:T(8,128)(2,1)} %fusion.9.tb_ref), custom_call_target="tpu_custom_call" | custom-call | tf_op jit(solution)/shard_map/pallas_call | solution.py:461
  310.3 1.9 slice_bitcast_fusion
  (3 shorter events, 0.0 us)
Async XLA Ops:
  0.6 205.1 %slice-start = ((s8[7340032]{0:T(1024)(128)(4,1)}), s8[3145728]{0:T(1024)(128)(4,1)S(1)}, s32[]{:S(2)}) async-start(s8[7340032]{0:T(1024)(128)(4,1)} %bitcast.13), calls=%async_computation | async-start | bytes 6291456
  190.9 10.2 %copy-start = (bf16[4096,896]{1,0:T(8,128)(2,1)S(1)}, bf16[4096,896]{1,0:T(8,128)(2,1)}, u32[]{:S(2)}) copy-start(bf16[4096,896]{1,0:T(8,128)(2,1)} %get-tuple-element.10) | copy-start | bytes 22020100
  190.9 10.2 %copy-start.1 = (bf16[512,4096]{1,0:T(8,128)(2,1)S(1)}, bf16[512,4096]{1,0:T(8,128)(2,1)}, u32[]{:S(2)}) copy-start(bf16[512,4096]{1,0:T(8,128)(2,1)} %get-tuple-element.8) | copy-start | bytes 12582916
  190.9 14.8 %slice-start.1 = ((s8[7340032]{0:T(1024)(128)(4,1)}), s8[4194304]{0:T(1024)(128)(4,1)S(1)}, s32[]{:S(2)}) async-start(s8[7340032]{0:T(1024)(128)(4,1)} %bitcast.13), calls=%async_computation.1 | async-start | bytes 8388608
  190.9 25.1 %slice-start.2 = ((s8[7340032]{0:T(1024)(128)(4,1)}), s8[4194304]{0:T(1024)(128)(4,1)S(1)}, s32[]{:S(2)}) async-start(s8[7340032]{0:T(1024)(128)(4,1)} %bitcast.15), calls=%async_computation.2 | async-start | bytes 8388608
  201.1 14.9 %slice-start.3 = ((s8[7340032]{0:T(1024)(128)(4,1)}), s8[3145728]{0:T(1024)(128)(4,1)S(1)}, s32[]{:S(2)}) async-start(s8[7340032]{0:T(1024)(128)(4,1)} %bitcast.15), calls=%async_computation.3 | async-start | bytes 6291456
  205.7 29.7 %slice-start.4 = ((s8[7340032]{0:T(1024)(128)(4,1)}), s8[4194304]{0:T(1024)(128)(4,1)S(1)}, s32[]{:S(2)}) async-start(s8[7340032]{0:T(1024)(128)(4,1)} %bitcast.17), calls=%async_computation.4 | async-start | bytes 8388608
  216.0 19.4 %slice-start.5 = ((s8[7340032]{0:T(1024)(128)(4,1)}), s8[3145728]{0:T(1024)(128)(4,1)S(1)}, s32[]{:S(2)}) async-start(s8[7340032]{0:T(1024)(128)(4,1)} %bitcast.17), calls=%async_computation.5 | async-start | bytes 6291456

commit v13 on v12

--- a/solution.py
+++ b/solution.py
@@ -485,6 +485,69 @@
     )(ta, tb)
 
 
+def gate_up_kernel(h_ref, go_ref, gp_ref, uo_ref, upv_ref, io_ref, it_ref, acc, tbuf):
+    k = pl.program_id(0)
+    tile = 128
+    chunk = 64
+    f32 = jnp.float32
+
+    @pl.when(k == 0)
+    def _():
+        acc[...] = jnp.zeros_like(acc)
+
+    def mix(i, carry):
+        r = pl.ds(pl.multiple_of(i * chunk, chunk), chunk)
+        for j, (on_ref, pv_ref) in enumerate(((go_ref, gp_ref), (uo_ref, upv_ref))):
+            on = on_ref[r, :].astype(f32)
+            pv = pv_ref[r, :].astype(f32)
+            tbuf[j, r, :] = (POLYAK * on + (1.0 - POLYAK) * pv).astype(tbuf.dtype)
+        return carry
+
+    lax.fori_loop(0, go_ref.shape[0] // chunk, mix, 0)
+
+    def mm(i, carry):
+        r = pl.ds(pl.multiple_of(i * tile, tile), tile)
+        hs = h_ref[r, :]
+        acc[0, r, :] += jnp.dot(hs, go_ref[...], preferred_element_type=f32)
+        acc[1, r, :] += jnp.dot(hs, tbuf[0], preferred_element_type=f32)
+        acc[2, r, :] += jnp.dot(hs, uo_ref[...], preferred_element_type=f32)
+        acc[3, r, :] += jnp.dot(hs, tbuf[1], preferred_element_type=f32)
+        return carry
+
+    lax.fori_loop(0, h_ref.shape[0] // tile, mm, 0)
+
+    @pl.when(k == pl.num_programs(0) - 1)
+    def _():
+        def finish(i, carry):
+            r = pl.ds(pl.multiple_of(i * chunk, chunk), chunk)
+            io_ref[r, :] = (jax.nn.silu(acc[0, r, :]) * acc[2, r, :]).astype(io_ref.dtype)
+            it_ref[r, :] = (jax.nn.silu(acc[1, r, :]) * acc[3, r, :]).astype(it_ref.dtype)
+            return carry
+
+        lax.fori_loop(0, io_ref.shape[0] // chunk, finish, 0)
+
+
+def gate_up(h_full, go, gp, uo, upv, kb):
+    tokens, kdim = h_full.shape
+    ff = go.shape[1]
+    wspec = pl.BlockSpec((kb, ff), lambda k: (k, 0))
+    ospec = pl.BlockSpec((tokens, ff), lambda k: (0, 0))
+    flops = 8 * tokens * kdim * ff
+    nbytes = 2 * (tokens * kdim + 4 * kdim * ff + 2 * tokens * ff)
+    return pl.pallas_call(
+        gate_up_kernel,
+        grid=(kdim // kb,),
+        out_shape=(jax.ShapeDtypeStruct((tokens, ff), jnp.bfloat16),) * 2,
+        in_specs=[pl.BlockSpec((tokens, kb), lambda k: (0, k))] + [wspec] * 4,
+        out_specs=[ospec, ospec],
+        scratch_shapes=[pltpu.VMEM((4, tokens, ff), jnp.float32),
+                        pltpu.VMEM((2, kb, ff), jnp.bfloat16)],
+        compiler_params=pltpu.CompilerParams(vmem_limit_bytes=48 * 1024 * 1024),
+        cost_estimate=pl.CostEstimate(flops=flops, bytes_accessed=nbytes,
+                                      transcendentals=2 * tokens * ff),
+    )(h_full, go, gp, uo, upv)
+
+
 def local(ndp, nmp, hidden_states, gate_online, up_online, down_online, gate_previous,
           up_previous, down_previous):
     if ndp == 8 and nmp == 16:
@@ -495,17 +558,8 @@
         gate_full, up_full, down_full = gather_weights_direct(gate_online, up_online,
                                                               down_online, ndp)
 
-    def pair(piece, previous):
-        target_piece = blend(piece, previous)
-        o = jnp.dot(features_all, piece, preferred_element_type=jnp.float32)
-        t = jnp.dot(features_all, target_piece, preferred_element_type=jnp.float32)
-        return o, t
-
-    gate_o, gate_t = pair(gate_full, gate_previous)
-    up_o, up_t = pair(up_full, up_previous)
-    inner_o = (jax.nn.silu(gate_o) * up_o).astype(jnp.bfloat16)
-    inner_t = (jax.nn.silu(gate_t) * up_t).astype(jnp.bfloat16)
-    inner_o, inner_t = lax.optimization_barrier((inner_o, inner_t))
+    inner_o, inner_t = gate_up(features_all, gate_full, gate_previous, up_full, up_previous,
+                               gate_online.shape[0])
     target_down = blend(down_full, down_previous)
     online_part = jnp.dot(inner_o, down_full, preferred_element_type=jnp.float32)
     target_part = jnp.dot(inner_t, target_down, preferred_element_type=jnp.float32)

time: 312 us -> 304 us (0.974)
  matrix products: 55.7 us -> 12.3 us
  Pallas kernels: 254 us -> 287 us
    dot_general x4 -> x0, matrix products: 34.9 us -> none  [the longest x2 20.1 us: pair(): t = jnp.dot(features_all, target_piece, preferred_element_type=jnp.float32)]
    pallas_call x0 -> x1, Pallas kernels: none -> 32.8 us  [gate_up(): pl.pallas_call(gate_up_kernel, grid=(kdim // kb,), out_shape=(jax.ShapeDt...]
    dot_general x1, matrix products: 11.4 us -> 6.23 us  [local(): jnp.dot(inner_t, target_down, preferred_element_type=jnp.float32)]
    dot_general x1, matrix products: 9.5 us -> 6.06 us  [local(): jnp.dot(inner_o, down_full, preferred_element_type=jnp.float32)]
where the time goes in v13:
time: 304 us
  Pallas kernels  287 us (94%)
  matrix products  12.3 us (4%)
  local copies, waits for them, and re-layouts  4.04 us (1%)
    pallas_call x1, Pallas kernels, gather_relay(): pl.pallas_call(relay_gather_kernel, out_shape=(jax.ShapeDtypeStruct((h.sh...  190 us
    pallas_call x1, Pallas kernels, split_reduce_scatter(): pl.pallas_call(split_reduce_kernel, out_shape=jax.ShapeDtypeStruct((n, t,...  63.6 us
    pallas_call x1, Pallas kernels, gate_up(): pl.pallas_call(gate_up_kernel, grid=(kdim // kb,), out_shape=(jax.ShapeDt...  32.8 us
    dot_general x1, matrix products, local(): jnp.dot(inner_t, target_down, preferred_element_type=jnp.float32)  6.23 us

profile of v13, /device:TPU:1, one launch (start us, length us, event | category | flops | bytes accessed | tf_op | source)
XLA Modules:
  0.0 303.6 jit_solution(3365363412745308186)
XLA Ops:
  0.6 190.2 %shard_map.86 = (bf16[512,4096]{1,0:T(8,128)(2,1)}, bf16[4096,896]{1,0:T(8,128)(2,1)}, bf16[4096,896]{1,0:T(8,128)(2,1)}, bf16[896,4096]{1,0:T(8,128)(2,1)}) custom-call(bf16[512,256]{1,0:T(8,128)(2,1)} %h_ref.1, bf16[512,896]{1,0:T(8,128)(2,1)} %g_ref.1, bf16[512,896]{1,0:T(8,128)(2,1)} %u_ref.1, bf16[896,512]{1,0:T(8,128)(2,1)} %dn_ref.1), custom_call_target="tpu_custom_call" | custom-call | tf_op jit(solution)/shard_map/pallas_call | solution.py:169
  190.9 0.0 copy-start
  190.9 2.2 copy-done
  193.1 0.0 copy-start.2
  193.1 32.8 %shard_map.87 = (bf16[512,896]{1,0:T(8,128)(2,1)S(1)}, bf16[512,896]{1,0:T(8,128)(2,1)S(1)}) custom-call(bf16[512,4096]{1,0:T(8,128)(2,1)S(1)} %copy-done, bf16[4096,896]{1,0:T(8,128)(2,1)} %get-tuple-element.9.go_ref, bf16[4096,896]{1,0:T(8,128)(2,1)} %gp_ref.1, bf16[4096,896]{1,0:T(8,128)(2,1)} %get-tuple-element.10.uo_ref, bf16[4096,896]{1,0:T(8,128)(2,1)} %upv_ref.1), custom_call_target="tpu_custom_call" | custom-call | flops 15032385536 | bytes 35389440 | tf_op jit(solution)/shard_map/pallas_call | solution.py:537
  225.8 0.0 copy-done.2
  225.8 0.0 copy-start.1
  225.9 6.1 %convolution_convert_fusion.ta_ref = bf16[512,4096]{1,0:T(8,128)(2,1)} fusion(bf16[512,896]{1,0:T(8,128)(2,1)S(1)} %get-tuple-element.11, bf16[896,4096]{1,0:T(8,128)(2,1)S(1)} %copy-done.2), kind=kOutput, calls=%fused_computation.5 | convolution fusion | flops 3760193536 | bytes 12451840 | tf_op jit(solution)/shard_map/dot_general | solution.py:564
  231.9 0.0 copy-done.1
  231.9 6.2 %fusion.3.tb_ref = bf16[512,4096]{1,0:T(8,128)(2,1)} fusion(bf16[512,896]{1,0:T(8,128)(2,1)S(1)} %get-tuple-element.13, bf16[896,4096]{1,0:T(8,128)(2,1)S(1)} %copy-done.1, bf16[896,4096]{1,0:T(8,128)(2,1)S(1)} %copy-done.2), kind=kOutput, calls=%fused_computation.4 | convolution fusion | flops 3782213632 | bytes 19791872 | tf_op jit(solution)/shard_map/dot_general | solution.py:565
  238.2 63.6 %shard_map.88 = bf16[2,512,256]{2,1,0:T(8,128)(2,1)} custom-call(bf16[512,4096]{1,0:T(8,128)(2,1)} %convolution_convert_fusion.ta_ref, bf16[512,4096]{1,0:T(8,128)(2,1)} %fusion.3.tb_ref), custom_call_target="tpu_custom_call" | custom-call | tf_op jit(solution)/shard_map/pallas_call | solution.py:461
  301.7 1.9 slice_bitcast_fusion
Async XLA Ops:
  190.9 2.2 copy-start
  193.1 32.8 %copy-start.2 = (bf16[896,4096]{1,0:T(8,128)(2,1)S(1)}, bf16[896,4096]{1,0:T(8,128)(2,1)}, u32[]{:S(2)}) copy-start(bf16[896,4096]{1,0:T(8,128)(2,1)} %get-tuple-element.12) | copy-start | bytes 22020100
  225.8 6.1 %copy-start.1 = (bf16[896,4096]{1,0:T(8,128)(2,1)S(1)}, bf16[896,4096]{1,0:T(8,128)(2,1)}, u32[]{:S(2)}) copy-start(bf16[896,4096]{1,0:T(8,128)(2,1)} %param.13) | copy-start | bytes 22020100

commit v14 on v13

--- a/solution.py
+++ b/solution.py
@@ -559,7 +559,7 @@
                                                               down_online, ndp)
 
     inner_o, inner_t = gate_up(features_all, gate_full, gate_previous, up_full, up_previous,
-                               gate_online.shape[0])
+                               2 * gate_online.shape[0])
     target_down = blend(down_full, down_previous)
     online_part = jnp.dot(inner_o, down_full, preferred_element_type=jnp.float32)
     target_part = jnp.dot(inner_t, target_down, preferred_element_type=jnp.float32)

time: 304 us -> 302 us (level)
  no operation moved by 1% of the time
where the time goes in v14:
time: 302 us
  Pallas kernels  285 us (94%)
  matrix products  12.3 us (4%)
  local copies, waits for them, and re-layouts  4.04 us (1%)
    pallas_call x1, Pallas kernels, gather_relay(): pl.pallas_call(relay_gather_kernel, out_shape=(jax.ShapeDtypeStruct((h.sh...  190 us
    pallas_call x1, Pallas kernels, split_reduce_scatter(): pl.pallas_call(split_reduce_kernel, out_shape=jax.ShapeDtypeStruct((n, t,...  63.5 us
    pallas_call x1, Pallas kernels, gate_up(): pl.pallas_call(gate_up_kernel, grid=(kdim // kb,), out_shape=(jax.ShapeDt...  30.9 us
    dot_general x1, matrix products, local(): jnp.dot(inner_t, target_down, preferred_element_type=jnp.float32)  6.23 us
    dot_general x1, matrix products, local(): jnp.dot(inner_o, down_full, preferred_element_type=jnp.float32)  6.06 us

profile of v14, /device:TPU:1, one launch (start us, length us, event | category | flops | bytes accessed | tf_op | source)
XLA Modules:
  0.0 301.6 jit_solution(14682493213390041733)
XLA Ops:
  0.6 190.2 %shard_map.86 = (bf16[512,4096]{1,0:T(8,128)(2,1)}, bf16[4096,896]{1,0:T(8,128)(2,1)}, bf16[4096,896]{1,0:T(8,128)(2,1)}, bf16[896,4096]{1,0:T(8,128)(2,1)}) custom-call(bf16[512,256]{1,0:T(8,128)(2,1)} %h_ref.1, bf16[512,896]{1,0:T(8,128)(2,1)} %g_ref.1, bf16[512,896]{1,0:T(8,128)(2,1)} %u_ref.1, bf16[896,512]{1,0:T(8,128)(2,1)} %dn_ref.1), custom_call_target="tpu_custom_call" | custom-call | tf_op jit(solution)/shard_map/pallas_call | solution.py:169
  190.9 0.0 copy-start
  190.9 2.2 copy-done
  193.1 0.0 copy-start.2
  193.1 30.9 %shard_map.87 = (bf16[512,896]{1,0:T(8,128)(2,1)S(1)}, bf16[512,896]{1,0:T(8,128)(2,1)S(1)}) custom-call(bf16[512,4096]{1,0:T(8,128)(2,1)S(1)} %copy-done, bf16[4096,896]{1,0:T(8,128)(2,1)} %get-tuple-element.9.go_ref, bf16[4096,896]{1,0:T(8,128)(2,1)} %gp_ref.1, bf16[4096,896]{1,0:T(8,128)(2,1)} %get-tuple-element.10.uo_ref, bf16[4096,896]{1,0:T(8,128)(2,1)} %upv_ref.1), custom_call_target="tpu_custom_call" | custom-call | flops 15032385536 | bytes 35389440 | tf_op jit(solution)/shard_map/pallas_call | solution.py:537
  223.9 0.0 copy-done.2
  223.9 0.0 copy-start.1
  224.0 6.1 %convolution_convert_fusion.ta_ref = bf16[512,4096]{1,0:T(8,128)(2,1)} fusion(bf16[512,896]{1,0:T(8,128)(2,1)S(1)} %get-tuple-element.11, bf16[896,4096]{1,0:T(8,128)(2,1)S(1)} %copy-done.2), kind=kOutput, calls=%fused_computation.5 | convolution fusion | flops 3760193536 | bytes 12451840 | tf_op jit(solution)/shard_map/dot_general | solution.py:564
  230.0 0.0 copy-done.1
  230.0 6.2 %fusion.3.tb_ref = bf16[512,4096]{1,0:T(8,128)(2,1)} fusion(bf16[512,896]{1,0:T(8,128)(2,1)S(1)} %get-tuple-element.13, bf16[896,4096]{1,0:T(8,128)(2,1)S(1)} %copy-done.1, bf16[896,4096]{1,0:T(8,128)(2,1)S(1)} %copy-done.2), kind=kOutput, calls=%fused_computation.4 | convolution fusion | flops 3782213632 | bytes 19791872 | tf_op jit(solution)/shard_map/dot_general | solution.py:565
  236.3 63.5 %shard_map.88 = bf16[2,512,256]{2,1,0:T(8,128)(2,1)} custom-call(bf16[512,4096]{1,0:T(8,128)(2,1)} %convolution_convert_fusion.ta_ref, bf16[512,4096]{1,0:T(8,128)(2,1)} %fusion.3.tb_ref), custom_call_target="tpu_custom_call" | custom-call | tf_op jit(solution)/shard_map/pallas_call | solution.py:461
  299.8 1.9 slice_bitcast_fusion
Async XLA Ops:
  190.9 2.2 copy-start
  193.1 30.9 %copy-start.2 = (bf16[896,4096]{1,0:T(8,128)(2,1)S(1)}, bf16[896,4096]{1,0:T(8,128)(2,1)}, u32[]{:S(2)}) copy-start(bf16[896,4096]{1,0:T(8,128)(2,1)} %get-tuple-element.12) | copy-start | bytes 22020100
  223.9 6.1 %copy-start.1 = (bf16[896,4096]{1,0:T(8,128)(2,1)S(1)}, bf16[896,4096]{1,0:T(8,128)(2,1)}, u32[]{:S(2)}) copy-start(bf16[896,4096]{1,0:T(8,128)(2,1)} %param.13) | copy-start | bytes 22020100

commit v15 on v14

--- a/solution.py
+++ b/solution.py
@@ -487,7 +487,7 @@
 
 def gate_up_kernel(h_ref, go_ref, gp_ref, uo_ref, upv_ref, io_ref, it_ref, acc, tbuf):
     k = pl.program_id(0)
-    tile = 128
+    tile = 256
     chunk = 64
     f32 = jnp.float32
 

time: 302 us -> 300 us (level)
  no operation moved by 1% of the time
where the time goes in v15:
time: 300 us
  Pallas kernels  283 us (94%)
  matrix products  12.3 us (4%)
  local copies, waits for them, and re-layouts  4.04 us (1%)
    pallas_call x1, Pallas kernels, gather_relay(): pl.pallas_call(relay_gather_kernel, out_shape=(jax.ShapeDtypeStruct((h.sh...  190 us
    pallas_call x1, Pallas kernels, split_reduce_scatter(): pl.pallas_call(split_reduce_kernel, out_shape=jax.ShapeDtypeStruct((n, t,...  63.6 us
    pallas_call x1, Pallas kernels, gate_up(): pl.pallas_call(gate_up_kernel, grid=(kdim // kb,), out_shape=(jax.ShapeDt...  29.3 us
    dot_general x1, matrix products, local(): jnp.dot(inner_t, target_down, preferred_element_type=jnp.float32)  6.23 us
    dot_general x1, matrix products, local(): jnp.dot(inner_o, down_full, preferred_element_type=jnp.float32)  6.06 us

profile of v15, /device:TPU:1, one launch (start us, length us, event | category | flops | bytes accessed | tf_op | source)
XLA Modules:
  0.0 300.1 jit_solution(11046132843620047870)
XLA Ops:
  0.6 190.2 %shard_map.86 = (bf16[512,4096]{1,0:T(8,128)(2,1)}, bf16[4096,896]{1,0:T(8,128)(2,1)}, bf16[4096,896]{1,0:T(8,128)(2,1)}, bf16[896,4096]{1,0:T(8,128)(2,1)}) custom-call(bf16[512,256]{1,0:T(8,128)(2,1)} %h_ref.1, bf16[512,896]{1,0:T(8,128)(2,1)} %g_ref.1, bf16[512,896]{1,0:T(8,128)(2,1)} %u_ref.1, bf16[896,512]{1,0:T(8,128)(2,1)} %dn_ref.1), custom_call_target="tpu_custom_call" | custom-call | tf_op jit(solution)/shard_map/pallas_call | solution.py:169
  190.9 0.0 copy-start
  190.9 2.2 copy-done
  193.1 0.0 copy-start.2
  193.1 29.3 %shard_map.87 = (bf16[512,896]{1,0:T(8,128)(2,1)S(1)}, bf16[512,896]{1,0:T(8,128)(2,1)S(1)}) custom-call(bf16[512,4096]{1,0:T(8,128)(2,1)S(1)} %copy-done, bf16[4096,896]{1,0:T(8,128)(2,1)} %get-tuple-element.9.go_ref, bf16[4096,896]{1,0:T(8,128)(2,1)} %gp_ref.1, bf16[4096,896]{1,0:T(8,128)(2,1)} %get-tuple-element.10.uo_ref, bf16[4096,896]{1,0:T(8,128)(2,1)} %upv_ref.1), custom_call_target="tpu_custom_call" | custom-call | flops 15032385536 | bytes 35389440 | tf_op jit(solution)/shard_map/pallas_call | solution.py:537
  222.3 0.0 copy-done.2
  222.4 0.0 copy-start.1
  222.4 6.1 %convolution_convert_fusion.ta_ref = bf16[512,4096]{1,0:T(8,128)(2,1)} fusion(bf16[512,896]{1,0:T(8,128)(2,1)S(1)} %get-tuple-element.11, bf16[896,4096]{1,0:T(8,128)(2,1)S(1)} %copy-done.2), kind=kOutput, calls=%fused_computation.5 | convolution fusion | flops 3760193536 | bytes 12451840 | tf_op jit(solution)/shard_map/dot_general | solution.py:564
  228.4 0.0 copy-done.1
  228.4 6.2 %fusion.3.tb_ref = bf16[512,4096]{1,0:T(8,128)(2,1)} fusion(bf16[512,896]{1,0:T(8,128)(2,1)S(1)} %get-tuple-element.13, bf16[896,4096]{1,0:T(8,128)(2,1)S(1)} %copy-done.1, bf16[896,4096]{1,0:T(8,128)(2,1)S(1)} %copy-done.2), kind=kOutput, calls=%fused_computation.4 | convolution fusion | flops 3782213632 | bytes 19791872 | tf_op jit(solution)/shard_map/dot_general | solution.py:565
  234.7 63.6 %shard_map.88 = bf16[2,512,256]{2,1,0:T(8,128)(2,1)} custom-call(bf16[512,4096]{1,0:T(8,128)(2,1)} %convolution_convert_fusion.ta_ref, bf16[512,4096]{1,0:T(8,128)(2,1)} %fusion.3.tb_ref), custom_call_target="tpu_custom_call" | custom-call | tf_op jit(solution)/shard_map/pallas_call | solution.py:461
  298.2 1.9 slice_bitcast_fusion
Async XLA Ops:
  190.9 2.2 copy-start
  193.1 29.3 %copy-start.2 = (bf16[896,4096]{1,0:T(8,128)(2,1)S(1)}, bf16[896,4096]{1,0:T(8,128)(2,1)}, u32[]{:S(2)}) copy-start(bf16[896,4096]{1,0:T(8,128)(2,1)} %get-tuple-element.12) | copy-start | bytes 22020100
  222.4 6.1 %copy-start.1 = (bf16[896,4096]{1,0:T(8,128)(2,1)S(1)}, bf16[896,4096]{1,0:T(8,128)(2,1)}, u32[]{:S(2)}) copy-start(bf16[896,4096]{1,0:T(8,128)(2,1)} %param.13) | copy-start | bytes 22020100

commit v16 on v15

--- a/solution.py
+++ b/solution.py
@@ -74,8 +74,9 @@
     )(g, u, dn)
 
 
-def relay_gather_kernel(h_ref, g_ref, u_ref, dn_ref, hf_ref, gf_ref, uf_ref, df_ref, send_sem,
-                        recv_sem, local_sem, hsend, hrecv):
+def relay_gather_kernel(h_ref, g_ref, u_ref, dn_ref, gp_ref, upv_ref, hf_ref, gf_ref, uf_ref,
+                        df_ref, pg_ref, pu_ref, send_sem, recv_sem, local_sem, hsend, hrecv,
+                        hv, wb, wsem):
     ndp = 8
     d = lax.axis_index("dp")
     m = lax.axis_index("mp")
@@ -147,6 +148,35 @@
         c[w, 0].wait_recv()
         c[w, 3].start()
         c[w, 4].start()
+
+    hlocal.wait()
+    for cp in hcopies:
+        cp.wait_recv()
+    hload = pltpu.make_async_copy(hf_ref, hv, wsem.at[2])
+    hload.start()
+    hload.wait()
+    pg_ref[...] = jnp.zeros_like(pg_ref)
+    pu_ref[...] = jnp.zeros_like(pu_ref)
+    kr = g_ref.shape[0]
+    tile = 256
+    for slot_i in range(ndp):
+        rows = pl.ds(slot_i * kr, kr)
+        lg = pltpu.make_async_copy(gp_ref.at[rows], wb.at[0], wsem.at[0])
+        lu = pltpu.make_async_copy(upv_ref.at[rows], wb.at[1], wsem.at[1])
+        lg.start()
+        lu.start()
+        lg.wait()
+        lu.wait()
+
+        def mm(i, carry, rows=rows):
+            r = pl.ds(pl.multiple_of(i * tile, tile), tile)
+            hs = hv[r, rows]
+            pg_ref[r, :] += jnp.dot(hs, wb[0], preferred_element_type=jnp.float32)
+            pu_ref[r, :] += jnp.dot(hs, wb[1], preferred_element_type=jnp.float32)
+            return carry
+
+        lax.fori_loop(0, hv.shape[0] // tile, mm, 0)
+
     for w in range(3):
         for k in (3, 4, 7):
             c[w, k].wait_recv()
@@ -154,32 +184,39 @@
         for k in range(8):
             c[w, k].wait_send()
         locals_[w].wait()
-    hlocal.wait()
     for cp in hcopies:
-        cp.wait()
-
-
-def gather_relay(h, g, u, dn, ndp):
+        cp.wait_send()
+
+
+def gather_relay(h, g, u, dn, gp, upv, ndp):
     any_spec = pl.BlockSpec(memory_space=pl.ANY)
     out_shape = (
         jax.ShapeDtypeStruct((g.shape[0] * ndp, g.shape[1]), g.dtype),
         jax.ShapeDtypeStruct((u.shape[0] * ndp, u.shape[1]), u.dtype),
         jax.ShapeDtypeStruct((dn.shape[0], dn.shape[1] * ndp), dn.dtype),
     )
+    tokens, ff = h.shape[0], g.shape[1]
+    prod = jax.ShapeDtypeStruct((tokens, ff), jnp.float32)
+    vspec = pl.BlockSpec(memory_space=pltpu.VMEM)
     return pl.pallas_call(
         relay_gather_kernel,
-        out_shape=(jax.ShapeDtypeStruct((h.shape[0], h.shape[1] * 16), h.dtype),) + out_shape,
-        in_specs=[any_spec] * 4,
-        out_specs=[any_spec] * 4,
+        out_shape=(jax.ShapeDtypeStruct((tokens, h.shape[1] * 16), h.dtype),) + out_shape
+        + (prod, prod),
+        in_specs=[any_spec] * 6,
+        out_specs=[any_spec] * 4 + [vspec] * 2,
         scratch_shapes=[
             pltpu.SemaphoreType.DMA((24,)),
             pltpu.SemaphoreType.DMA((24,)),
             pltpu.SemaphoreType.DMA((4,)),
             pltpu.SemaphoreType.DMA((15,)),
             pltpu.SemaphoreType.DMA((15,)),
+            pltpu.VMEM((tokens, h.shape[1] * 16), h.dtype),
+            pltpu.VMEM((2, g.shape[0], ff), g.dtype),
+            pltpu.SemaphoreType.DMA((3,)),
         ],
-        compiler_params=pltpu.CompilerParams(has_side_effects=True),
-    )(h, g, u, dn)
+        compiler_params=pltpu.CompilerParams(has_side_effects=True,
+                                             vmem_limit_bytes=48 * 1024 * 1024),
+    )(h, g, u, dn, gp, upv)
 
 
 def reduce_kernel(nmp, t_ref, o_ref, buf, send_sem, recv_sem, local_sem):
@@ -548,18 +585,72 @@
     )(h_full, go, gp, uo, upv)
 
 
+def gate_up_online_kernel(h_ref, go_ref, uo_ref, pg_ref, pu_ref, io_ref, it_ref, acc):
+    k = pl.program_id(0)
+    tile = 256
+    chunk = 64
+    f32 = jnp.float32
+
+    @pl.when(k == 0)
+    def _():
+        acc[...] = jnp.zeros_like(acc)
+
+    def mm(i, carry):
+        r = pl.ds(pl.multiple_of(i * tile, tile), tile)
+        hs = h_ref[r, :]
+        acc[0, r, :] += jnp.dot(hs, go_ref[...], preferred_element_type=f32)
+        acc[1, r, :] += jnp.dot(hs, uo_ref[...], preferred_element_type=f32)
+        return carry
+
+    lax.fori_loop(0, h_ref.shape[0] // tile, mm, 0)
+
+    @pl.when(k == pl.num_programs(0) - 1)
+    def _():
+        def finish(i, carry):
+            r = pl.ds(pl.multiple_of(i * chunk, chunk), chunk)
+            g_o = acc[0, r, :]
+            u_o = acc[1, r, :]
+            g_t = POLYAK * g_o + (1.0 - POLYAK) * pg_ref[r, :]
+            u_t = POLYAK * u_o + (1.0 - POLYAK) * pu_ref[r, :]
+            io_ref[r, :] = (jax.nn.silu(g_o) * u_o).astype(io_ref.dtype)
+            it_ref[r, :] = (jax.nn.silu(g_t) * u_t).astype(it_ref.dtype)
+            return carry
+
+        lax.fori_loop(0, io_ref.shape[0] // chunk, finish, 0)
+
+
+def gate_up_online(h_full, go, uo, pg, pu, kb):
+    tokens, kdim = h_full.shape
+    ff = go.shape[1]
+    wspec = pl.BlockSpec((kb, ff), lambda k: (k, 0))
+    ospec = pl.BlockSpec((tokens, ff), lambda k: (0, 0))
+    return pl.pallas_call(
+        gate_up_online_kernel,
+        grid=(kdim // kb,),
+        out_shape=(jax.ShapeDtypeStruct((tokens, ff), jnp.bfloat16),) * 2,
+        in_specs=[pl.BlockSpec((tokens, kb), lambda k: (0, k)), wspec, wspec, ospec, ospec],
+        out_specs=[ospec, ospec],
+        scratch_shapes=[pltpu.VMEM((2, tokens, ff), jnp.float32)],
+        compiler_params=pltpu.CompilerParams(vmem_limit_bytes=48 * 1024 * 1024),
+        cost_estimate=pl.CostEstimate(flops=4 * tokens * kdim * ff,
+                                      bytes_accessed=2 * (tokens * kdim + 2 * kdim * ff),
+                                      transcendentals=2 * tokens * ff),
+    )(h_full, go, uo, pg, pu)
+
+
 def local(ndp, nmp, hidden_states, gate_online, up_online, down_online, gate_previous,
           up_previous, down_previous):
+    kb = 2 * gate_online.shape[0]
     if ndp == 8 and nmp == 16:
-        features_all, gate_full, up_full, down_full = gather_relay(
-            hidden_states, gate_online, up_online, down_online, ndp)
+        features_all, gate_full, up_full, down_full, prev_g, prev_u = gather_relay(
+            hidden_states, gate_online, up_online, down_online, gate_previous, up_previous, ndp)
+        inner_o, inner_t = gate_up_online(features_all, gate_full, up_full, prev_g, prev_u, kb)
     else:
         features_all = lax.all_gather(hidden_states, "mp", axis=1, tiled=True)
         gate_full, up_full, down_full = gather_weights_direct(gate_online, up_online,
                                                               down_online, ndp)
-
-    inner_o, inner_t = gate_up(features_all, gate_full, gate_previous, up_full, up_previous,
-                               2 * gate_online.shape[0])
+        inner_o, inner_t = gate_up(features_all, gate_full, gate_previous, up_full, up_previous,
+                                   kb)
     target_down = blend(down_full, down_previous)
     online_part = jnp.dot(inner_o, down_full, preferred_element_type=jnp.float32)
     target_part = jnp.dot(inner_t, target_down, preferred_element_type=jnp.float32)

time: 300 us -> 298 us (level)
  Pallas kernels: 283 us -> 269 us
  matrix products: 12.3 us -> 20 us
  local copies, waits for them, and re-layouts: 4.04 us -> 7.83 us
    pallas_call x2, Pallas kernels: 220 us -> 205 us  [the longest x1 191 us: gather_relay(): pl.pallas_call(relay_gather_kernel, out_shape=(jax.ShapeDtypeStruct((toke...]
    dot_general x1, matrix products: 6.23 us -> 11 us  [local(): jnp.dot(inner_t, target_down, preferred_element_type=jnp.float32)]
    unnamed x6 -> x14, local copies, waits for them, and re-layouts: 2.19 us -> 5.98 us
    dot_general x1, matrix products: 6.06 us -> 9.09 us  [local(): jnp.dot(inner_o, down_full, preferred_element_type=jnp.float32)]
where the time goes in v16:
time: 298 us; the launch traced here: 297 us
  Pallas kernels  269 us (90%)
  matrix products  20 us (7%)
  local copies, waits for them, and re-layouts  7.83 us (3%)
    pallas_call x1, Pallas kernels, gather_relay(): pl.pallas_call(relay_gather_kernel, out_shape=(jax.ShapeDtypeStruct((toke...  191 us
    pallas_call x1, Pallas kernels, split_reduce_scatter(): pl.pallas_call(split_reduce_kernel, out_shape=jax.ShapeDtypeStruct((n, t,...  63.5 us
    pallas_call x1, Pallas kernels, gate_up_online(): pl.pallas_call(gate_up_online_kernel, grid=(kdim // kb,), out_shape=(jax....  14 us
    dot_general x1, matrix products, local(): jnp.dot(inner_t, target_down, preferred_element_type=jnp.float32)  11 us
    dot_general x1, matrix products, local(): jnp.dot(inner_o, down_full, preferred_element_type=jnp.float32)  9.09 us
    unnamed x14, local copies, waits for them, and re-layouts  5.98 us

profile of v16, /device:TPU:1, one launch (start us, length us, event | category | flops | bytes accessed | tf_op | source)
XLA Modules:
  0.0 297.2 jit_solution(17350126804266466001)
XLA Ops:
  0.6 0.0 copy-start
  0.6 1.2 copy-done
  1.8 0.0 copy-start.1
  1.8 1.2 copy-done.1
  3.0 0.0 copy-start.2
  3.0 1.2 copy-done.2
  4.2 0.0 copy-start.3
  4.2 0.9 copy-done.3
  5.1 0.0 slice-start
  5.1 191.2 %shard_map.86 = (bf16[512,4096]{1,0:T(8,128)(2,1)}, bf16[4096,896]{1,0:T(8,128)(2,1)}, bf16[4096,896]{1,0:T(8,128)(2,1)}, bf16[896,4096]{1,0:T(8,128)(2,1)}, f32[512,896]{1,0:T(8,128)S(1)}, /*index=5*/f32[512,896]{1,0:T(8,128)}) custom-call(bf16[512,256]{1,0:T(8,128)(2,1)S(1)} %copy-done.3, bf16[512,896]{1,0:T(8,128)(2,1)S(1)} %copy-done, ...), custom_call_target="tpu_custom_call" | custom-call | tf_op jit(solution)/shard_map/pallas_call | solution.py:201
  196.3 0.0 copy-start.4
  196.3 1.5 copy-done.4
  197.8 0.0 slice-start.1
  197.8 14.0 %shard_map.87 = (bf16[512,896]{1,0:T(8,128)(2,1)S(1)}, bf16[512,896]{1,0:T(8,128)(2,1)S(1)}) custom-call(bf16[512,4096]{1,0:T(8,128)(2,1)} %get-tuple-element.10.h_ref, bf16[4096,896]{1,0:T(8,128)(2,1)} %get-tuple-element.11.go_ref, bf16[4096,896]{1,0:T(8,128)(2,1)} %get-tuple-element.12.uo_ref, f32[512,896]{1,0:T(8,128)S(1)} %get-tuple-element.13.pg_ref, ...), custom_call_target="tpu_custom_call" | custom-call | flops 7516192768 | bytes 18874368 | tf_op jit(solution)/shard_map/pallas_call | solution.py:627
  211.8 9.1 %convolution_convert_fusion.ta_ref = bf16[512,4096]{1,0:T(8,128)(2,1)} fusion(bf16[512,896]{1,0:T(8,128)(2,1)S(1)} %get-tuple-element.15, bf16[896,4096]{1,0:T(8,128)(2,1)} %get-tuple-element.16), kind=kOutput, calls=%fused_computation.5 | convolution fusion | flops 3760193536 | bytes 12451840 | tf_op jit(solution)/shard_map/dot_general | solution.py:655
  220.9 0.0 slice-done
  220.9 0.0 slice-done.1
  220.9 11.0 %fusion.3.tb_ref = bf16[512,4096]{1,0:T(8,128)(2,1)} fusion(bf16[512,896]{1,0:T(8,128)(2,1)S(1)} %get-tuple-element.17, bf16[896,4096]{1,0:T(8,128)(2,1)S(1)} %bitcast.8, bf16[896,4096]{1,0:T(8,128)(2,1)} %get-tuple-element.16), kind=kOutput, calls=%fused_computation.4 | convolution fusion | flops 3782213632 | bytes 19791872 | tf_op jit(solution)/shard_map/dot_general | solution.py:656
  231.9 63.5 %shard_map.88 = bf16[2,512,256]{2,1,0:T(8,128)(2,1)} custom-call(bf16[512,4096]{1,0:T(8,128)(2,1)} %convolution_convert_fusion.ta_ref, bf16[512,4096]{1,0:T(8,128)(2,1)} %fusion.3.tb_ref), custom_call_target="tpu_custom_call" | custom-call | tf_op jit(solution)/shard_map/pallas_call | solution.py:498
  295.4 1.9 slice_bitcast_fusion
  (1 shorter events, 0.0 us)
Async XLA Ops:
  0.6 1.2 copy-start
  1.8 1.2 copy-start.1
  3.0 1.2 copy-start.2
  4.2 0.9 copy-start.3
  5.1 215.8 %slice-start = ((s8[7340032]{0:T(1024)(128)(4,1)}), s8[4194304]{0:T(1024)(128)(4,1)S(1)}, s32[]{:S(2)}) async-start(s8[7340032]{0:T(1024)(128)(4,1)} %bitcast.7), calls=%async_computation | async-start | bytes 8388608
  196.3 1.5 copy-start.4
  197.8 23.1 %slice-start.1 = ((s8[7340032]{0:T(1024)(128)(4,1)}), s8[3145728]{0:T(1024)(128)(4,1)S(1)}, s32[]{:S(2)}) async-start(s8[7340032]{0:T(1024)(128)(4,1)} %bitcast.7), calls=%async_computation.1 | async-start | bytes 6291456

commit v17 on v16

--- a/solution.py
+++ b/solution.py
@@ -638,6 +638,34 @@
     )(h_full, go, uo, pg, pu)
 
 
+def down_kernel(io_ref, it_ref, do_ref, dp_ref, oo_ref, ot_ref):
+    f32 = jnp.float32
+    wt = (POLYAK * do_ref[...].astype(f32)
+          + (1.0 - POLYAK) * dp_ref[...].astype(f32)).astype(do_ref.dtype)
+    oo_ref[...] = jnp.dot(io_ref[...], do_ref[...], preferred_element_type=f32).astype(oo_ref.dtype)
+    ot_ref[...] = jnp.dot(it_ref[...], wt, preferred_element_type=f32).astype(ot_ref.dtype)
+
+
+def down_products(inner_o, inner_t, down_full, down_previous, cb):
+    tokens, ff = inner_o.shape
+    width = down_full.shape[1]
+    ispec = pl.BlockSpec((tokens, ff), lambda j: (0, 0))
+    wspec = pl.BlockSpec((ff, cb), lambda j: (0, j))
+    ospec = pl.BlockSpec((tokens, cb), lambda j: (0, j))
+    return pl.pallas_call(
+        down_kernel,
+        grid=(width // cb,),
+        out_shape=(jax.ShapeDtypeStruct((tokens, width), jnp.bfloat16),) * 2,
+        in_specs=[ispec, ispec, wspec, wspec],
+        out_specs=[ospec, ospec],
+        compiler_params=pltpu.CompilerParams(vmem_limit_bytes=32 * 1024 * 1024),
+        cost_estimate=pl.CostEstimate(flops=4 * tokens * ff * width,
+                                      bytes_accessed=2 * (2 * tokens * ff + 2 * ff * width
+                                                          + 2 * tokens * width),
+                                      transcendentals=0),
+    )(inner_o, inner_t, down_full, down_previous)
+
+
 def local(ndp, nmp, hidden_states, gate_online, up_online, down_online, gate_previous,
           up_previous, down_previous):
     kb = 2 * gate_online.shape[0]
@@ -651,13 +679,14 @@
                                                               down_online, ndp)
         inner_o, inner_t = gate_up(features_all, gate_full, gate_previous, up_full, up_previous,
                                    kb)
-    target_down = blend(down_full, down_previous)
-    online_part = jnp.dot(inner_o, down_full, preferred_element_type=jnp.float32)
-    target_part = jnp.dot(inner_t, target_down, preferred_element_type=jnp.float32)
     if nmp == 16:
-        result = split_reduce_scatter(online_part.astype(jnp.bfloat16),
-                                      target_part.astype(jnp.bfloat16))
+        online_part, target_part = down_products(inner_o, inner_t, down_full, down_previous,
+                                                 down_online.shape[1])
+        result = split_reduce_scatter(online_part, target_part)
     else:
+        target_down = blend(down_full, down_previous)
+        online_part = jnp.dot(inner_o, down_full, preferred_element_type=jnp.float32)
+        target_part = jnp.dot(inner_t, target_down, preferred_element_type=jnp.float32)
         terms = jnp.stack([online_part, target_part], axis=0).astype(jnp.bfloat16)
         result = reduce_scatter(terms, nmp)
     return (result[0], result[1])

time: 298 us -> 294 us (0.987)
  matrix products: 20 us -> 0 us
  Pallas kernels: 269 us -> 281 us
  local copies, waits for them, and re-layouts: 7.83 us -> 11.7 us
    dot_general x2 -> x0, matrix products: 20 us -> none  [the longest x1 11 us: local(): jnp.dot(inner_t, target_down, preferred_element_type=jnp.float32)]
    pallas_call x0 -> x1, Pallas kernels: none -> 12.3 us  [down_products(): pl.pallas_call(down_kernel, grid=(width // cb,), out_shape=(jax.ShapeDtyp...]
    unnamed x14 -> x16, local copies, waits for them, and re-layouts: 5.98 us -> 9.89 us
where the time goes in v17:
time: 294 us; the launch traced here: 293 us
  Pallas kernels  281 us (96%)
  local copies, waits for them, and re-layouts  11.7 us (4%)
    pallas_call x1, Pallas kernels, gather_relay(): pl.pallas_call(relay_gather_kernel, out_shape=(jax.ShapeDtypeStruct((toke...  191 us
    pallas_call x1, Pallas kernels, split_reduce_scatter(): pl.pallas_call(split_reduce_kernel, out_shape=jax.ShapeDtypeStruct((n, t,...  63.5 us
    pallas_call x1, Pallas kernels, gate_up_online(): pl.pallas_call(gate_up_online_kernel, grid=(kdim // kb,), out_shape=(jax....  14 us
    pallas_call x1, Pallas kernels, down_products(): pl.pallas_call(down_kernel, grid=(width // cb,), out_shape=(jax.ShapeDtyp...  12.3 us
    unnamed x16, local copies, waits for them, and re-layouts  9.89 us

profile of v17, /device:TPU:1, one launch (start us, length us, event | category | flops | bytes accessed | tf_op | source)
XLA Modules:
  0.0 293.5 jit_solution(4072313576190831602)
XLA Ops:
  0.6 0.0 copy-start.2
  0.6 1.2 copy-done.2
  1.8 0.0 copy-start.3
  1.8 1.2 copy-done.3
  3.0 0.0 copy-start.4
  3.0 1.2 copy-done.4
  4.2 0.0 copy-start.5
  4.2 0.9 copy-done.5
  5.1 191.2 %shard_map.86 = (bf16[512,4096]{1,0:T(8,128)(2,1)}, bf16[4096,896]{1,0:T(8,128)(2,1)}, bf16[4096,896]{1,0:T(8,128)(2,1)}, bf16[896,4096]{1,0:T(8,128)(2,1)}, f32[512,896]{1,0:T(8,128)S(1)}, /*index=5*/f32[512,896]{1,0:T(8,128)}) custom-call(bf16[512,256]{1,0:T(8,128)(2,1)S(1)} %copy-done.5, bf16[512,896]{1,0:T(8,128)(2,1)S(1)} %copy-done.2, ...), custom_call_target="tpu_custom_call" | custom-call | tf_op jit(solution)/shard_map/pallas_call | solution.py:201
  196.3 0.0 copy-start.7
  196.3 1.5 copy-done.7
  197.8 0.0 copy-start.6
  197.8 14.0 %shard_map.87 = (bf16[512,896]{1,0:T(8,128)(2,1)S(1)}, bf16[512,896]{1,0:T(8,128)(2,1)S(1)}) custom-call(bf16[512,4096]{1,0:T(8,128)(2,1)} %get-tuple-element.12.h_ref, bf16[4096,896]{1,0:T(8,128)(2,1)} %get-tuple-element.13.go_ref, bf16[4096,896]{1,0:T(8,128)(2,1)} %get-tuple-element.14.uo_ref, f32[512,896]{1,0:T(8,128)S(1)} %get-tuple-element.15.pg_ref, ...), custom_call_target="tpu_custom_call" | custom-call | flops 7516192768 | bytes 18874368 | tf_op jit(solution)/shard_map/pallas_call | solution.py:627
  211.8 0.0 copy-done.6
  211.8 12.3 %shard_map.88 = (bf16[512,4096]{1,0:T(8,128)(2,1)S(1)}, bf16[512,4096]{1,0:T(8,128)(2,1)S(1)}) custom-call(bf16[512,896]{1,0:T(8,128)(2,1)S(1)} %get-tuple-element.17.io_ref, bf16[512,896]{1,0:T(8,128)(2,1)S(1)} %get-tuple-element.18.it_ref, bf16[896,4096]{1,0:T(8,128)(2,1)S(1)} %copy-done.6, bf16[896,4096]{1,0:T(8,128)(2,1)} %dp_ref.1), custom_call_target="tpu_custom_call" | custom-call | flops 7516192768 | bytes 24903680 | tf_op jit(solution)/shard_map/pallas_call | solution.py:655
  224.1 0.0 copy-start
  224.1 1.9 copy-done
  226.1 0.0 copy-start.1
  226.1 2.0 copy-done.1
  228.1 63.5 %shard_map.89 = bf16[2,512,256]{2,1,0:T(8,128)(2,1)} custom-call(bf16[512,4096]{1,0:T(8,128)(2,1)} %copy-done, bf16[512,4096]{1,0:T(8,128)(2,1)} %copy-done.1), custom_call_target="tpu_custom_call" | custom-call | tf_op jit(solution)/shard_map/pallas_call | solution.py:498
  291.6 1.9 slice_bitcast_fusion
Async XLA Ops:
  0.6 1.2 copy-start.2
  1.8 1.2 copy-start.3
  3.0 1.2 copy-start.4
  4.2 0.9 copy-start.5
  196.3 1.5 copy-start.7
  197.8 14.0 %copy-start.6 = (bf16[896,4096]{1,0:T(8,128)(2,1)S(1)}, bf16[896,4096]{1,0:T(8,128)(2,1)}, u32[]{:S(2)}) copy-start(bf16[896,4096]{1,0:T(8,128)(2,1)} %get-tuple-element.19.do_ref) | copy-start | bytes 22020100
  224.1 2.0 copy-start
  226.1 2.0 copy-start.1

commit v18 on v17

--- a/solution.py
+++ b/solution.py
@@ -75,8 +75,8 @@
 
 
 def relay_gather_kernel(h_ref, g_ref, u_ref, dn_ref, gp_ref, upv_ref, hf_ref, gf_ref, uf_ref,
-                        df_ref, pg_ref, pu_ref, send_sem, recv_sem, local_sem, hsend, hrecv,
-                        hv, wb, wsem):
+                        df_ref, io_ref, it_ref, send_sem, recv_sem, local_sem, hsend, hrecv,
+                        hv, wb, wsem, acc):
     ndp = 8
     d = lax.axis_index("dp")
     m = lax.axis_index("mp")
@@ -152,38 +152,63 @@
     hlocal.wait()
     for cp in hcopies:
         cp.wait_recv()
+    for w in range(3):
+        locals_[w].wait()
     hload = pltpu.make_async_copy(hf_ref, hv, wsem.at[2])
     hload.start()
     hload.wait()
-    pg_ref[...] = jnp.zeros_like(pg_ref)
-    pu_ref[...] = jnp.zeros_like(pu_ref)
+    acc[...] = jnp.zeros_like(acc)
     kr = g_ref.shape[0]
     tile = 256
-    for slot_i in range(ndp):
-        rows = pl.ds(slot_i * kr, kr)
-        lg = pltpu.make_async_copy(gp_ref.at[rows], wb.at[0], wsem.at[0])
-        lu = pltpu.make_async_copy(upv_ref.at[rows], wb.at[1], wsem.at[1])
-        lg.start()
-        lu.start()
-        lg.wait()
-        lu.wait()
-
-        def mm(i, carry, rows=rows):
+
+    def products(a_ref, b_ref, idx, first):
+        rows = pl.ds(pl.multiple_of(idx * kr, kr), kr)
+        la = pltpu.make_async_copy(a_ref.at[rows], wb.at[0], wsem.at[0])
+        lb = pltpu.make_async_copy(b_ref.at[rows], wb.at[1], wsem.at[1])
+        la.start()
+        lb.start()
+        la.wait()
+        lb.wait()
+
+        def mm(i, carry):
             r = pl.ds(pl.multiple_of(i * tile, tile), tile)
             hs = hv[r, rows]
-            pg_ref[r, :] += jnp.dot(hs, wb[0], preferred_element_type=jnp.float32)
-            pu_ref[r, :] += jnp.dot(hs, wb[1], preferred_element_type=jnp.float32)
+            acc[first, r, :] += jnp.dot(hs, wb[0], preferred_element_type=jnp.float32)
+            acc[first + 1, r, :] += jnp.dot(hs, wb[1], preferred_element_type=jnp.float32)
             return carry
 
         lax.fori_loop(0, hv.shape[0] // tile, mm, 0)
+
+    def prev_slot(i, carry):
+        products(gp_ref, upv_ref, i, 2)
+        return carry
+
+    lax.fori_loop(0, ndp, prev_slot, 0)
+    for idx in (d, partner, prv, nxt, far):
+        products(gf_ref, uf_ref, idx, 0)
 
     for w in range(3):
         for k in (3, 4, 7):
             c[w, k].wait_recv()
+    for idx in ((partner + 2) % ndp, (partner + ndp - 2) % ndp, (partner + 4) % ndp):
+        products(gf_ref, uf_ref, idx, 0)
+
+    chunk = 64
+
+    def finish(i, carry):
+        r = pl.ds(pl.multiple_of(i * chunk, chunk), chunk)
+        g_o = acc[0, r, :]
+        u_o = acc[1, r, :]
+        g_t = POLYAK * g_o + (1.0 - POLYAK) * acc[2, r, :]
+        u_t = POLYAK * u_o + (1.0 - POLYAK) * acc[3, r, :]
+        io_ref[r, :] = (jax.nn.silu(g_o) * u_o).astype(io_ref.dtype)
+        it_ref[r, :] = (jax.nn.silu(g_t) * u_t).astype(it_ref.dtype)
+        return carry
+
+    lax.fori_loop(0, io_ref.shape[0] // chunk, finish, 0)
     for w in range(3):
         for k in range(8):
             c[w, k].wait_send()
-        locals_[w].wait()
     for cp in hcopies:
         cp.wait_send()
 
@@ -196,7 +221,7 @@
         jax.ShapeDtypeStruct((dn.shape[0], dn.shape[1] * ndp), dn.dtype),
     )
     tokens, ff = h.shape[0], g.shape[1]
-    prod = jax.ShapeDtypeStruct((tokens, ff), jnp.float32)
+    prod = jax.ShapeDtypeStruct((tokens, ff), jnp.bfloat16)
     vspec = pl.BlockSpec(memory_space=pltpu.VMEM)
     return pl.pallas_call(
         relay_gather_kernel,
@@ -213,6 +238,7 @@
             pltpu.VMEM((tokens, h.shape[1] * 16), h.dtype),
             pltpu.VMEM((2, g.shape[0], ff), g.dtype),
             pltpu.SemaphoreType.DMA((3,)),
+            pltpu.VMEM((4, tokens, ff), jnp.float32),
         ],
         compiler_params=pltpu.CompilerParams(has_side_effects=True,
                                              vmem_limit_bytes=48 * 1024 * 1024),
@@ -670,9 +696,8 @@
           up_previous, down_previous):
     kb = 2 * gate_online.shape[0]
     if ndp == 8 and nmp == 16:
-        features_all, gate_full, up_full, down_full, prev_g, prev_u = gather_relay(
+        _, _, _, down_full, inner_o, inner_t = gather_relay(
             hidden_states, gate_online, up_online, down_online, gate_previous, up_previous, ndp)
-        inner_o, inner_t = gate_up_online(features_all, gate_full, up_full, prev_g, prev_u, kb)
     else:
         features_all = lax.all_gather(hidden_states, "mp", axis=1, tiled=True)
         gate_full, up_full, down_full = gather_weights_direct(gate_online, up_online,

time: 294 us -> 290 us (0.986)
  Pallas kernels: 281 us -> 275 us
    pallas_call x1 -> x0, Pallas kernels: 14 us -> none  [gate_up_online(): pl.pallas_call(gate_up_online_kernel, grid=(kdim // kb,), out_shape=(jax....]
    pallas_call x1, Pallas kernels: 191 us -> 199 us  [gather_relay(): pl.pallas_call(relay_gather_kernel, out_shape=(jax.ShapeDtypeStruct((toke...]
    unnamed x16 -> x14, local copies, waits for them, and re-layouts: 9.89 us -> 11.5 us
where the time goes in v18:
time: 290 us; the launch traced here: 289 us
  Pallas kernels  275 us (95%)
  local copies, waits for them, and re-layouts  13.3 us (5%)
    pallas_call x1, Pallas kernels, gather_relay(): pl.pallas_call(relay_gather_kernel, out_shape=(jax.ShapeDtypeStruct((toke...  199 us
    pallas_call x1, Pallas kernels, split_reduce_scatter(): pl.pallas_call(split_reduce_kernel, out_shape=jax.ShapeDtypeStruct((n, t,...  63.6 us
    pallas_call x1, Pallas kernels, down_products(): pl.pallas_call(down_kernel, grid=(width // cb,), out_shape=(jax.ShapeDtyp...  12.3 us
    unnamed x14, local copies, waits for them, and re-layouts  11.5 us

profile of v18, /device:TPU:1, one launch (start us, length us, event | category | flops | bytes accessed | tf_op | source)
XLA Modules:
  0.0 289.1 jit_solution(6783988053534906717)
XLA Ops:
  0.6 0.0 copy-start.2
  0.6 1.2 copy-done.2
  1.8 0.0 copy-start.3
  1.8 1.2 copy-done.3
  3.0 0.0 copy-start.4
  3.0 1.2 copy-done.4
  4.2 0.0 copy-start.5
  4.2 0.9 copy-done.5
  5.1 199.2 %shard_map.86 = (bf16[512,4096]{1,0:T(8,128)(2,1)}, bf16[4096,896]{1,0:T(8,128)(2,1)}, bf16[4096,896]{1,0:T(8,128)(2,1)}, bf16[896,4096]{1,0:T(8,128)(2,1)}, bf1...) custom-call(bf16[512,256]{1,0:T(8,128)(2,1)S(1)} %copy-done.5, bf16[512,896]{1,0:T(8,128)(2,1)S(1)} %copy-done.2, ...), custom_call_target="tpu_custom_call" | custom-call | tf_op jit(solution)/shard_map/pallas_call | solution.py:226
  204.3 0.0 copy-start.6
  204.4 3.1 %copy-done.6 = bf16[896,4096]{1,0:T(8,128)(2,1)S(1)} copy-done((bf16[896,4096]{1,0:T(8,128)(2,1)S(1)}, bf16[896,4096]{1,0:T(8,128)(2,1)}, u32[]{:S(2)}) %copy-start.6) | copy-done | bytes 7340056
  207.4 12.3 %shard_map.87 = (bf16[512,4096]{1,0:T(8,128)(2,1)S(1)}, bf16[512,4096]{1,0:T(8,128)(2,1)S(1)}) custom-call(bf16[512,896]{1,0:T(8,128)(2,1)S(1)} %get-tuple-element.7.io_ref, bf16[512,896]{1,0:T(8,128)(2,1)S(1)} %get-tuple-element.8.it_ref, bf16[896,4096]{1,0:T(8,128)(2,1)S(1)} %copy-done.6, bf16[896,4096]{1,0:T(8,128)(2,1)} %dp_ref.1), custom_call_target="tpu_custom_call" | custom-call | flops 7516192768 | bytes 24903680 | tf_op jit(solution)/shard_map/pallas_call | solution.py:681
  219.7 0.0 copy-start
  219.8 1.9 copy-done
  221.7 0.0 copy-start.1
  221.7 2.0 copy-done.1
  223.7 63.6 %shard_map.88 = bf16[2,512,256]{2,1,0:T(8,128)(2,1)} custom-call(bf16[512,4096]{1,0:T(8,128)(2,1)} %copy-done, bf16[512,4096]{1,0:T(8,128)(2,1)} %copy-done.1), custom_call_target="tpu_custom_call" | custom-call | tf_op jit(solution)/shard_map/pallas_call | solution.py:524
  287.2 1.9 slice_bitcast_fusion
Async XLA Ops:
  0.6 1.2 copy-start.2
  1.8 1.2 copy-start.3
  3.0 1.2 copy-start.4
  4.2 0.9 copy-start.5
  204.3 3.1 %copy-start.6 = (bf16[896,4096]{1,0:T(8,128)(2,1)S(1)}, bf16[896,4096]{1,0:T(8,128)(2,1)}, u32[]{:S(2)}) copy-start(bf16[896,4096]{1,0:T(8,128)(2,1)} %get-tuple-element.9.do_ref) | copy-start | bytes 22020100
  219.7 1.9 copy-start
  221.7 2.0 copy-start.1

commit v19 on v18

--- a/solution.py
+++ b/solution.py
@@ -188,9 +188,12 @@
         products(gf_ref, uf_ref, idx, 0)
 
     for w in range(3):
-        for k in (3, 4, 7):
-            c[w, k].wait_recv()
-    for idx in ((partner + 2) % ndp, (partner + ndp - 2) % ndp, (partner + 4) % ndp):
+        c[w, 7].wait_recv()
+    products(gf_ref, uf_ref, (partner + 4) % ndp, 0)
+    for w in range(3):
+        c[w, 3].wait_recv()
+        c[w, 4].wait_recv()
+    for idx in ((partner + 2) % ndp, (partner + ndp - 2) % ndp):
         products(gf_ref, uf_ref, idx, 0)
 
     chunk = 64

time: 290 us -> 290 us (level)
  no operation moved by 1% of the time
where the time goes in v19:
time: 290 us; the launch traced here: 289 us
  Pallas kernels  275 us (95%)
  local copies, waits for them, and re-layouts  13.3 us (5%)
    pallas_call x1, Pallas kernels, gather_relay(): pl.pallas_call(relay_gather_kernel, out_shape=(jax.ShapeDtypeStruct((toke...  199 us
    pallas_call x1, Pallas kernels, split_reduce_scatter(): pl.pallas_call(split_reduce_kernel, out_shape=jax.ShapeDtypeStruct((n, t,...  63.6 us
    pallas_call x1, Pallas kernels, down_products(): pl.pallas_call(down_kernel, grid=(width // cb,), out_shape=(jax.ShapeDtyp...  12.3 us
    unnamed x14, local copies, waits for them, and re-layouts  11.5 us

profile of v19, /device:TPU:1, one launch (start us, length us, event | category | flops | bytes accessed | tf_op | source)
XLA Modules:
  0.0 289.3 jit_solution(80351600794487259)
XLA Ops:
  0.6 0.0 copy-start.2
  0.6 1.2 copy-done.2
  1.8 0.0 copy-start.3
  1.8 1.2 copy-done.3
  3.0 0.0 copy-start.4
  3.0 1.2 copy-done.4
  4.2 0.0 copy-start.5
  4.2 0.9 copy-done.5
  5.1 199.5 %shard_map.86 = (bf16[512,4096]{1,0:T(8,128)(2,1)}, bf16[4096,896]{1,0:T(8,128)(2,1)}, bf16[4096,896]{1,0:T(8,128)(2,1)}, bf16[896,4096]{1,0:T(8,128)(2,1)}, bf1...) custom-call(bf16[512,256]{1,0:T(8,128)(2,1)S(1)} %copy-done.5, bf16[512,896]{1,0:T(8,128)(2,1)S(1)} %copy-done.2, ...), custom_call_target="tpu_custom_call" | custom-call | tf_op jit(solution)/shard_map/pallas_call | solution.py:229
  204.6 0.0 copy-start.6
  204.6 3.1 %copy-done.6 = bf16[896,4096]{1,0:T(8,128)(2,1)S(1)} copy-done((bf16[896,4096]{1,0:T(8,128)(2,1)S(1)}, bf16[896,4096]{1,0:T(8,128)(2,1)}, u32[]{:S(2)}) %copy-start.6) | copy-done | bytes 7340056
  207.7 12.3 %shard_map.87 = (bf16[512,4096]{1,0:T(8,128)(2,1)S(1)}, bf16[512,4096]{1,0:T(8,128)(2,1)S(1)}) custom-call(bf16[512,896]{1,0:T(8,128)(2,1)S(1)} %get-tuple-element.7.io_ref, bf16[512,896]{1,0:T(8,128)(2,1)S(1)} %get-tuple-element.8.it_ref, bf16[896,4096]{1,0:T(8,128)(2,1)S(1)} %copy-done.6, bf16[896,4096]{1,0:T(8,128)(2,1)} %dp_ref.1), custom_call_target="tpu_custom_call" | custom-call | flops 7516192768 | bytes 24903680 | tf_op jit(solution)/shard_map/pallas_call | solution.py:684
  220.0 0.0 copy-start
  220.0 1.9 copy-done
  221.9 0.0 copy-start.1
  221.9 2.0 copy-done.1
  223.9 63.6 %shard_map.88 = bf16[2,512,256]{2,1,0:T(8,128)(2,1)} custom-call(bf16[512,4096]{1,0:T(8,128)(2,1)} %copy-done, bf16[512,4096]{1,0:T(8,128)(2,1)} %copy-done.1), custom_call_target="tpu_custom_call" | custom-call | tf_op jit(solution)/shard_map/pallas_call | solution.py:527
  287.5 1.9 slice_bitcast_fusion
Async XLA Ops:
  0.6 1.2 copy-start.2
  1.8 1.2 copy-start.3
  3.0 1.2 copy-start.4
  4.2 0.9 copy-start.5
  204.6 3.1 %copy-start.6 = (bf16[896,4096]{1,0:T(8,128)(2,1)S(1)}, bf16[896,4096]{1,0:T(8,128)(2,1)}, u32[]{:S(2)}) copy-start(bf16[896,4096]{1,0:T(8,128)(2,1)} %get-tuple-element.9.do_ref) | copy-start | bytes 22020100
  220.0 1.9 copy-start
  221.9 2.0 copy-start.1

commit v20 on v19

--- a/solution.py
+++ b/solution.py
@@ -709,7 +709,7 @@
                                    kb)
     if nmp == 16:
         online_part, target_part = down_products(inner_o, inner_t, down_full, down_previous,
-                                                 down_online.shape[1])
+                                                 2 * down_online.shape[1])
         result = split_reduce_scatter(online_part, target_part)
     else:
         target_down = blend(down_full, down_previous)

time: 290 us -> 290 us (level)
  no operation moved by 1% of the time
where the time goes in v20:
time: 290 us; the launch traced here: 289 us
  Pallas kernels  275 us (95%)
  local copies, waits for them, and re-layouts  13.3 us (5%)
    pallas_call x1, Pallas kernels, gather_relay(): pl.pallas_call(relay_gather_kernel, out_shape=(jax.ShapeDtypeStruct((toke...  199 us
    pallas_call x1, Pallas kernels, split_reduce_scatter(): pl.pallas_call(split_reduce_kernel, out_shape=jax.ShapeDtypeStruct((n, t,...  63.6 us
    pallas_call x1, Pallas kernels, down_products(): pl.pallas_call(down_kernel, grid=(width // cb,), out_shape=(jax.ShapeDtyp...  11.8 us
    unnamed x14, local copies, waits for them, and re-layouts  11.5 us

profile of v20, /device:TPU:1, one launch (start us, length us, event | category | flops | bytes accessed | tf_op | source)
XLA Modules:
  0.0 288.8 jit_solution(7446760888875838552)
XLA Ops:
  0.6 0.0 copy-start.2
  0.6 1.2 copy-done.2
  1.8 0.0 copy-start.3
  1.8 1.2 copy-done.3
  3.0 0.0 copy-start.4
  3.0 1.2 copy-done.4
  4.2 0.0 copy-start.5
  4.2 0.9 copy-done.5
  5.1 199.5 %shard_map.86 = (bf16[512,4096]{1,0:T(8,128)(2,1)}, bf16[4096,896]{1,0:T(8,128)(2,1)}, bf16[4096,896]{1,0:T(8,128)(2,1)}, bf16[896,4096]{1,0:T(8,128)(2,1)}, bf1...) custom-call(bf16[512,256]{1,0:T(8,128)(2,1)S(1)} %copy-done.5, bf16[512,896]{1,0:T(8,128)(2,1)S(1)} %copy-done.2, ...), custom_call_target="tpu_custom_call" | custom-call | tf_op jit(solution)/shard_map/pallas_call | solution.py:229
  204.6 0.0 copy-start.6
  204.6 3.1 %copy-done.6 = bf16[896,4096]{1,0:T(8,128)(2,1)S(1)} copy-done((bf16[896,4096]{1,0:T(8,128)(2,1)S(1)}, bf16[896,4096]{1,0:T(8,128)(2,1)}, u32[]{:S(2)}) %copy-start.6) | copy-done | bytes 7340056
  207.7 11.8 %shard_map.87 = (bf16[512,4096]{1,0:T(8,128)(2,1)S(1)}, bf16[512,4096]{1,0:T(8,128)(2,1)S(1)}) custom-call(bf16[512,896]{1,0:T(8,128)(2,1)S(1)} %get-tuple-element.7.io_ref, bf16[512,896]{1,0:T(8,128)(2,1)S(1)} %get-tuple-element.8.it_ref, bf16[896,4096]{1,0:T(8,128)(2,1)S(1)} %copy-done.6, bf16[896,4096]{1,0:T(8,128)(2,1)} %dp_ref.1), custom_call_target="tpu_custom_call" | custom-call | flops 7516192768 | bytes 24903680 | tf_op jit(solution)/shard_map/pallas_call | solution.py:684
  219.5 0.0 copy-start
  219.5 1.9 copy-done
  221.4 0.0 copy-start.1
  221.4 2.0 copy-done.1
  223.4 63.6 %shard_map.88 = bf16[2,512,256]{2,1,0:T(8,128)(2,1)} custom-call(bf16[512,4096]{1,0:T(8,128)(2,1)} %copy-done, bf16[512,4096]{1,0:T(8,128)(2,1)} %copy-done.1), custom_call_target="tpu_custom_call" | custom-call | tf_op jit(solution)/shard_map/pallas_call | solution.py:527
  286.9 1.9 slice_bitcast_fusion
Async XLA Ops:
  0.6 1.2 copy-start.2
  1.8 1.2 copy-start.3
  3.0 1.2 copy-start.4
  4.2 0.9 copy-start.5
  204.6 3.1 %copy-start.6 = (bf16[896,4096]{1,0:T(8,128)(2,1)S(1)}, bf16[896,4096]{1,0:T(8,128)(2,1)}, u32[]{:S(2)}) copy-start(bf16[896,4096]{1,0:T(8,128)(2,1)} %get-tuple-element.9.do_ref) | copy-start | bytes 22020100
  219.5 1.9 copy-start
  221.4 2.0 copy-start.1

commit v21 on v20

--- a/solution.py
+++ b/solution.py
@@ -159,7 +159,7 @@
     hload.wait()
     acc[...] = jnp.zeros_like(acc)
     kr = g_ref.shape[0]
-    tile = 256
+    tile = 512
 
     def products(a_ref, b_ref, idx, first):
         rows = pl.ds(pl.multiple_of(idx * kr, kr), kr)

time: 290 us -> 289 us (level)
  no operation moved by 1% of the time
where the time goes in v21:
time: 289 us; the launch traced here: 288 us
  Pallas kernels  274 us (95%)
  local copies, waits for them, and re-layouts  13.3 us (5%)
    pallas_call x1, Pallas kernels, gather_relay(): pl.pallas_call(relay_gather_kernel, out_shape=(jax.ShapeDtypeStruct((toke...  199 us
    pallas_call x1, Pallas kernels, split_reduce_scatter(): pl.pallas_call(split_reduce_kernel, out_shape=jax.ShapeDtypeStruct((n, t,...  63.6 us
    pallas_call x1, Pallas kernels, down_products(): pl.pallas_call(down_kernel, grid=(width // cb,), out_shape=(jax.ShapeDtyp...  11.8 us
    unnamed x14, local copies, waits for them, and re-layouts  11.5 us

profile of v21, /device:TPU:1, one launch (start us, length us, event | category | flops | bytes accessed | tf_op | source)
XLA Modules:
  0.0 288.1 jit_solution(12710461900195112738)
XLA Ops:
  0.6 0.0 copy-start.2
  0.6 1.2 copy-done.2
  1.8 0.0 copy-start.3
  1.8 1.2 copy-done.3
  3.0 0.0 copy-start.4
  3.0 1.2 copy-done.4
  4.2 0.0 copy-start.5
  4.2 0.9 copy-done.5
  5.1 198.8 %shard_map.86 = (bf16[512,4096]{1,0:T(8,128)(2,1)}, bf16[4096,896]{1,0:T(8,128)(2,1)}, bf16[4096,896]{1,0:T(8,128)(2,1)}, bf16[896,4096]{1,0:T(8,128)(2,1)}, bf1...) custom-call(bf16[512,256]{1,0:T(8,128)(2,1)S(1)} %copy-done.5, bf16[512,896]{1,0:T(8,128)(2,1)S(1)} %copy-done.2, ...), custom_call_target="tpu_custom_call" | custom-call | tf_op jit(solution)/shard_map/pallas_call | solution.py:229
  203.9 0.0 copy-start.6
  203.9 3.1 %copy-done.6 = bf16[896,4096]{1,0:T(8,128)(2,1)S(1)} copy-done((bf16[896,4096]{1,0:T(8,128)(2,1)S(1)}, bf16[896,4096]{1,0:T(8,128)(2,1)}, u32[]{:S(2)}) %copy-start.6) | copy-done | bytes 7340056
  207.0 11.8 %shard_map.87 = (bf16[512,4096]{1,0:T(8,128)(2,1)S(1)}, bf16[512,4096]{1,0:T(8,128)(2,1)S(1)}) custom-call(bf16[512,896]{1,0:T(8,128)(2,1)S(1)} %get-tuple-element.7.io_ref, bf16[512,896]{1,0:T(8,128)(2,1)S(1)} %get-tuple-element.8.it_ref, bf16[896,4096]{1,0:T(8,128)(2,1)S(1)} %copy-done.6, bf16[896,4096]{1,0:T(8,128)(2,1)} %dp_ref.1), custom_call_target="tpu_custom_call" | custom-call | flops 7516192768 | bytes 24903680 | tf_op jit(solution)/shard_map/pallas_call | solution.py:684
  218.8 0.0 copy-start
  218.8 1.9 copy-done
  220.7 0.0 copy-start.1
  220.7 2.0 copy-done.1
  222.7 63.6 %shard_map.88 = bf16[2,512,256]{2,1,0:T(8,128)(2,1)} custom-call(bf16[512,4096]{1,0:T(8,128)(2,1)} %copy-done, bf16[512,4096]{1,0:T(8,128)(2,1)} %copy-done.1), custom_call_target="tpu_custom_call" | custom-call | tf_op jit(solution)/shard_map/pallas_call | solution.py:527
  286.3 1.9 slice_bitcast_fusion
Async XLA Ops:
  0.6 1.2 copy-start.2
  1.8 1.2 copy-start.3
  3.0 1.2 copy-start.4
  4.2 0.9 copy-start.5
  203.9 3.1 %copy-start.6 = (bf16[896,4096]{1,0:T(8,128)(2,1)S(1)}, bf16[896,4096]{1,0:T(8,128)(2,1)}, u32[]{:S(2)}) copy-start(bf16[896,4096]{1,0:T(8,128)(2,1)} %get-tuple-element.9.do_ref) | copy-start | bytes 22020100
  218.8 1.9 copy-start
  220.7 2.0 copy-start.1
